TPU v7x, 32 devices: a whole 2x2x4 slice. The times are simulated.
32 devices in a mesh: seq: 8 (over y, x, core), pipe: 4 (over z).
Axes of the slice: x: 2, y: 2, z: 4, core: 2. Of those that a mesh axis runs over, the one named last changes fastest.
Arguments:
- query_in: bfloat16 [4, 1024, 4096], P('pipe', 'seq'), may hold values from -6 to 6
- key_in: bfloat16 [4, 1024, 4096], P('pipe', 'seq'), may hold values from -6 to 6
- value_in: bfloat16 [4, 1024, 4096], P('pipe', 'seq'), may hold values from -6 to 6
- grad_out: bfloat16 [4, 1024, 4096], P('pipe', 'seq'), may hold values from -6 to 6
- long_filter: float32 [4, 1024, 256], P('pipe', 'seq'), may hold values from -2 to 2, as said below
- short_taps: float32 [4, 3, 3, 4096], P('pipe'), may hold values from -3 to 3
Outputs:
- layer_out: bfloat16 [4, 1024, 4096], P('pipe', 'seq')
- passed_grads: bfloat16 [4, 3, 1024, 4096], P('pipe', None, 'seq')
- filter_grad: float32 [4, 1024, 256], P('pipe', 'seq')
- tap_grads: float32 [4, 3, 3, 4096], P('pipe')
Inputs may be any that keep to these rules, and one draw needn't show every extreme that they name: `long_filter`: one filter for each channel group of each section.
All inputs are finite; a program needn't handle non-finite values.
Results may differ from a plain program's by a relative error of at most 0.005.
Values may be sent and summed in bfloat16 or wider, within the bound.
No kernel may reach another device: no remote copies, remote signals or barrier semaphores. Data moves between devices by JAX's collectives and lax.ppermute only.
A program may use at most 256 MiB of HBM per device.

v0:
```python
import math

import jax
import jax.numpy as jnp
from jax import lax
from jax.sharding import PartitionSpec as P

exact_mode = lax.Precision.HIGHEST


def passed_along(x, axis, by):
    count = lax.axis_size(axis)
    pairs = [(i, i + by) for i in range(count) if 0 <= i + by < count]
    return lax.ppermute(x, axis, pairs)


def counting(length):
    return jnp.arange(length, dtype=jnp.int32)


def matmul(left, right):
    return jnp.dot(left, right, precision=exact_mode, preferred_element_type=jnp.float32)


def phases(row_index, col_index, modulus, direction):
    index_product = row_index[:, None] * col_index[None, :] % modulus
    phase_angle = index_product.astype(jnp.float32) * (-2.0 * math.pi * direction / modulus)
    return (jnp.cos(phase_angle), jnp.sin(phase_angle))


def complex_table(row_index, col_index, modulus, direction, factor):
    cosine_part, sine_part = phases(row_index, col_index, modulus, direction)
    upper = jnp.concatenate([cosine_part, -sine_part], axis=1)
    lower = jnp.concatenate([sine_part, cosine_part], axis=1)
    return jnp.concatenate([upper, lower], axis=0) * factor


def lead_segment(packed, row_index, col_index, modulus, direction, factor):
    in_shape = packed.shape
    flattened = packed.reshape(2 * in_shape[1], -1)
    table = complex_table(row_index, col_index, modulus, direction, factor)
    joined = matmul(table, flattened)
    return joined.reshape((2, row_index.shape[0]) + in_shape[2:])


def middle_segment(packed, row_index, col_index, modulus, direction):
    table = complex_table(row_index, col_index, modulus, direction, 1.0)
    table = table.reshape(2, row_index.shape[0], 2, col_index.shape[0])
    return jnp.einsum(
        "xrzb,zkbw->xkrw", table, packed, precision=exact_mode, preferred_element_type=jnp.float32
    )


def twiddle(packed, row_index, col_index, modulus, direction):
    cosine_part, sine_part = phases(row_index, col_index, modulus, direction)
    cosine_part = cosine_part[:, :, None]
    sine_part = sine_part[:, :, None]
    return jnp.stack(
        [
            packed[0] * cosine_part - packed[1] * sine_part,
            packed[0] * sine_part + packed[1] * cosine_part,
        ]
    )


def pack_pairs(values, pack_block):
    lead_dims = values.shape[:-1]
    split_view = values.reshape(lead_dims + (values.shape[-1] // (2 * pack_block), 2, pack_block))
    return jnp.stack(
        [
            split_view[..., 0, :].reshape(lead_dims + (-1,)),
            split_view[..., 1, :].reshape(lead_dims + (-1,)),
        ]
    )


def unpack_pairs(packed, pack_block):
    lead_dims = packed.shape[1:-1]
    pair_view = packed.reshape((2,) + lead_dims + (packed.shape[-1] // pack_block, pack_block))
    joined = jnp.stack([pair_view[0], pair_view[1]], axis=-2)
    return joined.reshape(lead_dims + (-1,))


def group_table(first_packed, col_count, half_group, groups):
    packed_index = first_packed + counting(col_count)
    return (packed_index[None, :] // half_group == counting(groups)[:, None]).astype(jnp.float32)


def spec_product(first_spec, second_spec):
    return jnp.stack(
        [
            first_spec[0] * second_spec[0] - first_spec[1] * second_spec[1],
            first_spec[0] * second_spec[1] + first_spec[1] * second_spec[0],
        ]
    )


def conj_product(first_spec, second_spec):
    return jnp.stack(
        [
            first_spec[0] * second_spec[0] + first_spec[1] * second_spec[1],
            first_spec[1] * second_spec[0] - first_spec[0] * second_spec[1],
        ]
    )


def spread_groups(spectrum, group_map):
    return jnp.einsum(
        "rktg,gq->rktq",
        spectrum,
        group_map,
        precision=exact_mode,
        preferred_element_type=jnp.float32,
    )


def sum_groups(spectrum, group_map):
    return jnp.einsum(
        "rktq,gq->rktg",
        spectrum,
        group_map,
        precision=exact_mode,
        preferred_element_type=jnp.float32,
    )


def local(query_in, key_in, value_in, grad_out, long_filter, short_taps):
    seq_size = lax.axis_size("seq")
    seq_rank = lax.axis_index("seq")
    rows_dev = query_in.shape[1]
    width = query_in.shape[2]
    groups = long_filter.shape[2]
    half_group = width // groups // 2
    pack_block = half_group // 2
    total_rows = rows_dev * seq_size
    fft_length = 2 * total_rows
    tap_table = short_taps[0]
    stacked_in = jnp.stack([query_in[0], key_in[0], value_in[0]])
    before = passed_along(stacked_in[:, rows_dev - 2 :, :], "seq", 1)
    extended = jnp.concatenate([before, stacked_in], axis=1).astype(jnp.float32)
    featured = tap_table[:, 0, None, :] * extended[:, 2 : 2 + rows_dev, :]
    featured = featured + tap_table[:, 1, None, :] * extended[:, 1 : 1 + rows_dev, :]
    featured = featured + tap_table[:, 2, None, :] * extended[:, 0:rows_dev, :]
    query_feat = featured[0]
    keyed = featured[1]
    valued = featured[2]
    grad_float = grad_out[0].astype(jnp.float32)
    product = (keyed * valued).astype(jnp.bfloat16)
    scaled = (grad_float * query_feat).astype(jnp.bfloat16)
    block_rows = rows_dev // seq_size
    group_map = group_table(0, width // 2, half_group, groups)
    freq_index = (
        (2 * seq_rank + counting(2))[:, None] + 2 * seq_size * counting(rows_dev)[None, :]
    ).reshape(-1)
    whole_filter = lax.all_gather(long_filter[0], "seq", axis=0, tiled=True)
    filter_cos, filter_sin = phases(freq_index, counting(total_rows), fft_length, 1)
    own_spec = jnp.stack(
        [matmul(filter_cos, whole_filter), matmul(filter_sin, whole_filter)]
    ).reshape(2, 2, rows_dev, groups)
    kernel = spread_groups(own_spec, group_map)

    def forward(signal):
        arrived = lax.all_to_all(signal[None], "seq", split_axis=1, concat_axis=0, tiled=True)
        packed = pack_pairs(arrived.astype(jnp.float32), pack_block)
        first_segment = lead_segment(
            packed, counting(2 * seq_size), counting(seq_size), 2 * seq_size, 1, 1.0
        )
        turned = twiddle(
            first_segment,
            counting(2 * seq_size),
            seq_rank * block_rows + counting(block_rows),
            fft_length,
            1,
        )
        gathered = lax.all_to_all(turned, "seq", split_axis=1, concat_axis=2, tiled=True)
        return middle_segment(gathered, counting(rows_dev), counting(rows_dev), rows_dev, 1)

    def inverse(spectrum):
        back_segment = middle_segment(
            spectrum, counting(rows_dev), counting(rows_dev), rows_dev, -1
        )
        turned = twiddle(
            back_segment, 2 * seq_rank + counting(2), counting(rows_dev), fft_length, -1
        )
        arrived = lax.all_to_all(turned, "seq", split_axis=2, concat_axis=1, tiled=True)
        row_data = lead_segment(
            arrived, counting(seq_size), counting(2 * seq_size), 2 * seq_size, -1, 1.0 / fft_length
        )
        spread_back = unpack_pairs(row_data, pack_block)
        return lax.all_to_all(spread_back, "seq", split_axis=0, concat_axis=1, tiled=True)[0]

    prod_spec = forward(product)
    conv_out = inverse(spec_product(prod_spec, kernel))
    scaled_spec = forward(scaled)
    back_out = inverse(conj_product(scaled_spec, kernel))
    cross_spec = sum_groups(conj_product(scaled_spec, prod_spec), group_map)
    cross_real = cross_spec[0].reshape(2 * rows_dev, groups)
    cross_imag = cross_spec[1].reshape(2 * rows_dev, groups)
    layer_out = (query_feat * conv_out).astype(jnp.bfloat16)
    grad_stack = jnp.stack([grad_float * conv_out, back_out * valued, back_out * keyed])
    after_rows = passed_along(grad_stack[:, :2, :].astype(jnp.bfloat16), "seq", -1).astype(
        jnp.float32
    )
    padded = jnp.concatenate([grad_stack, after_rows], axis=1)
    input_grads = tap_table[:, 0, None, :] * padded[:, 0:rows_dev, :]
    input_grads = input_grads + tap_table[:, 1, None, :] * padded[:, 1 : 1 + rows_dev, :]
    input_grads = input_grads + tap_table[:, 2, None, :] * padded[:, 2 : 2 + rows_dev, :]
    input_grads = input_grads.astype(jnp.bfloat16)
    tap_terms = jnp.stack(
        [
            jnp.sum(grad_stack * extended[:, 2 - tap_lag : 2 - tap_lag + rows_dev, :], axis=1)
            for tap_lag in range(3)
        ],
        axis=1,
    )
    tap_grads = lax.psum(tap_terms, "seq") / math.sqrt(total_rows)
    positions = counting(rows_dev * lax.axis_size("seq"))
    cosine_part, sine_part = phases(positions, freq_index, fft_length, -1)
    filter_grad = lax.psum_scatter(
        (matmul(cosine_part, cross_real) - matmul(sine_part, cross_imag)) / fft_length,
        "seq",
        scatter_dimension=0,
        tiled=True,
    ) / math.sqrt(total_rows * 2 * half_group)
    passed_grads = passed_along(input_grads, "pipe", -1)
    return (layer_out[None], passed_grads[None], filter_grad[None], tap_grads[None])


def solution(mesh):
    in_specs = (
        P("pipe", "seq", None),
        P("pipe", "seq", None),
        P("pipe", "seq", None),
        P("pipe", "seq", None),
        P("pipe", "seq", None),
        P("pipe", None, None, None),
    )
    out_specs = (
        P("pipe", "seq", None),
        P("pipe", None, "seq", None),
        P("pipe", "seq", None),
        P("pipe", None, None, None),
    )
    return jax.shard_map(local, mesh=mesh, in_specs=in_specs, out_specs=out_specs, check_vma=False)
```

profile of v0, /device:TPU:0, one launch (start us, length us, event | category | flops | bytes accessed | tf_op | source)
XLA Modules:
  0.0 850.4 jit_solution(6586171705041286776)
XLA Ops:
  36.9 15.1 %all-to-all-done.4 = bf16[8,2,32768]{2,1,0:T(2,128)(2,1)S(1)} async-done(((bf16[8,2,32768]{2,1,0:T(2,128)(2,1)}), bf16[8,2,32768]{2,1,0:T(2,128)(2,1)S(1)}, u32[]{:S(2)}, u32[]{:S(2)}) %all-to-all-start.4) | async-done | bytes 1048608 | tf_op jit(solution)/shard_map/all_to_all | solution.py:163
  66.4 11.0 %fusion.148 = (f32[8,16,512,1,4]{1,0,4,3,2:T(8,128)}, f32[8,16,512,1,4]{1,0,4,3,2:T(8,128)}) fusion(f32[8,16,512,2,4]{1,0,4,3,2:T(8,128)} %reshape.367), kind=kLoop, calls=%fused_computation.231 | loop fusion | bytes 4194304 | tf_op jit(solution)/shard_map/slice | solution.py:71
  105.5 39.8 %all-gather.3.cloned.1.call-done = f32[1,1024,256]{2,1,0:T(8,128)} async-done(((f32[1,128,256]{2,1,0:T(8,128)}), f32[1,1024,256]{2,1,0:T(8,128)}) %all-gather.3.cloned.1.call-update) | async-done | bytes 1048592 | tf_op jit(solution)/shard_map/all_gather | solution.py:155
  193.3 49.7 %all-to-all-done.6 = f32[2,2,128,2048]{3,0,1,2:T(2,128)} async-done(((f32[2,2,128,2048]{3,0,1,2:T(2,128)}), f32[2,2,128,2048]{3,0,1,2:T(2,128)}, u32[]{:S(2)}, u32[]{:S(2)}) %all-to-all-start.6) | async-done | bytes 4194336 | tf_op jit(solution)/shard_map/all_to_all | solution.py:185
  252.9 8.8 %copy.197 = f32[8,32768]{0,1:T(8,128)} copy(f32[8,32768]{1,0:T(8,128)S(1)} %get-tuple-element.37) | data formatting | bytes 2097152 | tf_op jit(solution)/shard_map/slice | solution.py:80
  261.7 8.8 %copy.198 = f32[8,32768]{0,1:T(8,128)} copy(f32[8,32768]{1,0:T(8,128)S(1)} %get-tuple-element.38) | data formatting | bytes 2097152 | tf_op jit(solution)/shard_map/slice | solution.py:80
  270.6 23.0 %pad_maximum_fusion.1 = f32[8,16,512,2,4]{0,4,2,1,3:T(4,128)} fusion(f32[8,16,512,1,4]{0,4,2,1,3:T(4,128)} %bitcast.249, f32[8,16,512,1,4]{0,4,2,1,3:T(4,128)} %bitcast.247), kind=kLoop, calls=%fused_computation.1 | loop fusion | flops 524288 | bytes 4194304 | tf_op jit(solution)/shard_map/stack | solution.py:80
  293.6 30.4 %copy.199 = f32[8,16,512,2,4]{1,0,4,3,2:T(8,128)} copy(f32[8,16,512,2,4]{0,4,2,1,3:T(4,128)} %pad_maximum_fusion.1) | data formatting | bytes 4194304 | tf_op jit(solution)/shard_map/stack | solution.py:80
  324.0 9.6 %copy.200 = f32[8,16,4096]{2,1,0:T(8,128)S(1)} copy(f32[8,16,4096]{1,0,2:T(8,128)} %bitcast.245) | data formatting | bytes 4194304 | tf_op jit(solution)/shard_map/reshape | solution.py:81
  333.6 29.4 %all_to_all.102 = f32[8,16,4096]{2,1,0:T(8,128)S(1)} all-to-all(f32[8,16,4096]{2,1,0:T(8,128)S(1)} %copy.200), channel_id=1, replica_groups=mesh['seq'=8,'pipe'=4] {'seq'}, dimensions={0} | all-to-all | bytes 4194304 | tf_op jit(solution)/shard_map/all_to_all | solution.py:190
  380.7 18.8 %all_to_all.103 = bf16[8,2,32768]{2,1,0:T(2,128)(2,1)S(1)} all-to-all(bf16[8,2,32768]{2,1,0:T(2,128)(2,1)} %reshape.382), channel_id=1, replica_groups=mesh['seq'=8,'pipe'=4] {'seq'}, dimensions={0} | all-to-all | bytes 2097152 | tf_op jit(solution)/shard_map/all_to_all | solution.py:163
  410.5 10.6 %reshape.366 = f32[8,16,512,2,4]{1,0,4,3,2:T(8,128)} reshape(f32[1,128,4096]{1,2,0:T(8,128)} %copy.159) | data formatting | bytes 4194304 | tf_op jit(solution)/shard_map/convert_element_type | solution.py:164
  421.0 11.0 %fusion.149 = (f32[8,16,512,1,4]{1,0,4,3,2:T(8,128)}, f32[8,16,512,1,4]{1,0,4,3,2:T(8,128)}) fusion(f32[8,16,512,2,4]{1,0,4,3,2:T(8,128)} %reshape.366), kind=kLoop, calls=%fused_computation.232 | loop fusion | bytes 4194304 | tf_op jit(solution)/shard_map/slice | solution.py:71
  453.6 51.9 %all_to_all.104 = f32[2,16,16,2048]{3,2,0,1:T(8,128)S(1)} all-to-all(f32[2,16,16,2048]{3,2,0,1:T(8,128)S(1)} %pad_maximum_fusion.4), channel_id=1, replica_groups=mesh['seq'=8,'pipe'=4] {'seq'}, dimensions={1} | all-to-all | bytes 8388608 | tf_op jit(solution)/shard_map/all_to_all | solution.py:175
  535.3 52.8 %all_to_all.105 = f32[2,2,128,2048]{3,0,1,2:T(2,128)S(1)} all-to-all(f32[2,2,128,2048]{3,0,1,2:T(2,128)} %copy.173), channel_id=1, replica_groups=mesh['seq'=8,'pipe'=4] {'seq'}, dimensions={2} | all-to-all | bytes 8388608 | tf_op jit(solution)/shard_map/all_to_all | solution.py:185
  596.7 9.1 %copy.176 = f32[8,32768]{0,1:T(8,128)} copy(f32[8,32768]{1,0:T(8,128)} %get-tuple-element.39) | data formatting | bytes 2097152 | tf_op jit(solution)/shard_map/slice | solution.py:80
  605.8 8.8 %copy.177 = f32[8,32768]{0,1:T(8,128)} copy(f32[8,32768]{1,0:T(8,128)S(1)} %get-tuple-element.40) | data formatting | bytes 2097152 | tf_op jit(solution)/shard_map/slice | solution.py:80
  614.7 23.0 %pad_maximum_fusion = f32[8,16,512,2,4]{0,4,2,1,3:T(4,128)} fusion(f32[8,16,512,1,4]{0,4,2,1,3:T(4,128)} %bitcast.250, f32[8,16,512,1,4]{0,4,2,1,3:T(4,128)} %bitcast.248), kind=kLoop, calls=%fused_computation | loop fusion | flops 524288 | bytes 4194304 | tf_op jit(solution)/shard_map/stack | solution.py:80
  637.7 30.4 %copy.178 = f32[8,16,512,2,4]{1,0,4,3,2:T(8,128)} copy(f32[8,16,512,2,4]{0,4,2,1,3:T(4,128)} %pad_maximum_fusion) | data formatting | bytes 4194304 | tf_op jit(solution)/shard_map/stack | solution.py:80
  668.1 10.6 %copy.179 = f32[8,16,4096]{2,1,0:T(8,128)} copy(f32[8,16,4096]{1,0,2:T(8,128)} %bitcast.246) | data formatting | bytes 4194304 | tf_op jit(solution)/shard_map/reshape | solution.py:81
  690.1 19.8 %all-to-all-done.3 = f32[8,16,4096]{2,1,0:T(8,128)} async-done(((f32[8,16,4096]{2,1,0:T(8,128)}), f32[8,16,4096]{2,1,0:T(8,128)}, u32[]{:S(2)}, u32[]{:S(2)}) %all-to-all-start.3) | async-done | bytes 2097184 | tf_op jit(solution)/shard_map/all_to_all | solution.py:190
  720.9 9.4 %multiply_reduce_fusion.2 = (f32[3,4096]{1,0:T(4,128)S(1)}, f32[3,4096]{1,0:T(4,128)S(1)}, f32[3,4096]{1,0:T(4,128)S(1)}, bf16[3,128,4096]{2,1,0:T(8,128)(2,1)}) fusion(f32[3,130,4096]{2,1,0:T(8,128)S(1)} %bitcast.244, f32[1,128,4096]{2,1,0:T(8,128)} %get-tuple-element.14, f32[1,128,4096]{2,1,0:T(8,128)S(1)} %get-tuple-element.13, ...), kind=kLoop, calls=%fused_computation.11 | loop fusion | flops 21983232 | bytes 41189376 | tf_op jit(solution)/shard_map/reduce_sum | solution.py:211
  745.0 38.3 %reduce-scatter.2.cloned.1.call-done = f32[128,256]{1,0:T(8,128)} async-done(((f32[1024,256]{1,0:T(8,128)}), f32[128,256]{1,0:T(8,128)}) %reduce-scatter.2.cloned.1.call-update) | async-done | bytes 131088 | tf_op jit(solution)/shard_map/reduce_scatter | solution.py:219
  784.8 55.2 %all-reduce.2.cloned.1.call-done = f32[3,3,4096]{2,1,0:T(4,128)} async-done(((f32[3,3,4096]{2,1,0:T(4,128)}), f32[3,3,4096]{2,1,0:T(4,128)}) %all-reduce.2.cloned.1.call-update) | async-done | bytes 147472 | tf_op jit(solution)/shard_map/psum | solution.py:216
  (189 shorter events, 259.7 us)
Async XLA Ops:
  7.2 5.3 copy-start.23
  10.0 3.3 collective-permute-start
  29.1 22.9 %all-to-all-start.4 = ((bf16[8,2,32768]{2,1,0:T(2,128)(2,1)}), bf16[8,2,32768]{2,1,0:T(2,128)(2,1)S(1)}, u32[]{:S(2)}, u32[]{:S(2)}) async-start(bf16[8,2,32768]{2,1,0:T(2,128)(2,1)} %reshape.384), calls=%async_computation.4 | async-start | bytes 2097152 | tf_op jit(solution)/shard_map/all_to_all | solution.py:163
  98.5 63.6 %all-to-all-start.5 = ((f32[2,16,16,2048]{3,2,0,1:T(8,128)}), f32[2,16,16,2048]{3,2,0,1:T(8,128)}, u32[]{:S(2)}, u32[]{:S(2)}) async-start(f32[2,16,16,2048]{3,2,0,1:T(8,128)} %pad_maximum_fusion.6), calls=%async_computation.5 | async-start | bytes 8388608 | tf_op jit(solution)/shard_map/all_to_all | solution.py:175
  103.1 42.3 %all-gather.3.cloned.1.call-start = ((), (), s32[]{:S(2)}) async-start(), calls=%async_computation.11 | async-start | bytes 1179648 | tf_op jit(solution)/shard_map/all_gather | solution.py:155
  104.6 60.0 %copy-start.10 = (f32[2,128,2,128]{3,2,1,0:T(2,128)}, f32[2,128,2,128]{3,2,1,0:T(2,128)S(1)}, u32[]{:S(2)}) copy-start(f32[2,128,2,128]{3,2,1,0:T(2,128)S(1)} %reshape.359) | copy-start | bytes 786436
  105.3 68.5 %copy-start.12 = (f32[2,128,2,128]{3,2,1,0:T(2,128)}, f32[2,128,2,128]{3,2,1,0:T(2,128)S(1)}, u32[]{:S(2)}) copy-start(f32[2,128,2,128]{3,2,1,0:T(2,128)S(1)} %reshape.360) | copy-start | bytes 786436
  105.3 53.1 %copy-start.24 = (s32[2048]{0:T(1024)}, s32[2048]{0:T(1024)S(1)}, u32[]{:S(2)}) copy-start(s32[2048]{0:T(1024)S(1)} %add_select_fusion.3) | copy-start | bytes 24580
  105.4 53.0 %copy-start.26 = (s32[256]{0:T(256)}, s32[256]{0:T(256)S(1)}, u32[]{:S(2)}) copy-start(s32[256]{0:T(256)S(1)} %add_bitcast_fusion) | copy-start | bytes 3076
  145.4 6.3 copy-start.28
  164.6 7.1 copy-start.1
  187.3 55.8 %all-to-all-start.6 = ((f32[2,2,128,2048]{3,0,1,2:T(2,128)}), f32[2,2,128,2048]{3,0,1,2:T(2,128)}, u32[]{:S(2)}, u32[]{:S(2)}) async-start(f32[2,2,128,2048]{3,0,1,2:T(2,128)} %copy.194), calls=%async_computation.6 | async-start | bytes 8388608 | tf_op jit(solution)/shard_map/all_to_all | solution.py:185
  506.5 8.3 copy-start.2
  506.5 8.3 copy-start.4
  514.8 5.4 copy-start.13
  678.7 31.1 %all-to-all-start.3 = ((f32[8,16,4096]{2,1,0:T(8,128)}), f32[8,16,4096]{2,1,0:T(8,128)}, u32[]{:S(2)}, u32[]{:S(2)}) async-start(f32[8,16,4096]{2,1,0:T(8,128)} %copy.179), calls=%async_computation.3 | async-start | bytes 4194304 | tf_op jit(solution)/shard_map/all_to_all | solution.py:190
  683.2 100.1 %reduce-scatter.2.cloned.1.call-start = ((), (), s32[]{:S(2)}) async-start(), calls=%async_computation.9 | async-start | bytes 1179648 | tf_op jit(solution)/shard_map/reduce_scatter | solution.py:219
  683.5 26.4 %copy-start.9 = (bf16[1,128,4096]{2,1,0:T(8,128)(2,1)S(1)}, bf16[1,128,4096]{2,1,0:T(8,128)(2,1)}, u32[]{:S(2)}) copy-start(bf16[1,128,4096]{2,1,0:T(8,128)(2,1)} %param.9) | copy-start | bytes 3145732
  713.6 7.3 slice-start
  714.3 3.4 collective-permute-start.1
  720.9 11.1 %copy-start.27 = (s32[256]{0:T(256)S(1)}, s32[256]{0:T(256)}, u32[]{:S(2)}) copy-start(s32[256]{0:T(256)} %copy-done.26) | copy-start | bytes 3076
  730.3 7.4 copy-start.22
  730.3 111.5 %collective-permute-start.2 = (bf16[3,128,4096]{2,1,0:T(8,128)(2,1)}, bf16[3,128,4096]{2,1,0:T(8,128)(2,1)S(1)}, u32[]{:S(2)}, u32[]{:S(2)}) collective-permute-start(bf16[3,128,4096]{2,1,0:T(8,128)(2,1)} %get-tuple-element.19), channel_id=1, source_target_pairs={{1,0},{2,1},{3,2},{5,4},{6,5},{7,6},{9,8},{10,9},{11,10},{13,12},{... | collective-permute-start | bytes 9437192 | tf_op jit(solution)/shard_map/ppermute | solution.py:14
  743.9 96.1 %all-reduce.2.cloned.1.call-start = ((), (), s32[]{:S(2)}) async-start(), calls=%async_computation.10 | async-start | bytes 393216 | tf_op jit(solution)/shard_map/psum | solution.py:216
  (17 other events, 45.9 us)
Sparse Core Ops, SparseCore 0:
  105.8 39.5 all-gather.2
  744.0 39.1 reduce-scatter.1
  786.3 53.6 all-reduce.1
where the time goes:
time: 862 us; the launch traced here: 850 us
  local copies, waits for them, and re-layouts  248 us (29%)
  waiting for transfers between devices  220 us (26%)
  blocking collectives  153 us (18%)
  other arithmetic  116 us (13%)
  matrix products  70.2 us (8%)
  starting transfers between devices  29 us (3%)
  between operations  15.1 us (2%)
    another operation x2, local copies, waits for them, and re-layouts, unpack_pairs(): joined = jnp.stack([pair_view[0], pair_view[1]], axis=-2)  60.9 us
    psum x1, waiting for transfers between devices, local(): tap_grads = lax.psum(tap_terms, 'seq') / math.sqrt(total_rows)  55.2 us
    all_to_all x1, blocking collectives, inverse(): lax.all_to_all(turned, 'seq', split_axis=2, concat_axis=1, tiled=True)  52.8 us
    all_to_all x1, blocking collectives, forward(): lax.all_to_all(turned, 'seq', split_axis=1, concat_axis=2, tiled=True)  51.9 us
    all_to_all x1, waiting for transfers between devices, inverse(): lax.all_to_all(turned, 'seq', split_axis=2, concat_axis=1, tiled=True)  49.7 us
    another operation x2, other arithmetic, unpack_pairs(): joined = jnp.stack([pair_view[0], pair_view[1]], axis=-2)  46 us
    all_gather x1, waiting for transfers between devices, local(): whole_filter = lax.all_gather(long_filter[0], 'seq', axis=0, tiled=True)  39.8 us
    reduce_scatter x1, waiting for transfers between devices, local(): lax.psum_scatter((matmul(cosine_part, cross_real) - matmul(sine_part, cro...  38.3 us
  transfers between devices with their start and end apart: 10, of which 8 were waited for; matrix products, arithmetic and copies ran while one was open for 5% of the time, Pallas kernels for 0%

commit v1 on v0

v1 whole, which is shorter than its diff:
```python
import functools
import math

import jax
import jax.numpy as jnp
from jax import lax
from jax.experimental import pallas as pl
from jax.experimental.pallas import tpu as pltpu
from jax.sharding import PartitionSpec as P

F32 = jnp.float32
BF16 = jnp.bfloat16
CHUNKS = 1
TILE = 16
LANES = 128


def passed_along(x, axis, by):
    count = lax.axis_size(axis)
    pairs = [(i, i + by) for i in range(count) if 0 <= i + by < count]
    return lax.ppermute(x, axis, pairs)


def exchange(x):
    return lax.all_to_all(x, "seq", split_axis=0, concat_axis=0, tiled=True)


def dot_nt(left, right):
    return lax.dot_general(
        left, right, (((1,), (1,)), ((), ())), preferred_element_type=F32
    )


def dot_nn(left, right):
    return lax.dot_general(
        left, right, (((1,), (0,)), ((), ())), preferred_element_type=F32
    )


def grid_index(shape, dim):
    return lax.broadcasted_iota(jnp.int32, shape, dim)


def identity(size):
    shape = (size, size)
    return (grid_index(shape, 0) == grid_index(shape, 1)).astype(F32).astype(BF16)


def delayed(x, before):
    row = grid_index(x.shape, 0)
    one = jnp.where(row == 0, before[1:2], pltpu.roll(x, 1, 0))
    two = jnp.where(row == 0, before[0:1], pltpu.roll(x, 2, 0))
    two = jnp.where(row == 1, before[1:2], two)
    return one, two


def advanced(x, after):
    rows = x.shape[0]
    row = grid_index(x.shape, 0)
    one = jnp.where(row == rows - 1, after[0:1], pltpu.roll(x, rows - 1, 0))
    two = jnp.where(row == rows - 1, after[1:2], pltpu.roll(x, rows - 2, 0))
    two = jnp.where(row == rows - 2, after[0:1], two)
    return one, two


def featured_of(taps, branch, x, one, two):
    base = 3 * branch
    out = taps[base : base + 1] * x
    out = out + taps[base + 1 : base + 2] * one
    return out + taps[base + 2 : base + 3] * two


def send_kernel(query_ref, key_ref, value_ref, grad_ref, before_ref, taps_ref, filter_ref, out_ref):
    own = query_ref.shape[1]
    groups = filter_ref.shape[0]
    unit = identity(LANES)
    for lane in range(0, own, LANES):
        cols = pl.ds(lane, LANES)
        taps = taps_ref[:, cols]
        feats = []
        for branch, ref in enumerate((query_ref, key_ref, value_ref)):
            x = ref[:, cols].astype(F32)
            one, two = delayed(x, before_ref[branch, :, cols].astype(F32))
            feats.append(featured_of(taps, branch, x, one, two))
        product = (feats[1] * feats[2]).astype(BF16)
        scaled = (grad_ref[:, cols].astype(F32) * feats[0]).astype(BF16)
        out_ref[0, pl.ds(lane, LANES), :] = dot_nt(unit, product).astype(BF16)
        out_ref[0, pl.ds(own + lane, LANES), :] = dot_nt(unit, scaled).astype(BF16)
    tail = out_ref.shape[1] - 2 * own
    taken = filter_ref[...]
    if tail > groups:
        taken = jnp.concatenate([taken, jnp.zeros((tail - groups, LANES), F32)], axis=0)
    out_ref[0, pl.ds(2 * own, tail), :] = taken.astype(BF16)


def conv_kernel(own, groups, scale, in_ref, out_ref, corr_ref, first_pad, second_pad, taps):
    blocks = in_ref.shape[0]
    wide = own // groups
    rows = blocks * wide
    skip = rows - wide
    lane = grid_index((LANES, LANES), 1)
    sub = grid_index((LANES, LANES), 0)
    flip = (lane + sub == LANES - 1).astype(F32).astype(BF16)
    first_pad[pl.ds(0, skip), :] = jnp.zeros((skip, LANES), BF16)
    second_pad[pl.ds(rows, skip), :] = jnp.zeros((skip, LANES), BF16)
    held = in_ref[:, pl.ds(2 * own, in_ref.shape[1] - 2 * own), :].astype(F32)
    taps[...] = held

    def one_group(g, carry):
        at = pl.multiple_of(g * wide, wide)
        first = in_ref[:, pl.ds(at, wide), :].reshape(rows, LANES)
        second = in_ref[:, pl.ds(own + at, wide), :].reshape(rows, LANES)
        first_pad[pl.ds(skip, rows), :] = first
        second_pad[pl.ds(0, rows), :] = second
        turned = []
        for k in range(blocks):
            line = taps[k, pl.ds(g, 1), :]
            spread = jnp.broadcast_to(line, (LANES, LANES))
            turned.append(pltpu.roll(spread, 0, 1, stride=1, stride_axis=0))
        toeplitz = []
        for k in range(blocks):
            lower = turned[k - 1] if k else jnp.zeros((LANES, LANES), F32)
            toeplitz.append(jnp.where(lane >= sub, turned[k], lower).astype(BF16))
        shifted = [first_pad[pl.ds(skip - wide * k, rows), :] for k in range(blocks)]
        ahead = [second_pad[pl.ds(wide * k, rows), :] for k in range(blocks)]
        ahead = jnp.concatenate(ahead, axis=1)
        conv = dot_nn(jnp.concatenate(shifted, axis=1), jnp.concatenate(toeplitz, axis=0))
        back = dot_nt(ahead, jnp.concatenate(toeplitz, axis=1))
        out_ref[:, pl.ds(at, wide), :] = conv.astype(BF16).reshape(blocks, wide, LANES)
        out_ref[:, pl.ds(own + at, wide), :] = back.astype(BF16).reshape(blocks, wide, LANES)
        backwards = dot_nt(flip, first).astype(BF16)
        cross = dot_nn(backwards, ahead)
        rolled = [
            pltpu.roll(cross[:, k * LANES : (k + 1) * LANES], 1, 1, stride=1, stride_axis=0)
            for k in range(blocks)
        ]
        for k in range(blocks):
            later = rolled[k + 1] if k + 1 < blocks else jnp.zeros((LANES, LANES), F32)
            mixed = jnp.where(lane <= sub, rolled[k], later)
            corr_ref[k, pl.ds(g, 1), :] = jnp.sum(mixed, axis=0, keepdims=True) * scale
        return carry

    lax.fori_loop(0, groups, one_group, 0)
    pick_row = grid_index((TILE, 2 * LANES), 0)
    pick_lane = grid_index((TILE, 2 * LANES), 1)
    for a in range(blocks):
        total = jnp.zeros((TILE, LANES), F32)
        if a + 1 < blocks:
            for part in range(own // LANES):
                local_row = pick_row - 4 * part
                wanted = (local_row // 2) * LANES + local_row % 2
                used = (local_row >= 0) & (local_row < 4) & (pick_lane == wanted)
                both = jnp.concatenate(
                    [
                        out_ref[a + 1, pl.ds(part * LANES, LANES), :],
                        out_ref[a + 1, pl.ds(own + part * LANES, LANES), :],
                    ],
                    axis=1,
                )
                total = total + dot_nt(used.astype(F32).astype(BF16), both)
        out_ref[a, pl.ds(2 * own, TILE), :] = total.astype(BF16)


def finish_kernel(
    scale, has_old, query_ref, key_ref, value_ref, grad_ref, before_ref, after_ref, taps_ref, in_ref, *refs
):
    layer_ref, grads_ref, sums_ref = refs[1:] if has_old else refs
    own = query_ref.shape[1]
    rows = query_ref.shape[0]
    unit = identity(LANES)
    for part in range(own // LANES):
        cols = pl.ds(part * LANES, LANES)
        taps = taps_ref[:, cols]
        conv = dot_nt(unit, in_ref[0, pl.ds(part * LANES, LANES), :])
        back = dot_nt(unit, in_ref[0, pl.ds(own + part * LANES, LANES), :])
        edge = in_ref[0, pl.ds(2 * own, TILE), :].astype(F32)[4 * part : 4 * part + 4]
        raw = []
        feats = []
        nexts = []
        for branch, ref in enumerate((query_ref, key_ref, value_ref)):
            x = ref[:, cols].astype(F32)
            one, two = delayed(x, before_ref[branch, :, cols].astype(F32))
            raw.append((x, one, two))
            feats.append(featured_of(taps, branch, x, one, two))
            if branch:
                new = after_ref[branch - 1, :, cols].astype(F32)
                last = x[rows - 2 : rows]
                new_one = jnp.concatenate([last[1:2], new[0:1]], axis=0)
                nexts.append(featured_of(taps, branch, new, new_one, last))
        grad = grad_ref[:, cols].astype(F32)
        grad_next = after_ref[2, :, cols].astype(F32)
        layer_ref[:, cols] = (feats[0] * conv).astype(BF16)
        grads = (grad * conv, back * feats[2], back * feats[1])
        follow = (grad_next * edge[0:2], edge[2:4] * nexts[1], edge[2:4] * nexts[0])
        lines = []
        for branch in range(3):
            value = grads[branch]
            one, two = advanced(value, follow[branch])
            base = 3 * branch
            total = taps[base : base + 1] * value
            total = total + taps[base + 1 : base + 2] * one
            total = total + taps[base + 2 : base + 3] * two
            grads_ref[branch, :, cols] = total.astype(BF16)
            for lag in range(3):
                lines.append(jnp.sum(value * raw[branch][lag], axis=0, keepdims=True) * scale)
        lines.append(jnp.zeros((TILE - 9, LANES), F32))
        sums_ref[0, :, cols] = jnp.concatenate(lines, axis=0)


def local(query_in, key_in, value_in, grad_out, long_filter, short_taps):
    seq = lax.axis_size("seq")
    rows, width = query_in.shape[1:]
    groups = long_filter.shape[2]
    total_rows = rows * seq
    wide = width // groups
    chunks = min(CHUNKS, width // (LANES * seq))
    own = width // (chunks * seq)
    own_groups = own // wide
    tail = -(-own_groups // TILE) * TILE
    query, key, value, grad = query_in[0], key_in[0], value_in[0], grad_out[0]
    taps = short_taps[0].reshape(9, width)
    last = jnp.stack([query[rows - 2 :], key[rows - 2 :], value[rows - 2 :]])
    before = passed_along(last, "seq", 1)
    top = jnp.stack([key[:2], value[:2], grad[:2]])
    after = passed_along(top, "seq", -1)
    filter_t = long_filter[0].T

    layer = None
    corr_parts, sum_parts, grad_parts = [], [], []
    for chunk in range(chunks):
        base = chunk * seq
        main = pl.BlockSpec((rows, own), lambda d, base=base: (0, base + d))
        edge = pl.BlockSpec((3, 2, own), lambda d, base=base: (0, 0, base + d))
        tap_spec = pl.BlockSpec((9, own), lambda d, base=base: (0, base + d))
        sent = pl.pallas_call(
            send_kernel,
            grid=(seq,),
            in_specs=[
                main, main, main, main, edge, tap_spec,
                pl.BlockSpec((own_groups, rows), lambda d, base=base: (base + d, 0)),
            ],
            out_specs=pl.BlockSpec((1, 2 * own + tail, rows), lambda d: (d, 0, 0)),
            out_shape=jax.ShapeDtypeStruct((seq, 2 * own + tail, rows), BF16),
            name="send",
        )(query, key, value, grad, before, taps, filter_t)
        arrived = exchange(sent)
        returned, corr = pl.pallas_call(
            functools.partial(conv_kernel, own, own_groups, 1.0 / math.sqrt(total_rows * wide)),
            in_specs=[pl.BlockSpec(memory_space=pltpu.VMEM)],
            out_specs=[pl.BlockSpec(memory_space=pltpu.VMEM)] * 2,
            out_shape=[
                jax.ShapeDtypeStruct((seq, 2 * own + TILE, rows), BF16),
                jax.ShapeDtypeStruct((seq, own_groups, rows), F32),
            ],
            scratch_shapes=[
                pltpu.VMEM((2 * seq * wide - wide, LANES), BF16),
                pltpu.VMEM((2 * seq * wide - wide, LANES), BF16),
                pltpu.VMEM((seq, tail, LANES), F32),
            ],
            name="conv",
        )(arrived)
        back = exchange(returned)
        corr_parts.append(corr)
        has_old = layer is not None
        extra = (layer,) if has_old else ()
        layer, grads, sums = pl.pallas_call(
            functools.partial(finish_kernel, 1.0 / math.sqrt(total_rows), has_old),
            grid=(seq,),
            in_specs=[
                main, main, main, main, edge, edge, tap_spec,
                pl.BlockSpec((1, 2 * own + TILE, rows), lambda d: (d, 0, 0)),
            ] + [pl.BlockSpec(memory_space=pl.ANY)] * len(extra),
            out_specs=[
                main,
                pl.BlockSpec((3, rows, own), lambda d: (0, 0, d)),
                pl.BlockSpec((1, TILE, own), lambda d: (d, 0, 0)),
            ],
            out_shape=[
                jax.ShapeDtypeStruct((rows, width), BF16),
                jax.ShapeDtypeStruct((3, rows, own * seq), BF16),
                jax.ShapeDtypeStruct((seq, TILE, own), F32),
            ],
            input_output_aliases={8: 0} if has_old else {},
            name="finish",
        )(query, key, value, grad, before, after, taps, back, *extra)
        grad_parts.append(passed_along(grads, "pipe", -1))
        sum_parts.append(sums)

    corr = exchange(jnp.stack(corr_parts, axis=1))
    filter_grad = jnp.transpose(corr, (3, 1, 0, 2)).reshape(rows, groups)
    sums = jnp.sum(exchange(jnp.stack(sum_parts, axis=1)), axis=0)
    sums = exchange(jnp.broadcast_to(sums[None], (seq,) + sums.shape))
    tap_grads = jnp.transpose(sums[:, :, :9], (2, 1, 0, 3)).reshape(3, 3, width)
    passed_grads = jnp.concatenate(grad_parts, axis=2)
    return (layer[None], passed_grads[None], filter_grad[None], tap_grads[None])


def solution(mesh):
    in_specs = (
        P("pipe", "seq", None),
        P("pipe", "seq", None),
        P("pipe", "seq", None),
        P("pipe", "seq", None),
        P("pipe", "seq", None),
        P("pipe", None, None, None),
    )
    out_specs = (
        P("pipe", "seq", None),
        P("pipe", None, "seq", None),
        P("pipe", "seq", None),
        P("pipe", None, None, None),
    )
    return jax.shard_map(local, mesh=mesh, in_specs=in_specs, out_specs=out_specs, check_vma=False)
```

time: 862 us -> 194 us (0.23); the launches traced: 850 us -> 192 us
  local copies, waits for them, and re-layouts: 248 us -> 11.9 us
  waiting for transfers between devices: 220 us -> 75 us
  other arithmetic: 116 us -> 2.1 us
  blocking collectives: 153 us -> 42.6 us
  matrix products: 70.2 us -> 0 us
  Pallas kernels: 0 us -> 44.8 us
  between operations: 15.1 us -> 0.73 us
  starting transfers between devices: 29 us -> 15.4 us
    all_to_all x4 -> x2, blocking collectives: 153 us -> 42.6 us  [exchange(): return lax.all_to_all(x, 'seq', split_axis=0, concat_axis=0, tiled=True)]
    another operation x12 -> x2, local copies, waits for them, and re-layouts: 97.3 us -> 1.6 us  [the longest x1 0.83 us: local(): return (layer[None], passed_grads[None], filter_grad[None], tap_grads[None])]
    dot_general x14 -> x0, matrix products: 70.2 us -> none  [the longest x8 36 us: matmul(): jnp.dot(left, right, precision=exact_mode, preferred_element_type=jnp.flo...]
    slice x14 -> x3, local copies, waits for them, and re-layouts: 60.5 us -> 2.71 us  [the longest x2 1.85 us: local(): top = jnp.stack([key[:2], value[:2], grad[:2]])]
    psum x1 -> x0, waiting for transfers between devices: 55.2 us -> none  [local(): tap_grads = lax.psum(tap_terms, 'seq') / math.sqrt(total_rows)]
    another operation x8 -> x2, other arithmetic: 54.8 us -> 0.15 us  [the longest x1 0.08 us: local(): last = jnp.stack([query[rows - 2:], key[rows - 2:], value[rows - 2:]])]
    all_to_all x4 -> x3, waiting for transfers between devices: 84.6 us -> 33.7 us  [exchange(): return lax.all_to_all(x, 'seq', split_axis=0, concat_axis=0, tiled=True)]
    pallas_call x0 -> x3, Pallas kernels: none -> 44.8 us  [the longest x1 25.3 us: local(): pl.pallas_call(functools.partial(conv_kernel, own, own_groups, 1.0 / math...]
  transfers between devices with their start and end apart: 10 -> 6, of which waited for: 8 -> 5; matrix products, arithmetic and copies ran while one was open for 5% -> 4% of each run, Pallas kernels for 0% -> 0%
where the time goes in v1:
time: 194 us; the launch traced here: 192 us
  waiting for transfers between devices  75 us (39%)
  Pallas kernels  44.8 us (23%)
  blocking collectives  42.6 us (22%)
  starting transfers between devices  15.4 us (8%)
  local copies, waits for them, and re-layouts  11.9 us (6%)
  other arithmetic  2.1 us (1%)
    all_to_all x2, blocking collectives, exchange(): return lax.all_to_all(x, 'seq', split_axis=0, concat_axis=0, tiled=True)  42.6 us
    ppermute x3, waiting for transfers between devices, passed_along(): return lax.ppermute(x, axis, pairs)  41.2 us
    all_to_all x3, waiting for transfers between devices, exchange(): return lax.all_to_all(x, 'seq', split_axis=0, concat_axis=0, tiled=True)  33.7 us
    pallas_call x1, Pallas kernels, local(): pl.pallas_call(functools.partial(conv_kernel, own, own_groups, 1.0 / math...  25.3 us
    pallas_call x1, Pallas kernels, local(): pl.pallas_call(functools.partial(finish_kernel, 1.0 / math.sqrt(total_row...  11.5 us
    all_to_all x3, starting transfers between devices, exchange(): return lax.all_to_all(x, 'seq', split_axis=0, concat_axis=0, tiled=True)  10.4 us
    pallas_call x1, Pallas kernels, local(): pl.pallas_call(send_kernel, grid=(seq,), in_specs=[main, main, main, main...  7.98 us
    unnamed x9, local copies, waits for them, and re-layouts  6.05 us
  transfers between devices with their start and end apart: 6, of which 5 were waited for; matrix products, arithmetic and copies ran while one was open for 4% of the time, Pallas kernels for 0%

profile of v1, /device:TPU:0, one launch (start us, length us, event | category | flops | bytes accessed | tf_op | source)
XLA Modules:
  0.0 192.5 jit_solution(13789596746248403616)
XLA Ops:
  0.6 0.9 slice.27
  1.5 1.0 fusion
  2.6 2.4 %collective-permute-start = (bf16[3,2,4096]{2,1,0:T(2,128)(2,1)S(1)}, bf16[3,2,4096]{2,1,0:T(2,128)(2,1)S(1)}, u32[]{:S(2)}, u32[]{:S(2)}) collective-permute-start(bf16[3,2,4096]{2,1,0:T(2,128)(2,1)S(1)} %pad_maximum_fusion), channel_id=1, source_target_pairs={{0,4},{4,8},{8,12},{12,16},{16,20},{20,24},{24,28},{1,5},{5,9},{9,... | collective-permute-start | bytes 147464 | tf_op jit(solution)/shard_map/ppermute | solution.py:21
  5.0 1.7 copy.16
  6.6 1.3 reduce.1
  9.4 8.0 %send.1 = bf16[8,1056,128]{2,1,0:T(8,128)(2,1)} custom-call(bf16[128,4096]{1,0:T(8,128)(2,1)} %bitcast.26, bf16[128,4096]{1,0:T(8,128)(2,1)} %bitcast.22, bf16[128,4096]{1,0:T(8,128)(2,1)} %bitcast.24, bf16[128,4096]{1,0:T(8,128)(2,1)} %bitcast.28, bf16[3,2,4096]{2,1,0:T(2,128)(2,1)} %copy-done.1, f32[9,4096]{1,0:T(8,128)} %reshape_squeeze.3.taps_ref, ...), custom_call_target="tpu_custom_call" | custom-call | tf_op jit(solution)/shard_map/send/pallas_call | solution.py:235
  17.3 32.4 %all_to_all.25.in_ref = bf16[8,1056,128]{2,1,0:T(8,128)(2,1)} all-to-all(bf16[8,1056,128]{2,1,0:T(8,128)(2,1)} %send.1), channel_id=1, replica_groups=mesh['seq'=8,'pipe'=4] {'seq'}, dimensions={0} | all-to-all | bytes 4325376 | tf_op jit(solution)/shard_map/all_to_all | solution.py:25
  49.7 25.3 %conv.1 = (bf16[8,1040,128]{2,1,0:T(8,128)(2,1)}, f32[8,32,128]{2,1,0:T(8,128)}) custom-call(bf16[8,1056,128]{2,1,0:T(8,128)(2,1)} %all_to_all.25.in_ref), custom_call_target="tpu_custom_call" | custom-call | tf_op jit(solution)/shard_map/conv/pallas_call | solution.py:247
  75.0 3.6 %all-to-all-start.1 = ((bf16[8,1040,128]{2,1,0:T(8,128)(2,1)}), bf16[8,1040,128]{2,1,0:T(8,128)(2,1)S(1)}, u32[]{:S(2)}, u32[]{:S(2)}) async-start(bf16[8,1040,128]{2,1,0:T(8,128)(2,1)} %get-tuple-element.9), calls=%async_computation.1 | async-start | bytes 4259840 | tf_op jit(solution)/shard_map/all_to_all | solution.py:25
  78.6 0.9 slice.32
  79.5 1.3 collective-permute-start.1
  80.8 1.8 collective-permute-done.1.after_ref
  82.7 22.8 %all-to-all-done.1.in_ref = bf16[8,1040,128]{2,1,0:T(8,128)(2,1)S(1)} async-done(((bf16[8,1040,128]{2,1,0:T(8,128)(2,1)}), bf16[8,1040,128]{2,1,0:T(8,128)(2,1)S(1)}, u32[]{:S(2)}, u32[]{:S(2)}) %all-to-all-start.1) | async-done | bytes 2129952 | tf_op jit(solution)/shard_map/all_to_all | solution.py:25
  105.5 1.3 copy-done
  106.8 11.5 %finish.1 = (bf16[128,4096]{1,0:T(8,128)(2,1)}, bf16[3,128,4096]{2,1,0:T(8,128)(2,1)}, f32[8,16,512]{2,1,0:T(8,128)}) custom-call(bf16[128,4096]{1,0:T(8,128)(2,1)} %bitcast.27, bf16[128,4096]{1,0:T(8,128)(2,1)} %bitcast.23, bf16[128,4096]{1,0:T(8,128)(2,1)} %bitcast.25, bf16[128,4096]{1,0:T(8,128)(2,1)} %bitcast.29, bf16[3,2,4096]{2,1,0:T(2,128)(2,1)} %copy-done.1, ...), custom_call_target="tpu_custom_call" | custom-call | tf_op jit(solution)/shard_map/finish/pallas_call | solution.py:266
  118.3 1.3 collective-permute-start.2
  119.6 10.2 %all_to_all.26 = f32[8,1,16,512]{3,2,1,0:T(8,128)S(1)} all-to-all(f32[8,1,16,512]{3,2,1,0:T(8,128)} %bitcast.33), channel_id=1, replica_groups=mesh['seq'=8,'pipe'=4] {'seq'}, dimensions={0} | all-to-all | bytes 524288 | tf_op jit(solution)/shard_map/all_to_all | solution.py:25
  129.9 3.4 %all-to-all-start.2 = ((f32[8,1,32,128]{3,2,1,0:T(8,128)}), f32[8,1,32,128]{3,2,1,0:T(8,128)S(1)}, u32[]{:S(2)}, u32[]{:S(2)}) async-start(f32[8,1,32,128]{3,2,1,0:T(8,128)} %bitcast.34), calls=%async_computation.2 | async-start | bytes 262144 | tf_op jit(solution)/shard_map/all_to_all | solution.py:25
  133.9 4.8 %all-to-all-done.2 = f32[8,1,32,128]{3,2,1,0:T(8,128)S(1)} async-done(((f32[8,1,32,128]{3,2,1,0:T(8,128)}), f32[8,1,32,128]{3,2,1,0:T(8,128)S(1)}, u32[]{:S(2)}, u32[]{:S(2)}) %all-to-all-start.2) | async-done | bytes 131104 | tf_op jit(solution)/shard_map/all_to_all | solution.py:25
  138.7 1.5 broadcast_in_dim.14
  140.2 3.4 %all-to-all-start.4 = ((f32[8,1,16,512]{3,2,1,0:T(8,128)}), f32[8,1,16,512]{3,2,1,0:T(8,128)S(1)}, u32[]{:S(2)}, u32[]{:S(2)}) async-start(f32[8,1,16,512]{3,2,1,0:T(8,128)} %broadcast_in_dim.14), calls=%async_computation.4 | async-start | bytes 524288 | tf_op jit(solution)/shard_map/all_to_all | solution.py:25
  144.3 6.1 %all-to-all-done.4 = f32[8,1,16,512]{3,2,1,0:T(8,128)S(1)} async-done(((f32[8,1,16,512]{3,2,1,0:T(8,128)}), f32[8,1,16,512]{3,2,1,0:T(8,128)S(1)}, u32[]{:S(2)}, u32[]{:S(2)}) %all-to-all-start.4) | async-done | bytes 262176 | tf_op jit(solution)/shard_map/all_to_all | solution.py:25
  151.4 39.4 %collective-permute-done.2 = bf16[3,128,4096]{2,1,0:T(8,128)(2,1)S(1)} collective-permute-done((bf16[3,128,4096]{2,1,0:T(8,128)(2,1)}, bf16[3,128,4096]{2,1,0:T(8,128)(2,1)S(1)}, u32[]{:S(2)}, u32[]{:S(2)}) %collective-permute-start.2) | collective-permute-done | bytes 3145760 | tf_op jit(solution)/shard_map/ppermute | solution.py:21
  190.8 1.7 copy.23
  (14 shorter events, 3.9 us)
Async XLA Ops:
  2.6 6.2 %collective-permute-start = (bf16[3,2,4096]{2,1,0:T(2,128)(2,1)S(1)}, bf16[3,2,4096]{2,1,0:T(2,128)(2,1)S(1)}, u32[]{:S(2)}, u32[]{:S(2)}) collective-permute-start(bf16[3,2,4096]{2,1,0:T(2,128)(2,1)S(1)} %pad_maximum_fusion), channel_id=1, source_target_pairs={{0,4},{4,8},{8,12},{12,16},{16,20},{20,24},{24,28},{1,5},{5,9},{9,... | collective-permute-start | bytes 147464 | tf_op jit(solution)/shard_map/ppermute | solution.py:21
  8.7 0.6 copy-start.1
  75.0 30.5 %all-to-all-start.1 = ((bf16[8,1040,128]{2,1,0:T(8,128)(2,1)}), bf16[8,1040,128]{2,1,0:T(8,128)(2,1)S(1)}, u32[]{:S(2)}, u32[]{:S(2)}) async-start(bf16[8,1040,128]{2,1,0:T(8,128)(2,1)} %get-tuple-element.9), calls=%async_computation.1 | async-start | bytes 4259840 | tf_op jit(solution)/shard_map/all_to_all | solution.py:25
  79.5 3.1 %collective-permute-start.1 = (bf16[3,2,4096]{2,1,0:T(2,128)(2,1)S(1)}, bf16[3,2,4096]{2,1,0:T(2,128)(2,1)S(1)}, u32[]{:S(2)}, u32[]{:S(2)}) collective-permute-start(bf16[3,2,4096]{2,1,0:T(2,128)(2,1)S(1)} %pad_maximum_fusion.1), channel_id=1, source_target_pairs={{4,0},{8,4},{12,8},{16,12},{20,16},{24,20},{28,24},{5,1},{9,5},{13... | collective-permute-start | bytes 147464 | tf_op jit(solution)/shard_map/ppermute | solution.py:21
  82.7 22.8 %copy-start.2 = (bf16[3,2,4096]{2,1,0:T(2,128)(2,1)}, bf16[3,2,4096]{2,1,0:T(2,128)(2,1)S(1)}, u32[]{:S(2)}) copy-start(bf16[3,2,4096]{2,1,0:T(2,128)(2,1)S(1)} %collective-permute-done.1.after_ref) | copy-start | bytes 147460
  105.5 1.3 copy-start
  118.3 72.5 %collective-permute-start.2 = (bf16[3,128,4096]{2,1,0:T(8,128)(2,1)}, bf16[3,128,4096]{2,1,0:T(8,128)(2,1)S(1)}, u32[]{:S(2)}, u32[]{:S(2)}) collective-permute-start(bf16[3,128,4096]{2,1,0:T(8,128)(2,1)} %get-tuple-element.11), channel_id=1, source_target_pairs={{1,0},{2,1},{3,2},{5,4},{6,5},{7,6},{9,8},{10,9},{11,10},{13,12},{... | collective-permute-start | bytes 9437192 | tf_op jit(solution)/shard_map/ppermute | solution.py:21
  129.9 8.8 %all-to-all-start.2 = ((f32[8,1,32,128]{3,2,1,0:T(8,128)}), f32[8,1,32,128]{3,2,1,0:T(8,128)S(1)}, u32[]{:S(2)}, u32[]{:S(2)}) async-start(f32[8,1,32,128]{3,2,1,0:T(8,128)} %bitcast.34), calls=%async_computation.2 | async-start | bytes 262144 | tf_op jit(solution)/shard_map/all_to_all | solution.py:25
  140.2 10.3 %all-to-all-start.4 = ((f32[8,1,16,512]{3,2,1,0:T(8,128)}), f32[8,1,16,512]{3,2,1,0:T(8,128)S(1)}, u32[]{:S(2)}, u32[]{:S(2)}) async-start(f32[8,1,16,512]{3,2,1,0:T(8,128)} %broadcast_in_dim.14), calls=%async_computation.4 | async-start | bytes 524288 | tf_op jit(solution)/shard_map/all_to_all | solution.py:25

commit v2 on v1

v2 whole, which is shorter than its diff:
```python
import functools
import math

import jax
import jax.numpy as jnp
from jax import lax
from jax.experimental import pallas as pl
from jax.experimental.pallas import tpu as pltpu
from jax.sharding import PartitionSpec as P


F32 = jnp.float32
BF16 = jnp.bfloat16
GROUPS_AT_ONCE = 2
SPAN = 4
TILE = 16
LANES = 128


def passed_along(x, axis, by):
    count = lax.axis_size(axis)
    pairs = [(i, i + by) for i in range(count) if 0 <= i + by < count]
    return lax.ppermute(x, axis, pairs)


def exchange(x):
    return lax.all_to_all(x, "seq", split_axis=0, concat_axis=0, tiled=True)


def dot_nt(left, right):
    return lax.dot_general(
        left, right, (((1,), (1,)), ((), ())), preferred_element_type=F32
    )


def dot_nn(left, right):
    return lax.dot_general(
        left, right, (((1,), (0,)), ((), ())), preferred_element_type=F32
    )


def grid_index(shape, dim):
    return lax.broadcasted_iota(jnp.int32, shape, dim)


def identity(size):
    shape = (size, size)
    return (grid_index(shape, 0) == grid_index(shape, 1)).astype(F32).astype(BF16)


def patched_head(x, first_rows):
    return jnp.concatenate([first_rows, x[8:]], axis=0)


def patched_tail(x, last_rows):
    return jnp.concatenate([x[:-8], last_rows], axis=0)


def delayed(x, before):
    row = grid_index((8, x.shape[1]), 0)
    one = pltpu.roll(x, 1, 0)
    one = patched_head(one, jnp.where(row == 0, before[1:2], one[:8]))
    two = pltpu.roll(x, 2, 0)
    top = jnp.where(row == 0, before[0:1], jnp.where(row == 1, before[1:2], two[:8]))
    return one, patched_head(two, top)


def advanced(x, after):
    rows = x.shape[0]
    row = grid_index((8, x.shape[1]), 0)
    one = pltpu.roll(x, rows - 1, 0)
    one = patched_tail(one, jnp.where(row == 7, after[0:1], one[-8:]))
    two = pltpu.roll(x, rows - 2, 0)
    low = jnp.where(row == 7, after[1:2], jnp.where(row == 6, after[0:1], two[-8:]))
    return one, patched_tail(two, low)


def weighted(taps, branch, x, one, two):
    base = 3 * branch
    out = taps[base : base + 1] * x
    out = out + taps[base + 1 : base + 2] * one
    return out + taps[base + 2 : base + 3] * two


def next_featured(taps, branch, x, new):
    last = x[-8:][6:8]
    one = jnp.concatenate([last[1:2], new[0:1]], axis=0)
    return weighted(taps, branch, new, one, last)


def send_kernel(query_ref, key_ref, value_ref, grad_ref, before_ref, taps_ref, filter_ref, out_ref):
    seq, rows_out, _ = out_ref.shape
    groups = filter_ref.shape[0] // seq
    unit = identity(LANES)
    for d in range(seq):
        cols = pl.ds(d * LANES, LANES)
        taps = taps_ref[:, cols]
        feats = []
        for branch, ref in enumerate((query_ref, key_ref, value_ref)):
            x = ref[:, cols].astype(F32)
            one, two = delayed(x, before_ref[branch, :, cols].astype(F32))
            feats.append(weighted(taps, branch, x, one, two))
        product = (feats[1] * feats[2]).astype(BF16)
        scaled = (grad_ref[:, cols].astype(F32) * feats[0]).astype(BF16)
        out_ref[d, pl.ds(0, LANES), :] = dot_nt(unit, product).astype(BF16)
        out_ref[d, pl.ds(LANES, LANES), :] = dot_nt(unit, scaled).astype(BF16)
        taken = filter_ref[pl.ds(d * groups, groups), :]
        pad = jnp.zeros((rows_out - 2 * LANES - groups, LANES), F32)
        taken = jnp.concatenate([taken, pad], axis=0)
        out_ref[d, pl.ds(2 * LANES, rows_out - 2 * LANES), :] = taken.astype(BF16)


def toeplitz_blocks(lines):
    base = [
        pltpu.roll(jnp.broadcast_to(line, (8, LANES)), 0, 1, stride=1, stride_axis=0)
        for line in lines
    ]
    lane = grid_index((8, LANES), 1)
    sub = grid_index((8, LANES), 0)
    zero = jnp.zeros((8, LANES), F32)
    parts = [[] for _ in lines]
    for m in range(LANES // 8):
        below = zero
        for k, start in enumerate(base):
            turned = pltpu.roll(start, 8 * m, 1) if m else start
            parts[k].append(jnp.where(lane >= sub + 8 * m, turned, below))
            below = turned
    return [jnp.concatenate(part, axis=0).astype(BF16) for part in parts]


def diagonal_sums(cross, blocks):
    parts = [cross[:, k * LANES : (k + 1) * LANES] for k in range(blocks)]
    rows = LANES
    while rows > 8:
        half = rows // 2
        lane = grid_index((half, LANES), 1)
        turned = [pltpu.roll(part[half:rows], LANES - half, 1) for part in parts]
        turned.append(jnp.zeros((half, LANES), F32))
        parts = [
            parts[k][:half] + jnp.where(lane < LANES - half, turned[k], turned[k + 1])
            for k in range(blocks)
        ]
        rows = half
    lane = grid_index((8, LANES), 1)
    sub = grid_index((8, LANES), 0)
    turned = [pltpu.roll(part, LANES - 7, 1, stride=1, stride_axis=0) for part in parts]
    turned.append(jnp.zeros((8, LANES), F32))
    keep = lane < sub + (LANES - 7)
    return [
        jnp.sum(jnp.where(keep, turned[k], turned[k + 1]), axis=0, keepdims=True)
        for k in range(blocks)
    ]


def conv_kernel(groups, scale, in_ref, out_ref, corr_ref, taps):
    blocks = in_ref.shape[0]
    wide = LANES // groups
    rows = blocks * wide
    lane = grid_index((LANES, LANES), 1)
    sub = grid_index((LANES, LANES), 0)
    flipped = (sub // 8) * 8 + 7 - sub % 8
    flip = (lane == flipped).astype(F32).astype(BF16)
    taps[...] = in_ref[:, pl.ds(2 * LANES, in_ref.shape[1] - 2 * LANES), :].astype(F32)

    def one_group(g):
        at = pl.multiple_of(g * wide, wide)
        first = in_ref[:, pl.ds(at, wide), :].reshape(rows, LANES)
        second = in_ref[:, pl.ds(LANES + at, wide), :].reshape(rows, LANES)
        toeplitz = toeplitz_blocks([taps[k, pl.ds(g, 1), :] for k in range(blocks)])
        shifted, ahead = [first], [second]
        for k in range(1, blocks):
            gap = jnp.zeros((wide * k, LANES), BF16)
            shifted.append(jnp.concatenate([gap, first[: rows - wide * k]], axis=0))
            ahead.append(jnp.concatenate([second[wide * k :], gap], axis=0))
        ahead = jnp.concatenate(ahead, axis=1)
        conv = dot_nn(jnp.concatenate(shifted, axis=1), jnp.concatenate(toeplitz, axis=0))
        back = dot_nt(ahead, jnp.concatenate(toeplitz, axis=1))
        out_ref[:, pl.ds(at, wide), :] = conv.astype(BF16).reshape(blocks, wide, LANES)
        out_ref[:, pl.ds(LANES + at, wide), :] = back.astype(BF16).reshape(blocks, wide, LANES)
        cross = dot_nn(dot_nt(flip, first).astype(BF16), ahead)
        for k, line in enumerate(diagonal_sums(cross, blocks)):
            corr_ref[k, pl.ds(g, 1), :] = line * scale

    together = GROUPS_AT_ONCE if groups % GROUPS_AT_ONCE == 0 else 1

    def some_groups(step, carry):
        for part in range(together):
            one_group(step * together + part)
        return carry

    lax.fori_loop(0, groups // together, some_groups, 0)
    pick_row = grid_index((TILE, 2 * LANES), 0)
    pick_lane = grid_index((TILE, 2 * LANES), 1)
    wanted = (pick_row // 2) * LANES + pick_row % 2
    pick = ((pick_row < 4) & (pick_lane == wanted)).astype(F32).astype(BF16)
    for a in range(blocks):
        if a + 1 < blocks:
            both = [out_ref[a + 1, pl.ds(0, LANES), :], out_ref[a + 1, pl.ds(LANES, LANES), :]]
            line = dot_nt(pick, jnp.concatenate(both, axis=1)).astype(BF16)
        else:
            line = jnp.zeros((TILE, LANES), BF16)
        out_ref[a, pl.ds(2 * LANES, TILE), :] = line


def finish_kernel(
    scale, has_old, query_ref, key_ref, value_ref, grad_ref, before_ref, after_ref, taps_ref, in_ref, *refs
):
    layer_ref, late_ref, sums_ref = refs[1:] if has_old else refs
    rows = query_ref.shape[0]
    unit = identity(LANES)
    for part in range(in_ref.shape[0]):
        cols = pl.ds(part * LANES, LANES)
        taps = taps_ref[:, cols]
        conv = dot_nt(unit, in_ref[part, pl.ds(0, LANES), :])
        back = dot_nt(unit, in_ref[part, pl.ds(LANES, LANES), :])
        edge = in_ref[part, pl.ds(2 * LANES, TILE), :].astype(F32)
        grad = grad_ref[:, cols].astype(F32)
        lines = []

        def tap_lines(value, raw):
            for shifted in raw:
                lines.append(jnp.sum(value * shifted, axis=0, keepdims=True) * scale)

        x = query_ref[:, cols].astype(F32)
        raw = (x,) + delayed(x, before_ref[0, :, cols].astype(F32))
        layer_ref[:, cols] = (weighted(taps, 0, *raw) * conv).astype(BF16)
        value = grad * conv
        tap_lines(value, raw)
        follow = after_ref[2, :, cols].astype(F32) * edge[0:2]
        late_ref[pl.ds(0, rows), cols] = weighted(taps, 0, value, *advanced(value, follow)).astype(BF16)
        x = key_ref[:, cols].astype(F32)
        key_raw = (x,) + delayed(x, before_ref[1, :, cols].astype(F32))
        x = value_ref[:, cols].astype(F32)
        value_raw = (x,) + delayed(x, before_ref[2, :, cols].astype(F32))
        tap_lines(back * weighted(taps, 2, *value_raw), key_raw)
        tap_lines(back * weighted(taps, 1, *key_raw), value_raw)
        late_ref[pl.ds(rows, rows), cols] = back.astype(BF16)
        tail = jnp.concatenate([edge[2:4], jnp.zeros((TILE - 2, LANES), F32)], axis=0)
        late_ref[pl.ds(2 * rows, TILE), cols] = tail.astype(BF16)
        lines.append(jnp.zeros((TILE - 9, LANES), F32))
        sums_ref[:, cols] = jnp.concatenate(lines, axis=0)


def apply_kernel(has_old, key_ref, value_ref, before_ref, after_ref, taps_ref, late_ref, *refs):
    out_ref = refs[1] if has_old else refs[0]
    rows, width = key_ref.shape
    for part in range(width // LANES):
        cols = pl.ds(part * LANES, LANES)
        taps = taps_ref[:, cols]
        back = late_ref[pl.ds(rows, rows), cols].astype(F32)
        edge = late_ref[pl.ds(2 * rows, TILE), cols].astype(F32)[0:2]
        out_ref[0, :, cols] = late_ref[pl.ds(0, rows), cols]
        for branch, other, ref in ((1, 2, value_ref), (2, 1, key_ref)):
            x = ref[:, cols].astype(F32)
            one, two = delayed(x, before_ref[other, :, cols].astype(F32))
            value = back * weighted(taps, other, x, one, two)
            new = after_ref[other - 1, :, cols].astype(F32)
            follow = edge * next_featured(taps, other, x, new)
            out_ref[branch, :, cols] = weighted(taps, branch, value, *advanced(value, follow)).astype(BF16)


def summed(x, axis):
    count = lax.axis_size(axis)
    if count & (count - 1):
        return lax.psum(x, axis)
    step = 1
    while step < count:
        x = x + lax.ppermute(x, axis, [(i, i ^ step) for i in range(count)])
        step *= 2
    return x


def layer_step(query_in, key_in, value_in, grad_out, long_filter, short_taps):
    seq = lax.axis_size("seq")
    rows, width = query_in.shape[1:]
    groups = long_filter.shape[2]
    total_rows = rows * seq
    wide = width // groups
    across = LANES * seq
    chunks = width // across
    own_groups = LANES // wide
    chunk_groups = own_groups * seq
    height = 2 * LANES + TILE
    span = math.gcd(SPAN, seq)
    steps = seq // span
    query, key, value, grad = query_in[0], key_in[0], value_in[0], grad_out[0]
    taps = short_taps[0].reshape(9, width)
    last = jnp.stack([query[rows - 2 :], key[rows - 2 :], value[rows - 2 :]])
    before = passed_along(last, "seq", 1)
    top = jnp.stack([key[:2], value[:2], grad[:2]])
    after = passed_along(top, "seq", -1)
    filter_t = long_filter[0].T

    main = pl.BlockSpec((rows, across), lambda c: (0, c))
    sent = pl.pallas_call(
        send_kernel,
        grid=(chunks,),
        in_specs=[
            main, main, main, main,
            pl.BlockSpec((3, 2, across), lambda c: (0, 0, c)),
            pl.BlockSpec((9, across), lambda c: (0, c)),
            pl.BlockSpec((chunk_groups, rows), lambda c: (c, 0)),
        ],
        out_specs=pl.BlockSpec((seq, height, rows), lambda c: (0, c, 0)),
        out_shape=jax.ShapeDtypeStruct((seq, chunks * height, rows), BF16),
        name="send",
    )(query, key, value, grad, before, taps, filter_t)
    arrived = exchange(sent)

    early = {}
    for name, array in (
        ("key", key), ("value", value), ("before", before), ("after", after), ("taps", taps),
    ):
        early[name] = passed_along(array, "pipe", -1)

    layer, passed = None, None
    corr_parts, sum_parts = [], []
    for chunk in range(chunks):
        returned, corr = pl.pallas_call(
            functools.partial(conv_kernel, own_groups, 1.0 / math.sqrt(total_rows * wide)),
            grid=(1,),
            in_specs=[pl.BlockSpec((seq, height, rows), lambda i, chunk=chunk: (0, chunk, 0))],
            out_specs=[
                pl.BlockSpec((seq, height, rows), lambda i: (0, 0, 0)),
                pl.BlockSpec((seq, own_groups, rows), lambda i: (0, 0, 0)),
            ],
            out_shape=[
                jax.ShapeDtypeStruct((seq, height, rows), BF16),
                jax.ShapeDtypeStruct((seq, own_groups, rows), F32),
            ],
            scratch_shapes=[pltpu.VMEM((seq, TILE, LANES), F32)],
            name="conv",
        )(arrived)
        back = exchange(returned)
        corr_parts.append(corr)
        at = lambda i, chunk=chunk: (0, chunk * steps + i)
        at3 = lambda i, chunk=chunk: (0, 0, chunk * steps + i)
        main = pl.BlockSpec((rows, span * LANES), at)
        edge = pl.BlockSpec((3, 2, span * LANES), at3)
        tap_spec = pl.BlockSpec((9, span * LANES), at)
        here = pl.BlockSpec((2 * rows + TILE, span * LANES), lambda i: (0, i))
        has_old = layer is not None
        old = [pl.BlockSpec(memory_space=pl.ANY)] * has_old
        layer, late, sums = pl.pallas_call(
            functools.partial(finish_kernel, 1.0 / math.sqrt(total_rows), has_old),
            grid=(steps,),
            in_specs=[
                main, main, main, main, edge, edge, tap_spec,
                pl.BlockSpec((span, height, rows), lambda i: (i, 0, 0)),
            ]
            + old,
            out_specs=[main, here, pl.BlockSpec((TILE, span * LANES), lambda i: (0, i))],
            out_shape=[
                jax.ShapeDtypeStruct((rows, width), BF16),
                jax.ShapeDtypeStruct((2 * rows + TILE, across), BF16),
                jax.ShapeDtypeStruct((TILE, across), F32),
            ],
            input_output_aliases={8: 0} if has_old else {},
            name="finish",
        )(query, key, value, grad, before, after, taps, back, *([layer] * has_old))
        late = passed_along(late, "pipe", -1)
        sum_parts.append(sums)
        passed = pl.pallas_call(
            functools.partial(apply_kernel, has_old),
            grid=(steps,),
            in_specs=[main, main, edge, edge, tap_spec, here] + old,
            out_specs=pl.BlockSpec((3, rows, span * LANES), at3),
            out_shape=jax.ShapeDtypeStruct((3, rows, width), BF16),
            input_output_aliases={6: 0} if has_old else {},
            name="apply",
        )(
            early["key"], early["value"], early["before"], early["after"], early["taps"], late,
            *([passed] * has_old),
        )

    corr = exchange(jnp.concatenate(corr_parts, axis=1))
    corr = corr.reshape(seq, chunks, own_groups, rows)
    filter_grad = jnp.transpose(corr, (3, 1, 0, 2)).reshape(rows, groups)
    some = [summed(jnp.concatenate(sum_parts[:-1], axis=1), "seq")] if chunks > 1 else []
    some.append(summed(sum_parts[-1], "seq"))
    tap_grads = jnp.concatenate(some, axis=1)[:9].reshape(3, 3, width)
    return (layer[None], passed[None], filter_grad[None], tap_grads[None])


def solution(mesh):
    in_specs = (
        P("pipe", "seq", None),
        P("pipe", "seq", None),
        P("pipe", "seq", None),
        P("pipe", "seq", None),
        P("pipe", "seq", None),
        P("pipe", None, None, None),
    )
    out_specs = (
        P("pipe", "seq", None),
        P("pipe", None, "seq", None),
        P("pipe", "seq", None),
        P("pipe", None, None, None),
    )
    return jax.shard_map(layer_step, mesh=mesh, in_specs=in_specs, out_specs=out_specs, check_vma=False)
```

time: 194 us -> 207 us (1.067)
  waiting for transfers between devices: 75 us -> 38.1 us
  starting transfers between devices: 15.4 us -> 43.1 us
  Pallas kernels: 44.8 us -> 61.1 us
  local copies, waits for them, and re-layouts: 11.9 us -> 15.7 us
  other arithmetic: 2.1 us -> 5.11 us
    all_to_all x3 -> x4, waiting for transfers between devices: 33.7 us -> 5.38 us  [exchange(): return lax.all_to_all(x, 'seq', split_axis=0, concat_axis=0, tiled=True)]
    ppermute x3 -> x11, waiting for transfers between devices: 41.2 us -> 22.9 us  [passed_along(): return lax.ppermute(x, axis, pairs)]
    pallas_call x3 -> x13, Pallas kernels: 44.8 us -> 61.1 us  [the longest x4 29.2 us: layer_step(): pl.pallas_call(functools.partial(conv_kernel, own_groups, 1.0 / math.sqrt...]
    ppermute x0 -> x6, starting transfers between devices: none -> 11.7 us  [summed(): x = x + lax.ppermute(x, axis, [(i, i ^ step) for i in range(count)])]
    ppermute x3 -> x11, starting transfers between devices: 4.98 us -> 15.3 us  [passed_along(): return lax.ppermute(x, axis, pairs)]
    ppermute x0 -> x6, waiting for transfers between devices: none -> 9.9 us  [summed(): x = x + lax.ppermute(x, axis, [(i, i ^ step) for i in range(count)])]
    all_to_all x3 -> x4, starting transfers between devices: 10.4 us -> 16.1 us  [exchange(): return lax.all_to_all(x, 'seq', split_axis=0, concat_axis=0, tiled=True)]
    unnamed x9 -> x34, local copies, waits for them, and re-layouts: 6.05 us -> 9.07 us
  transfers between devices with their start and end apart: 6 -> 21, of which waited for: 5 -> 11; matrix products, arithmetic and copies ran while one was open for 4% -> 7% of each run, Pallas kernels for 0% -> 23%
where the time goes in v2:
time: 207 us; the launch traced here: 205 us
  Pallas kernels  61.1 us (30%)
  starting transfers between devices  43.1 us (21%)
  blocking collectives  41 us (20%)
  waiting for transfers between devices  38.1 us (18%)
  local copies, waits for them, and re-layouts  15.7 us (8%)
  other arithmetic  5.11 us (2%)
    all_to_all x2, blocking collectives, exchange(): return lax.all_to_all(x, 'seq', split_axis=0, concat_axis=0, tiled=True)  41 us
    pallas_call x4, Pallas kernels, layer_step(): pl.pallas_call(functools.partial(conv_kernel, own_groups, 1.0 / math.sqrt...  29.2 us
    ppermute x11, waiting for transfers between devices, passed_along(): return lax.ppermute(x, axis, pairs)  22.9 us
    all_to_all x4, starting transfers between devices, exchange(): return lax.all_to_all(x, 'seq', split_axis=0, concat_axis=0, tiled=True)  16.1 us
    ppermute x11, starting transfers between devices, passed_along(): return lax.ppermute(x, axis, pairs)  15.3 us
    pallas_call x4, Pallas kernels, layer_step(): pl.pallas_call(functools.partial(finish_kernel, 1.0 / math.sqrt(total_row...  14.8 us
    ppermute x6, starting transfers between devices, summed(): x = x + lax.ppermute(x, axis, [(i, i ^ step) for i in range(count)])  11.7 us
    pallas_call x4, Pallas kernels, layer_step(): pl.pallas_call(functools.partial(apply_kernel, has_old), grid=(steps,), i...  11 us
  transfers between devices with their start and end apart: 21, of which 11 were waited for; matrix products, arithmetic and copies ran while one was open for 7% of the time, Pallas kernels for 23%

profile of v2, /device:TPU:0, one launch (start us, length us, event | category | flops | bytes accessed | tf_op | source)
XLA Modules:
  0.0 205.0 jit_solution(2413251506813396323)
XLA Ops:
  10.2 6.1 %send.1 = bf16[8,1088,128]{2,1,0:T(8,128)(2,1)} custom-call(bf16[128,4096]{1,0:T(8,128)(2,1)} %bitcast.26, bf16[128,4096]{1,0:T(8,128)(2,1)} %bitcast.14, bf16[128,4096]{1,0:T(8,128)(2,1)} %bitcast.20, bf16[128,4096]{1,0:T(8,128)(2,1)} %bitcast.31, bf16[3,2,4096]{2,1,0:T(2,128)(2,1)} %copy-done.5, f32[9,4096]{1,0:T(8,128)} %reshape_squeeze.3.taps_ref, ...), custom_call_target="tpu_custom_call" | custom-call | tf_op jit(solution)/shard_map/send/pallas_call | solution.py:295
  16.3 33.1 %all_to_all.30.in_ref = bf16[8,1088,128]{2,1,0:T(8,128)(2,1)} all-to-all(bf16[8,1088,128]{2,1,0:T(8,128)(2,1)} %send.1), channel_id=1, replica_groups=mesh['seq'=8,'pipe'=4] {'seq'}, dimensions={0} | all-to-all | bytes 4456448 | tf_op jit(solution)/shard_map/all_to_all | solution.py:27
  49.4 7.3 %conv.7 = (bf16[8,272,128]{2,1,0:T(8,128)(2,1)}, f32[8,8,128]{2,1,0:T(8,128)}) custom-call(bf16[8,1088,128]{2,1,0:T(8,128)(2,1)} %all_to_all.30.in_ref), custom_call_target="tpu_custom_call" | custom-call | tf_op jit(solution)/shard_map/conv/pallas_call | solution.py:319
  56.6 3.5 %all-to-all-start.4 = ((bf16[8,272,128]{2,1,0:T(8,128)(2,1)}), bf16[8,272,128]{2,1,0:T(8,128)(2,1)S(1)}, u32[]{:S(2)}, u32[]{:S(2)}) async-start(bf16[8,272,128]{2,1,0:T(8,128)(2,1)} %get-tuple-element.27), calls=%async_computation.4 | async-start | bytes 1114112 | tf_op jit(solution)/shard_map/all_to_all | solution.py:27
  60.2 7.4 %conv.6 = (bf16[8,272,128]{2,1,0:T(8,128)(2,1)}, f32[8,8,128]{2,1,0:T(8,128)}) custom-call(bf16[8,1088,128]{2,1,0:T(8,128)(2,1)} %all_to_all.30.in_ref), custom_call_target="tpu_custom_call" | custom-call | tf_op jit(solution)/shard_map/conv/pallas_call | solution.py:319
  70.2 4.2 %all-to-all-start.3 = ((bf16[8,272,128]{2,1,0:T(8,128)(2,1)}), bf16[8,272,128]{2,1,0:T(8,128)(2,1)}, u32[]{:S(2)}, u32[]{:S(2)}) async-start(bf16[8,272,128]{2,1,0:T(8,128)(2,1)} %get-tuple-element.26), calls=%async_computation.3 | async-start | bytes 1114112 | tf_op jit(solution)/shard_map/all_to_all | solution.py:27
  74.4 7.3 %conv.5 = (bf16[8,272,128]{2,1,0:T(8,128)(2,1)}, f32[8,8,128]{2,1,0:T(8,128)}) custom-call(bf16[8,1088,128]{2,1,0:T(8,128)(2,1)} %all_to_all.30.in_ref), custom_call_target="tpu_custom_call" | custom-call | tf_op jit(solution)/shard_map/conv/pallas_call | solution.py:319
  81.6 2.8 %all-to-all-done.3.in_ref = bf16[8,272,128]{2,1,0:T(8,128)(2,1)} async-done(((bf16[8,272,128]{2,1,0:T(8,128)(2,1)}), bf16[8,272,128]{2,1,0:T(8,128)(2,1)}, u32[]{:S(2)}, u32[]{:S(2)}) %all-to-all-start.3) | async-done | bytes 557088 | tf_op jit(solution)/shard_map/all_to_all | solution.py:27
  84.5 4.2 %all-to-all-start.2 = ((bf16[8,272,128]{2,1,0:T(8,128)(2,1)}), bf16[8,272,128]{2,1,0:T(8,128)(2,1)}, u32[]{:S(2)}, u32[]{:S(2)}) async-start(bf16[8,272,128]{2,1,0:T(8,128)(2,1)} %get-tuple-element.25), calls=%async_computation.2 | async-start | bytes 1114112 | tf_op jit(solution)/shard_map/all_to_all | solution.py:27
  92.1 7.3 %conv.4 = (bf16[8,272,128]{2,1,0:T(8,128)(2,1)}, f32[8,8,128]{2,1,0:T(8,128)}) custom-call(bf16[8,1088,128]{2,1,0:T(8,128)(2,1)} %all_to_all.30.in_ref), custom_call_target="tpu_custom_call" | custom-call | tf_op jit(solution)/shard_map/conv/pallas_call | solution.py:319
  99.4 4.2 %all-to-all-start.1 = ((bf16[8,272,128]{2,1,0:T(8,128)(2,1)}), bf16[8,272,128]{2,1,0:T(8,128)(2,1)}, u32[]{:S(2)}, u32[]{:S(2)}) async-start(bf16[8,272,128]{2,1,0:T(8,128)(2,1)} %get-tuple-element.24), calls=%async_computation.1 | async-start | bytes 1114112 | tf_op jit(solution)/shard_map/all_to_all | solution.py:27
  107.4 3.7 %finish.4 = (bf16[128,4096]{1,0:T(8,128)(2,1)}, bf16[272,1024]{1,0:T(8,128)(2,1)}, f32[16,1024]{1,0:T(8,128)}) custom-call(bf16[128,4096]{1,0:T(8,128)(2,1)} %bitcast.27, bf16[128,4096]{1,0:T(8,128)(2,1)} %bitcast.15, bf16[128,4096]{1,0:T(8,128)(2,1)} %bitcast.21, bf16[128,4096]{1,0:T(8,128)(2,1)} %bitcast.32, bf16[3,2,4096]{2,1,0:T(2,128)(2,1)} %copy-done.5, ...), custom_call_target="tpu_custom_call" | custom-call | tf_op jit(solution)/shard_map/finish/pallas_call | solution.py:344
  111.1 3.7 %finish.5 = (bf16[128,4096]{1,0:T(8,128)(2,1)}, bf16[272,1024]{1,0:T(8,128)(2,1)}, f32[16,1024]{1,0:T(8,128)}) custom-call(bf16[128,4096]{1,0:T(8,128)(2,1)} %bitcast.28, bf16[128,4096]{1,0:T(8,128)(2,1)} %bitcast.16, bf16[128,4096]{1,0:T(8,128)(2,1)} %bitcast.22, bf16[128,4096]{1,0:T(8,128)(2,1)} %bitcast.33, ...), custom_call_target="tpu_custom_call", output_to_operand_aliasing={{0}: (8, {})} | custom-call | tf_op jit(solution)/shard_map/finish/pallas_call | solution.py:344
  114.8 3.7 %finish.6 = (bf16[128,4096]{1,0:T(8,128)(2,1)}, bf16[272,1024]{1,0:T(8,128)(2,1)}, f32[16,1024]{1,0:T(8,128)}) custom-call(bf16[128,4096]{1,0:T(8,128)(2,1)} %bitcast.29, bf16[128,4096]{1,0:T(8,128)(2,1)} %bitcast.17, bf16[128,4096]{1,0:T(8,128)(2,1)} %bitcast.23, bf16[128,4096]{1,0:T(8,128)(2,1)} %bitcast.34, ...), custom_call_target="tpu_custom_call", output_to_operand_aliasing={{0}: (8, {})} | custom-call | tf_op jit(solution)/shard_map/finish/pallas_call | solution.py:344
  123.0 6.6 %collective-permute-start.11 = (f32[16,3072]{1,0:T(8,128)}, f32[16,3072]{1,0:T(8,128)}, u32[]{:S(2)}, u32[]{:S(2)}) collective-permute-start(f32[16,3072]{1,0:T(8,128)} %constant_dynamic-update-slice_fusion), channel_id=1, source_target_pairs={{0,4},{4,0},{8,12},{12,8},{16,20},{20,16},{24,28},{28,24},{1,5},{5... | collective-permute-start | bytes 589832 | tf_op jit(solution)/shard_map/ppermute | solution.py:268
  132.2 3.7 %finish.7 = (bf16[128,4096]{1,0:T(8,128)(2,1)}, bf16[272,1024]{1,0:T(8,128)(2,1)}, f32[16,1024]{1,0:T(8,128)}) custom-call(bf16[128,4096]{1,0:T(8,128)(2,1)} %bitcast.30, bf16[128,4096]{1,0:T(8,128)(2,1)} %bitcast.18, bf16[128,4096]{1,0:T(8,128)(2,1)} %bitcast.24, bf16[128,4096]{1,0:T(8,128)(2,1)} %bitcast.35, ...), custom_call_target="tpu_custom_call", output_to_operand_aliasing={{0}: (8, {})} | custom-call | tf_op jit(solution)/shard_map/finish/pallas_call | solution.py:344
  135.9 4.2 %collective-permute-done.4.before_ref = bf16[3,2,4096]{2,1,0:T(2,128)(2,1)S(1)} collective-permute-done((bf16[3,2,4096]{2,1,0:T(2,128)(2,1)S(1)}, bf16[3,2,4096]{2,1,0:T(2,128)(2,1)S(1)}, u32[]{:S(2)}, u32[]{:S(2)}) %collective-permute-start.4) | collective-permute-done | bytes 49184 | tf_op jit(solution)/shard_map/ppermute | solution.py:23
  143.7 3.8 %collective-permute-done.5.after_ref = bf16[3,2,4096]{2,1,0:T(2,128)(2,1)S(1)} collective-permute-done((bf16[3,2,4096]{2,1,0:T(2,128)(2,1)S(1)}, bf16[3,2,4096]{2,1,0:T(2,128)(2,1)S(1)}, u32[]{:S(2)}, u32[]{:S(2)}) %collective-permute-start.5) | collective-permute-done | bytes 49184 | tf_op jit(solution)/shard_map/ppermute | solution.py:23
  156.0 5.5 %collective-permute-done.12 = f32[16,3072]{1,0:T(8,128)S(1)} collective-permute-done((f32[16,3072]{1,0:T(8,128)S(1)}, f32[16,3072]{1,0:T(8,128)S(1)}, u32[]{:S(2)}, u32[]{:S(2)}) %collective-permute-start.12) | collective-permute-done | bytes 196640 | tf_op jit(solution)/shard_map/ppermute | solution.py:268
  163.0 2.9 %collective-permute-done.16 = f32[16,1024]{1,0:T(8,128)S(1)} collective-permute-done((f32[16,1024]{1,0:T(8,128)S(1)}, f32[16,1024]{1,0:T(8,128)S(1)}, u32[]{:S(2)}, u32[]{:S(2)}) %collective-permute-start.16) | collective-permute-done | bytes 65568 | tf_op jit(solution)/shard_map/ppermute | solution.py:268
  168.2 7.9 %all_to_all.31 = f32[8,32,128]{2,1,0:T(8,128)S(1)} all-to-all(f32[8,32,128]{2,1,0:T(8,128)S(1)} %pad_maximum_fusion.1), channel_id=1, replica_groups=mesh['seq'=8,'pipe'=4] {'seq'}, dimensions={0} | all-to-all | bytes 262144 | tf_op jit(solution)/shard_map/all_to_all | solution.py:27
  182.5 2.8 %apply.5.refs_0_ = bf16[3,128,4096]{2,1,0:T(8,128)(2,1)} custom-call(bf16[128,4096]{1,0:T(8,128)(2,1)} %copy-done.2, bf16[128,4096]{1,0:T(8,128)(2,1)} %collective-permute-done.3.value_ref, bf16[3,2,4096]{2,1,0:T(2,128)(2,1)} %copy-done.7, bf16[3,2,4096]{2,1,0:T(2,128)(2,1)} %copy-done.8, ...), custom_call_target="tpu_custom_call", output_to_operand_aliasing={{}: (6, {})} | custom-call | tf_op jit(solution)/shard_map/apply/pallas_call | solution.py:363
  185.3 5.6 %collective-permute-done.8.late_ref = bf16[272,1024]{1,0:T(8,128)(2,1)S(1)} collective-permute-done((bf16[272,1024]{1,0:T(8,128)(2,1)}, bf16[272,1024]{1,0:T(8,128)(2,1)S(1)}, u32[]{:S(2)}, u32[]{:S(2)}) %collective-permute-start.8) | collective-permute-done | bytes 557088 | tf_op jit(solution)/shard_map/ppermute | solution.py:23
  194.5 6.1 %collective-permute-done.7.late_ref = bf16[272,1024]{1,0:T(8,128)(2,1)S(1)} collective-permute-done((bf16[272,1024]{1,0:T(8,128)(2,1)}, bf16[272,1024]{1,0:T(8,128)(2,1)S(1)}, u32[]{:S(2)}, u32[]{:S(2)}) %collective-permute-start.7) | collective-permute-done | bytes 557088 | tf_op jit(solution)/shard_map/ppermute | solution.py:23
  (86 shorter events, 56.5 us)
Async XLA Ops:
  3.4 6.2 %collective-permute-start = (bf16[3,2,4096]{2,1,0:T(2,128)(2,1)S(1)}, bf16[3,2,4096]{2,1,0:T(2,128)(2,1)S(1)}, u32[]{:S(2)}, u32[]{:S(2)}) collective-permute-start(bf16[3,2,4096]{2,1,0:T(2,128)(2,1)S(1)} %pad_maximum_fusion.2), channel_id=1, source_target_pairs={{0,4},{4,8},{8,12},{12,16},{16,20},{20,24},{24,28},{1,5},{5,9},{9,... | collective-permute-start | bytes 147464 | tf_op jit(solution)/shard_map/ppermute | solution.py:23
  56.6 13.5 %all-to-all-start.4 = ((bf16[8,272,128]{2,1,0:T(8,128)(2,1)}), bf16[8,272,128]{2,1,0:T(8,128)(2,1)S(1)}, u32[]{:S(2)}, u32[]{:S(2)}) async-start(bf16[8,272,128]{2,1,0:T(8,128)(2,1)} %get-tuple-element.27), calls=%async_computation.4 | async-start | bytes 1114112 | tf_op jit(solution)/shard_map/all_to_all | solution.py:27
  60.2 29.8 %copy-start.1 = (bf16[1,128,4096]{2,1,0:T(8,128)(2,1)S(1)}, bf16[1,128,4096]{2,1,0:T(8,128)(2,1)}, u32[]{:S(2)}) copy-start(bf16[1,128,4096]{2,1,0:T(8,128)(2,1)} %param.8) | copy-start | bytes 3145732
  70.2 14.3 %all-to-all-start.3 = ((bf16[8,272,128]{2,1,0:T(8,128)(2,1)}), bf16[8,272,128]{2,1,0:T(8,128)(2,1)}, u32[]{:S(2)}, u32[]{:S(2)}) async-start(bf16[8,272,128]{2,1,0:T(8,128)(2,1)} %get-tuple-element.26), calls=%async_computation.3 | async-start | bytes 1114112 | tf_op jit(solution)/shard_map/all_to_all | solution.py:27
  84.5 14.9 %all-to-all-start.2 = ((bf16[8,272,128]{2,1,0:T(8,128)(2,1)}), bf16[8,272,128]{2,1,0:T(8,128)(2,1)}, u32[]{:S(2)}, u32[]{:S(2)}) async-start(bf16[8,272,128]{2,1,0:T(8,128)(2,1)} %get-tuple-element.25), calls=%async_computation.2 | async-start | bytes 1114112 | tf_op jit(solution)/shard_map/all_to_all | solution.py:27
  88.7 62.1 %collective-permute-start.2 = (bf16[128,4096]{1,0:T(8,128)(2,1)S(1)}, bf16[128,4096]{1,0:T(8,128)(2,1)S(1)}, u32[]{:S(2)}, u32[]{:S(2)}) collective-permute-start(bf16[128,4096]{1,0:T(8,128)(2,1)S(1)} %bitcast.19), channel_id=1, source_target_pairs={{1,0},{2,1},{3,2},{5,4},{6,5},{7,6},{9,8},{10,9},{11,10},{13,12},{... | collective-permute-start | bytes 3145736 | tf_op jit(solution)/shard_map/ppermute | solution.py:23
  90.0 62.1 %collective-permute-start.3 = (bf16[128,4096]{1,0:T(8,128)(2,1)S(1)}, bf16[128,4096]{1,0:T(8,128)(2,1)}, u32[]{:S(2)}, u32[]{:S(2)}) collective-permute-start(bf16[128,4096]{1,0:T(8,128)(2,1)S(1)} %bitcast.25), channel_id=1, source_target_pairs={{1,0},{2,1},{3,2},{5,4},{6,5},{7,6},{9,8},{10,9},{11,10},{13,12},{... | collective-permute-start | bytes 3145736 | tf_op jit(solution)/shard_map/ppermute | solution.py:23
  99.4 32.8 %all-to-all-start.1 = ((bf16[8,272,128]{2,1,0:T(8,128)(2,1)}), bf16[8,272,128]{2,1,0:T(8,128)(2,1)}, u32[]{:S(2)}, u32[]{:S(2)}) async-start(bf16[8,272,128]{2,1,0:T(8,128)(2,1)} %get-tuple-element.24), calls=%async_computation.1 | async-start | bytes 1114112 | tf_op jit(solution)/shard_map/all_to_all | solution.py:27
  103.7 3.1 %collective-permute-start.1 = (bf16[3,2,4096]{2,1,0:T(2,128)(2,1)S(1)}, bf16[3,2,4096]{2,1,0:T(2,128)(2,1)S(1)}, u32[]{:S(2)}, u32[]{:S(2)}) collective-permute-start(bf16[3,2,4096]{2,1,0:T(2,128)(2,1)S(1)} %pad_maximum_fusion.3), channel_id=1, source_target_pairs={{4,0},{8,4},{12,8},{16,12},{20,16},{24,20},{28,24},{5,1},{9,5},{13... | collective-permute-start | bytes 147464 | tf_op jit(solution)/shard_map/ppermute | solution.py:23
  123.0 30.4 %collective-permute-start.11 = (f32[16,3072]{1,0:T(8,128)}, f32[16,3072]{1,0:T(8,128)}, u32[]{:S(2)}, u32[]{:S(2)}) collective-permute-start(f32[16,3072]{1,0:T(8,128)} %constant_dynamic-update-slice_fusion), channel_id=1, source_target_pairs={{0,4},{4,0},{8,12},{12,8},{16,20},{20,16},{24,28},{28,24},{1,5},{5... | collective-permute-start | bytes 589832 | tf_op jit(solution)/shard_map/ppermute | solution.py:268
  129.6 10.5 %collective-permute-start.4 = (bf16[3,2,4096]{2,1,0:T(2,128)(2,1)S(1)}, bf16[3,2,4096]{2,1,0:T(2,128)(2,1)S(1)}, u32[]{:S(2)}, u32[]{:S(2)}) collective-permute-start(bf16[3,2,4096]{2,1,0:T(2,128)(2,1)S(1)} %copy-done.6), channel_id=1, source_target_pairs={{1,0},{2,1},{3,2},{5,4},{6,5},{7,6},{9,8},{10,9},{11,10},{13,12},{... | collective-permute-start | bytes 147464 | tf_op jit(solution)/shard_map/ppermute | solution.py:23
  130.9 18.6 %collective-permute-start.6 = (f32[9,4096]{1,0:T(8,128)S(1)}, f32[9,4096]{1,0:T(8,128)}, u32[]{:S(2)}, u32[]{:S(2)}) collective-permute-start(f32[9,4096]{1,0:T(8,128)S(1)} %copy-done.3), channel_id=1, source_target_pairs={{1,0},{2,1},{3,2},{5,4},{6,5},{7,6},{9,8},{10,9},{11,10},{13,12},{... | collective-permute-start | bytes 442376 | tf_op jit(solution)/shard_map/ppermute | solution.py:23
  140.1 38.9 %copy-start.7 = (bf16[3,2,4096]{2,1,0:T(2,128)(2,1)}, bf16[3,2,4096]{2,1,0:T(2,128)(2,1)S(1)}, u32[]{:S(2)}) copy-start(bf16[3,2,4096]{2,1,0:T(2,128)(2,1)S(1)} %collective-permute-done.4.before_ref) | copy-start | bytes 147460
  140.1 1.5 collective-permute-start.14
  141.6 6.0 %collective-permute-start.5 = (bf16[3,2,4096]{2,1,0:T(2,128)(2,1)S(1)}, bf16[3,2,4096]{2,1,0:T(2,128)(2,1)S(1)}, u32[]{:S(2)}, u32[]{:S(2)}) collective-permute-start(bf16[3,2,4096]{2,1,0:T(2,128)(2,1)S(1)} %copy-done.10), channel_id=1, source_target_pairs={{1,0},{2,1},{3,2},{5,4},{6,5},{7,6},{9,8},{10,9},{11,10},{13,12},{... | collective-permute-start | bytes 147464 | tf_op jit(solution)/shard_map/ppermute | solution.py:23
  147.6 31.4 %copy-start.8 = (bf16[3,2,4096]{2,1,0:T(2,128)(2,1)}, bf16[3,2,4096]{2,1,0:T(2,128)(2,1)S(1)}, u32[]{:S(2)}) copy-start(bf16[3,2,4096]{2,1,0:T(2,128)(2,1)S(1)} %collective-permute-done.5.after_ref) | copy-start | bytes 147460
  147.6 8.2 %collective-permute-start.15 = (f32[16,1024]{1,0:T(8,128)S(1)}, f32[16,1024]{1,0:T(8,128)S(1)}, u32[]{:S(2)}, u32[]{:S(2)}) collective-permute-start(f32[16,1024]{1,0:T(8,128)S(1)} %add.21), channel_id=1, source_target_pairs={{0,8},{4,12},{8,0},{12,4},{16,24},{20,28},{24,16},{28,20},{1,9},{5... | collective-permute-start | bytes 196616 | tf_op jit(solution)/shard_map/ppermute | solution.py:268
  149.4 33.1 %collective-permute-start.9 = (bf16[272,1024]{1,0:T(8,128)(2,1)}, bf16[272,1024]{1,0:T(8,128)(2,1)}, u32[]{:S(2)}, u32[]{:S(2)}) collective-permute-start(bf16[272,1024]{1,0:T(8,128)(2,1)} %get-tuple-element.34), channel_id=1, source_target_pairs={{1,0},{2,1},{3,2},{5,4},{6,5},{7,6},{9,8},{10,9},{11,10},{13,12},{... | collective-permute-start | bytes 1671176 | tf_op jit(solution)/shard_map/ppermute | solution.py:23
  150.7 28.2 %collective-permute-start.10 = (bf16[272,1024]{1,0:T(8,128)(2,1)}, bf16[272,1024]{1,0:T(8,128)(2,1)S(1)}, u32[]{:S(2)}, u32[]{:S(2)}) collective-permute-start(bf16[272,1024]{1,0:T(8,128)(2,1)} %get-tuple-element.35), channel_id=1, source_target_pairs={{1,0},{2,1},{3,2},{5,4},{6,5},{7,6},{9,8},{10,9},{11,10},{13,12},{... | collective-permute-start | bytes 1671176 | tf_op jit(solution)/shard_map/ppermute | solution.py:23
  152.1 38.8 %collective-permute-start.8 = (bf16[272,1024]{1,0:T(8,128)(2,1)}, bf16[272,1024]{1,0:T(8,128)(2,1)S(1)}, u32[]{:S(2)}, u32[]{:S(2)}) collective-permute-start(bf16[272,1024]{1,0:T(8,128)(2,1)} %get-tuple-element.33), channel_id=1, source_target_pairs={{1,0},{2,1},{3,2},{5,4},{6,5},{7,6},{9,8},{10,9},{11,10},{13,12},{... | collective-permute-start | bytes 1671176 | tf_op jit(solution)/shard_map/ppermute | solution.py:23
  153.4 47.2 %collective-permute-start.7 = (bf16[272,1024]{1,0:T(8,128)(2,1)}, bf16[272,1024]{1,0:T(8,128)(2,1)S(1)}, u32[]{:S(2)}, u32[]{:S(2)}) collective-permute-start(bf16[272,1024]{1,0:T(8,128)(2,1)} %get-tuple-element.32), channel_id=1, source_target_pairs={{1,0},{2,1},{3,2},{5,4},{6,5},{7,6},{9,8},{10,9},{11,10},{13,12},{... | collective-permute-start | bytes 1671176 | tf_op jit(solution)/shard_map/ppermute | solution.py:23
  155.7 5.7 %collective-permute-start.12 = (f32[16,3072]{1,0:T(8,128)S(1)}, f32[16,3072]{1,0:T(8,128)S(1)}, u32[]{:S(2)}, u32[]{:S(2)}) collective-permute-start(f32[16,3072]{1,0:T(8,128)S(1)} %add.18), channel_id=1, source_target_pairs={{0,8},{4,12},{8,0},{12,4},{16,24},{20,28},{24,16},{28,20},{1,9},{5... | collective-permute-start | bytes 589832 | tf_op jit(solution)/shard_map/ppermute | solution.py:268
  161.5 4.4 %collective-permute-start.16 = (f32[16,1024]{1,0:T(8,128)S(1)}, f32[16,1024]{1,0:T(8,128)S(1)}, u32[]{:S(2)}, u32[]{:S(2)}) collective-permute-start(f32[16,1024]{1,0:T(8,128)S(1)} %add.22), channel_id=1, source_target_pairs={{0,16},{4,20},{8,24},{12,28},{16,0},{20,4},{24,8},{28,12},{1,17},{... | collective-permute-start | bytes 196616 | tf_op jit(solution)/shard_map/ppermute | solution.py:268
  165.9 38.2 %collective-permute-start.13 = (f32[16,3072]{1,0:T(8,128)S(1)}, f32[16,3072]{1,0:T(8,128)S(1)}, u32[]{:S(2)}, u32[]{:S(2)}) collective-permute-start(f32[16,3072]{1,0:T(8,128)S(1)} %add.19), channel_id=1, source_target_pairs={{0,16},{4,20},{8,24},{12,28},{16,0},{20,4},{24,8},{28,12},{1,17},{... | collective-permute-start | bytes 589832 | tf_op jit(solution)/shard_map/ppermute | solution.py:268
  (12 other events, 127.0 us)

commit v3 on v2

v3 whole, which is shorter than its diff:
```python
import functools
import math

import jax
import jax.numpy as jnp
from jax import lax
from jax.experimental import pallas as pl
from jax.experimental.pallas import tpu as pltpu
from jax.sharding import PartitionSpec as P


F32 = jnp.float32
BF16 = jnp.bfloat16
SPAN = 4
TILE = 16
LANES = 128


def passed_along(x, axis, by):
    count = lax.axis_size(axis)
    pairs = [(i, i + by) for i in range(count) if 0 <= i + by < count]
    return lax.ppermute(x, axis, pairs)


def exchange(x):
    return lax.all_to_all(x, "seq", split_axis=0, concat_axis=0, tiled=True)


def dot_nt(left, right):
    return lax.dot_general(
        left, right, (((1,), (1,)), ((), ())), preferred_element_type=F32
    )


def dot_nn(left, right):
    return lax.dot_general(
        left, right, (((1,), (0,)), ((), ())), preferred_element_type=F32
    )


def grid_index(shape, dim):
    return lax.broadcasted_iota(jnp.int32, shape, dim)


def identity(size):
    shape = (size, size)
    return (grid_index(shape, 0) == grid_index(shape, 1)).astype(F32).astype(BF16)


def delayed(x, before, held):
    rows = x.shape[0]
    held[pl.ds(6, 2), :] = before
    held[pl.ds(8, rows), :] = x
    return held[pl.ds(7, rows), :], held[pl.ds(6, rows), :]


def advanced(x, after, held):
    rows = x.shape[0]
    held[pl.ds(0, rows), :] = x
    held[pl.ds(rows, 2), :] = after
    return held[pl.ds(1, rows), :], held[pl.ds(2, rows), :]


def edge_kernel(query_ref, key_ref, value_ref, key_top, value_top, grad_top, last_ref, first_ref):
    for i, ref in enumerate((query_ref, key_ref, value_ref)):
        last_ref[i] = ref[...].astype(F32)[6:8].astype(BF16)
    for i, ref in enumerate((key_top, value_top, grad_top)):
        first_ref[i] = ref[...].astype(F32)[0:2].astype(BF16)


def weighted(taps, branch, x, one, two):
    base = 3 * branch
    out = taps[base : base + 1] * x
    out = out + taps[base + 1 : base + 2] * one
    return out + taps[base + 2 : base + 3] * two


def next_featured(taps, branch, x, new):
    last = x[-8:][6:8]
    one = jnp.concatenate([last[1:2], new[0:1]], axis=0)
    return weighted(taps, branch, new, one, last)


def send_kernel(query_ref, key_ref, value_ref, grad_ref, before_ref, taps_ref, filter_ref, out_ref, held):
    seq, _, _ = out_ref.shape
    all_groups = filter_ref.shape[1]
    count = all_groups // pl.num_programs(0)
    groups = count // seq
    unit = identity(LANES)
    for d in range(seq):
        cols = pl.ds(d * LANES, LANES)
        taps = taps_ref[:, 0, cols]
        feats = []
        for branch, ref in enumerate((query_ref, key_ref, value_ref)):
            x = ref[:, cols].astype(F32)
            one, two = delayed(x, before_ref[branch, :, cols].astype(F32), held.at[d % 2, branch])
            feats.append(weighted(taps, branch, x, one, two))
        product = (feats[1] * feats[2]).astype(BF16)
        scaled = (grad_ref[:, cols].astype(F32) * feats[0]).astype(BF16)
        out_ref[d, pl.ds(0, LANES), :] = dot_nt(unit, product).astype(BF16)
        out_ref[d, pl.ds(LANES, LANES), :] = dot_nt(unit, scaled).astype(BF16)
    shape = (TILE, all_groups)
    rounded = filter_ref[...].astype(BF16)
    for d in range(seq):
        row = grid_index(shape, 0)
        wanted = pl.program_id(0) * count + d * groups + row
        pick = ((row < groups) & (grid_index(shape, 1) == wanted)).astype(F32).astype(BF16)
        out_ref[d, pl.ds(2 * LANES, TILE), :] = dot_nt(pick, rounded).astype(BF16)


def toeplitz_blocks(lines):
    base = [
        pltpu.roll(jnp.broadcast_to(line, (8, LANES)), 0, 1, stride=1, stride_axis=0)
        for line in lines
    ]
    lane = grid_index((8, LANES), 1)
    sub = grid_index((8, LANES), 0)
    zero = jnp.zeros((8, LANES), F32)
    parts = [[] for _ in lines]
    for m in range(LANES // 8):
        below = zero
        for k, start in enumerate(base):
            turned = pltpu.roll(start, 8 * m, 1) if m else start
            parts[k].append(jnp.where(lane >= sub + 8 * m, turned, below))
            below = turned
    return [jnp.concatenate(part, axis=0).astype(BF16) for part in parts]


def diagonal_sums(cross, blocks):
    parts = [cross[:, k * LANES : (k + 1) * LANES] for k in range(blocks)]
    rows = LANES
    while rows > 8:
        half = rows // 2
        lane = grid_index((half, LANES), 1)
        turned = [pltpu.roll(part[half:rows], LANES - half, 1) for part in parts]
        turned.append(jnp.zeros((half, LANES), F32))
        parts = [
            parts[k][:half] + jnp.where(lane < LANES - half, turned[k], turned[k + 1])
            for k in range(blocks)
        ]
        rows = half
    lane = grid_index((8, LANES), 1)
    sub = grid_index((8, LANES), 0)
    turned = [pltpu.roll(part, LANES - 7, 1, stride=1, stride_axis=0) for part in parts]
    turned.append(jnp.zeros((8, LANES), F32))
    keep = lane < sub + (LANES - 7)
    return [
        jnp.sum(jnp.where(keep, turned[k], turned[k + 1]), axis=0, keepdims=True)
        for k in range(blocks)
    ]


def conv_kernel(groups, chunk, scale, in_ref, out_ref, corr, taps, even_taps, odd_taps, even_cross, odd_cross):
    blocks = in_ref.shape[0]
    wide = LANES // groups
    rows = blocks * wide
    start = chunk * (2 * LANES + TILE)
    lane = grid_index((LANES, LANES), 1)
    sub = grid_index((LANES, LANES), 0)
    flipped = (sub // 8) * 8 + 7 - sub % 8
    flip = (lane == flipped).astype(F32).astype(BF16)
    taps[...] = in_ref[:, pl.ds(start + 2 * LANES, TILE), :].astype(F32)
    odd_cross[...] = jnp.zeros(odd_cross.shape, F32)

    def spread(g, table):
        lines = [taps[k, pl.ds(g, 1), :] for k in range(blocks)]
        for k, block in enumerate(toeplitz_blocks(lines)):
            table[:, pl.ds(k * LANES, LANES)] = block

    def multiply(g, table, cross):
        at = pl.multiple_of(g * wide, wide)
        first = in_ref[:, pl.ds(start + at, wide), :].reshape(rows, LANES)
        second = in_ref[:, pl.ds(start + LANES + at, wide), :].reshape(rows, LANES)
        shifted, ahead = [first], [second]
        for k in range(1, blocks):
            gap = jnp.zeros((wide * k, LANES), BF16)
            shifted.append(jnp.concatenate([gap, first[: rows - wide * k]], axis=0))
            ahead.append(jnp.concatenate([second[wide * k :], gap], axis=0))
        ahead = jnp.concatenate(ahead, axis=1)
        stacked = [table[:, pl.ds(k * LANES, LANES)] for k in range(blocks)]
        conv = dot_nn(jnp.concatenate(shifted, axis=1), jnp.concatenate(stacked, axis=0))
        back = dot_nt(ahead, table[...])
        out_ref[:, pl.ds(at, wide), :] = conv.astype(BF16).reshape(blocks, wide, LANES)
        out_ref[:, pl.ds(LANES + at, wide), :] = back.astype(BF16).reshape(blocks, wide, LANES)
        cross[...] = dot_nn(dot_nt(flip, first).astype(BF16), ahead)

    def collect(g, cross):
        for k, line in enumerate(diagonal_sums(cross[...], blocks)):
            corr[k, pl.ds(g, 1), :] = line * scale

    spread(0, even_taps)

    def two_groups(step, carry):
        g = 2 * step
        spread(g + 1, odd_taps)
        multiply(g, even_taps, even_cross)
        collect(jnp.maximum(g - 1, 0), odd_cross)
        spread(jnp.minimum(g + 2, groups - 1), even_taps)
        multiply(g + 1, odd_taps, odd_cross)
        collect(g, even_cross)
        return carry

    lax.fori_loop(0, groups // 2, two_groups, 0)
    collect(groups - 1, odd_cross)
    pick_row = grid_index((TILE, 2 * LANES), 0)
    pick_lane = grid_index((TILE, 2 * LANES), 1)
    wanted = (pick_row // 2) * LANES + pick_row % 2
    pick = ((pick_row < 4) & (pick_lane == wanted)).astype(F32).astype(BF16)
    for a in range(blocks):
        if a + 1 < blocks:
            both = [out_ref[a + 1, pl.ds(0, LANES), :], out_ref[a + 1, pl.ds(LANES, LANES), :]]
            line = dot_nt(pick, jnp.concatenate(both, axis=1)).astype(BF16)
        else:
            line = jnp.zeros((TILE, LANES), BF16)
        out_ref[a, pl.ds(2 * LANES, TILE), :] = line
        full = corr[a]
        high = full.astype(BF16).astype(F32)
        pair = jnp.concatenate([high, full - high], axis=0).astype(BF16)
        out_ref[a, pl.ds(2 * LANES + TILE, 2 * groups), :] = pair


def finish_kernel(
    scale, has_old, query_ref, key_ref, value_ref, grad_ref, before_ref, after_ref, taps_ref, in_ref, *refs
):
    layer_ref, late_ref, sums_ref, corr_ref, held = refs[3:] if has_old else refs
    groups = corr_ref.shape[0] // in_ref.shape[0]
    rows = query_ref.shape[0]
    unit = identity(LANES)
    for part in range(in_ref.shape[0]):
        cols = pl.ds(part * LANES, LANES)
        taps = taps_ref[:, 0, cols]
        conv = dot_nt(unit, in_ref[part, pl.ds(0, LANES), :])
        back = dot_nt(unit, in_ref[part, pl.ds(LANES, LANES), :])
        edge = in_ref[part, pl.ds(2 * LANES, TILE), :].astype(F32)
        grad = grad_ref[:, cols].astype(F32)
        lines = []

        def raw_of(branch, ref):
            x = ref[:, cols].astype(F32)
            before = before_ref[branch, :, cols].astype(F32)
            return (x,) + delayed(x, before, held.at[part % 2, branch])

        def tap_lines(value, raw):
            for shifted in raw:
                lines.append(jnp.sum(value * shifted, axis=0, keepdims=True) * scale)

        raw = raw_of(0, query_ref)
        layer_ref[:, cols] = (weighted(taps, 0, *raw) * conv).astype(BF16)
        value = grad * conv
        tap_lines(value, raw)
        follow = after_ref[2, :, cols].astype(F32) * edge[0:2]
        total = weighted(taps, 0, value, *advanced(value, follow, held.at[part % 2, 3]))
        late_ref[pl.ds(0, rows), cols] = total.astype(BF16)
        key_raw = raw_of(1, key_ref)
        value_raw = raw_of(2, value_ref)
        tap_lines(back * weighted(taps, 2, *value_raw), key_raw)
        tap_lines(back * weighted(taps, 1, *key_raw), value_raw)
        late_ref[pl.ds(rows, rows), cols] = back.astype(BF16)
        tail = jnp.concatenate([edge[2:4], jnp.zeros((TILE - 2, LANES), F32)], axis=0)
        late_ref[pl.ds(2 * rows, TILE), cols] = tail.astype(BF16)
        for index, line in enumerate(lines):
            sums_ref[index, :, cols] = line
        pair = in_ref[part, pl.ds(2 * LANES + TILE, 2 * groups), :].astype(F32)
        corr_ref[pl.ds(part * groups, groups), :] = pair[:groups] + pair[groups:]


def apply_kernel(has_old, key_ref, value_ref, before_ref, after_ref, taps_ref, late_ref, *refs):
    out_ref, held = refs[1:] if has_old else refs
    rows, width = key_ref.shape
    for part in range(width // LANES):
        cols = pl.ds(part * LANES, LANES)
        taps = taps_ref[:, 0, cols]
        back = late_ref[pl.ds(rows, rows), cols].astype(F32)
        edge = late_ref[pl.ds(2 * rows, TILE), cols].astype(F32)[0:2]
        out_ref[0, :, cols] = late_ref[pl.ds(0, rows), cols]
        for branch, other, ref in ((1, 2, value_ref), (2, 1, key_ref)):
            x = ref[:, cols].astype(F32)
            one, two = delayed(x, before_ref[other, :, cols].astype(F32), held.at[part % 2, branch - 1])
            value = back * weighted(taps, other, x, one, two)
            new = after_ref[other - 1, :, cols].astype(F32)
            follow = edge * next_featured(taps, other, x, new)
            one, two = advanced(value, follow, held.at[part % 2, branch + 1])
            out_ref[branch, :, cols] = weighted(taps, branch, value, one, two).astype(BF16)


def summed(x, axis):
    count = lax.axis_size(axis)
    if count & (count - 1):
        return lax.psum(x, axis)
    for bit in range(count.bit_length() - 1):
        x = x + lax.ppermute(x, axis, [(i, i ^ (1 << bit)) for i in range(count)])
    return x


def layer_step(query_in, key_in, value_in, grad_out, long_filter, short_taps):
    seq = lax.axis_size("seq")
    rows, width = query_in.shape[1:]
    groups = long_filter.shape[2]
    total_rows = rows * seq
    wide = width // groups
    across = LANES * seq
    chunks = width // across
    own_groups = LANES // wide
    height = 2 * LANES + TILE
    back_height = height + 2 * own_groups
    span = math.gcd(SPAN, seq)
    steps = seq // span
    query, key, value, grad = query_in[0], key_in[0], value_in[0], grad_out[0]
    taps = short_taps[0].reshape(9, 1, width)
    low = pl.BlockSpec((8, width), lambda i: (rows // 8 - 1, 0))
    high = pl.BlockSpec((8, width), lambda i: (0, 0))
    two_rows = pl.BlockSpec((3, 2, width), lambda i: (0, 0, 0))
    last, top = pl.pallas_call(
        edge_kernel,
        grid=(1,),
        in_specs=[low, low, low, high, high, high],
        out_specs=[two_rows, two_rows],
        out_shape=[jax.ShapeDtypeStruct((3, 2, width), BF16)] * 2,
        name="edges",
    )(query, key, value, key, value, grad)
    before = passed_along(last, "seq", 1)
    after = passed_along(top, "seq", -1)

    main = pl.BlockSpec((rows, across), lambda c: (0, c))
    sent = pl.pallas_call(
        send_kernel,
        grid=(chunks,),
        in_specs=[
            main, main, main, main,
            pl.BlockSpec((3, 2, across), lambda c: (0, 0, c)),
            pl.BlockSpec((9, 1, across), lambda c: (0, 0, c)),
            pl.BlockSpec((rows, groups), lambda c: (0, 0)),
        ],
        out_specs=pl.BlockSpec((seq, height, rows), lambda c: (0, c, 0)),
        out_shape=jax.ShapeDtypeStruct((seq, chunks * height, rows), BF16),
        scratch_shapes=[pltpu.VMEM((2, 3, rows + 8, LANES), F32)],
        name="send",
    )(query, key, value, grad, before, taps, long_filter[0])
    arrived = exchange(sent)

    early = {}
    for name, array in (
        ("key", key), ("value", value), ("before", before), ("after", after), ("taps", taps),
    ):
        early[name] = passed_along(array, "pipe", -1)

    layer, passed, tap_sums, corr = None, None, None, None
    for chunk in range(chunks):
        returned = pl.pallas_call(
            functools.partial(conv_kernel, own_groups, chunk, 1.0 / math.sqrt(total_rows * wide)),
            in_specs=[pl.BlockSpec(memory_space=pltpu.VMEM)],
            out_specs=pl.BlockSpec(memory_space=pltpu.VMEM),
            out_shape=jax.ShapeDtypeStruct((seq, back_height, rows), BF16),
            scratch_shapes=[pltpu.VMEM((seq, own_groups, LANES), F32), pltpu.VMEM((seq, TILE, LANES), F32)]
            + [pltpu.VMEM((LANES, total_rows), BF16)] * 2
            + [pltpu.VMEM((LANES, total_rows), F32)] * 2,
            name="conv",
            compiler_params=pltpu.CompilerParams(vmem_limit_bytes=24 * 2**20),
        )(arrived)
        back = exchange(returned)
        at = lambda i, chunk=chunk: (0, chunk * steps + i)
        at3 = lambda i, chunk=chunk: (0, 0, chunk * steps + i)
        main = pl.BlockSpec((rows, span * LANES), at)
        edge = pl.BlockSpec((3, 2, span * LANES), at3)
        tap_spec = pl.BlockSpec((9, 1, span * LANES), at3)
        here = pl.BlockSpec((2 * rows + TILE, span * LANES), lambda i: (0, i))
        has_old = layer is not None
        old = [pl.BlockSpec(memory_space=pl.ANY)] * has_old
        layer, late, tap_sums, corr = pl.pallas_call(
            functools.partial(finish_kernel, 1.0 / math.sqrt(total_rows), has_old),
            grid=(steps,),
            in_specs=[
                main, main, main, main, edge, edge, tap_spec,
                pl.BlockSpec((span, back_height, rows), lambda i: (i, 0, 0)),
            ]
            + old * 3,
            out_specs=[
                main, here, tap_spec,
                pl.BlockSpec((span * own_groups, rows), lambda i, chunk=chunk: (chunk * steps + i, 0)),
            ],
            out_shape=[
                jax.ShapeDtypeStruct((rows, width), BF16),
                jax.ShapeDtypeStruct((2 * rows + TILE, across), BF16),
                jax.ShapeDtypeStruct((9, 1, width), F32),
                jax.ShapeDtypeStruct((groups, rows), F32),
            ],
            input_output_aliases={8: 0, 9: 2, 10: 3} if has_old else {},
            scratch_shapes=[pltpu.VMEM((2, 4, rows + 8, LANES), F32)],
            name="finish",
        )(query, key, value, grad, before, after, taps, back, *([layer, tap_sums, corr] if has_old else []))
        late = passed_along(late, "pipe", -1)
        passed = pl.pallas_call(
            functools.partial(apply_kernel, has_old),
            grid=(steps,),
            in_specs=[main, main, edge, edge, tap_spec, here] + old,
            out_specs=pl.BlockSpec((3, rows, span * LANES), at3),
            out_shape=jax.ShapeDtypeStruct((3, rows, width), BF16),
            input_output_aliases={6: 0} if has_old else {},
            scratch_shapes=[pltpu.VMEM((2, 4, rows + 8, LANES), F32)],
            name="apply",
        )(
            early["key"], early["value"], early["before"], early["after"], early["taps"], late,
            *([passed] * has_old),
        )

    filter_grad = corr.T
    tap_grads = summed(tap_sums, "seq").reshape(3, 3, width)
    return (layer[None], passed[None], filter_grad[None], tap_grads[None])


def solution(mesh):
    in_specs = (
        P("pipe", "seq", None),
        P("pipe", "seq", None),
        P("pipe", "seq", None),
        P("pipe", "seq", None),
        P("pipe", "seq", None),
        P("pipe", None, None, None),
    )
    out_specs = (
        P("pipe", "seq", None),
        P("pipe", None, "seq", None),
        P("pipe", "seq", None),
        P("pipe", None, None, None),
    )
    return jax.shard_map(layer_step, mesh=mesh, in_specs=in_specs, out_specs=out_specs, check_vma=False)
```

time: 207 us -> 203 us (0.981)
  waiting for transfers between devices: 38.1 us -> 62.8 us
  local copies, waits for them, and re-layouts: 15.7 us -> 5.36 us
  Pallas kernels: 61.1 us -> 54.3 us
  blocking collectives: 41 us -> 35.3 us
  other arithmetic: 5.11 us -> 2.03 us
    ppermute x11, waiting for transfers between devices: 22.9 us -> 43.9 us  [passed_along(): return lax.ppermute(x, axis, pairs)]
    all_to_all x4, waiting for transfers between devices: 5.38 us -> 14 us  [exchange(): return lax.all_to_all(x, 'seq', split_axis=0, concat_axis=0, tiled=True)]
    pallas_call x4 -> x5, Pallas kernels: 29.2 us -> 23 us  [the longest x4 21.3 us: layer_step(): pl.pallas_call(functools.partial(conv_kernel, own_groups, chunk, 1.0 / ma...]
    all_to_all x2 -> x1, blocking collectives: 41 us -> 35.3 us  [exchange(): return lax.all_to_all(x, 'seq', split_axis=0, concat_axis=0, tiled=True)]
    ppermute x6 -> x3, waiting for transfers between devices: 9.9 us -> 4.97 us  [summed(): x = x + lax.ppermute(x, axis, [(i, i ^ 1 << bit) for i in range(count)])]
    unnamed x34 -> x29, local copies, waits for them, and re-layouts: 9.07 us -> 5.36 us
    slice x4 -> x0, local copies, waits for them, and re-layouts: 3.52 us -> none  [the longest x3 2.66 us: layer_step(): top = jnp.stack([key[:2], value[:2], grad[:2]])]
    ppermute x6 -> x3, starting transfers between devices: 11.7 us -> 9.8 us  [summed(): x = x + lax.ppermute(x, axis, [(i, i ^ 1 << bit) for i in range(count)])]
  transfers between devices with their start and end apart: 21 -> 18, of which waited for: 11 -> 12; matrix products, arithmetic and copies ran while one was open for 7% -> 2% of each run, Pallas kernels for 23% -> 19%
where the time goes in v3:
time: 203 us; the launch traced here: 202 us
  waiting for transfers between devices  62.8 us (31%)
  Pallas kernels  54.3 us (27%)
  starting transfers between devices  41.2 us (20%)
  blocking collectives  35.3 us (17%)
  local copies, waits for them, and re-layouts  5.36 us (3%)
    ppermute x11, waiting for transfers between devices, passed_along(): return lax.ppermute(x, axis, pairs)  43.9 us
    all_to_all x1, blocking collectives, exchange(): return lax.all_to_all(x, 'seq', split_axis=0, concat_axis=0, tiled=True)  35.3 us
    pallas_call x4, Pallas kernels, layer_step(): pl.pallas_call(functools.partial(conv_kernel, own_groups, chunk, 1.0 / ma...  21.3 us
    all_to_all x4, starting transfers between devices, exchange(): return lax.all_to_all(x, 'seq', split_axis=0, concat_axis=0, tiled=True)  16.1 us
    ppermute x11, starting transfers between devices, passed_along(): return lax.ppermute(x, axis, pairs)  15.3 us
    pallas_call x4, Pallas kernels, layer_step(): pl.pallas_call(functools.partial(finish_kernel, 1.0 / math.sqrt(total_row...  14.3 us
    all_to_all x4, waiting for transfers between devices, exchange(): return lax.all_to_all(x, 'seq', split_axis=0, concat_axis=0, tiled=True)  14 us
    pallas_call x4, Pallas kernels, layer_step(): pl.pallas_call(functools.partial(apply_kernel, has_old), grid=(steps,), i...  10.6 us
  transfers between devices with their start and end apart: 18, of which 12 were waited for; matrix products, arithmetic and copies ran while one was open for 2% of the time, Pallas kernels for 19%

profile of v3, /device:TPU:0, one launch (start us, length us, event | category | flops | bytes accessed | tf_op | source)
XLA Modules:
  0.0 201.8 jit_solution(6401235209587228373)
XLA Ops:
  6.4 6.4 %send.1 = bf16[8,1088,128]{2,1,0:T(8,128)(2,1)} custom-call(bf16[128,4096]{1,0:T(8,128)(2,1)} %bitcast.30, bf16[128,4096]{1,0:T(8,128)(2,1)} %bitcast.14, bf16[128,4096]{1,0:T(8,128)(2,1)} %bitcast.22, bf16[128,4096]{1,0:T(8,128)(2,1)} %bitcast.36, bf16[3,2,4096]{2,1,0:T(2,128)(2,1)} %copy-done.5, f32[9,1,4096]{2,1,0:T(1,128)} %bitcast.42, f32[128,256]{1,0:T(8,128)} %bitcast.50), custom_call_target="tpu_custom_call" | custom-call | tf_op jit(solution)/shard_map/send/pallas_call | solution.py:325
  12.8 35.3 %all_to_all.25.in_ref = bf16[8,1088,128]{2,1,0:T(8,128)(2,1)S(1)} all-to-all(bf16[8,1088,128]{2,1,0:T(8,128)(2,1)} %send.1), channel_id=1, replica_groups=mesh['seq'=8,'pipe'=4] {'seq'}, dimensions={0} | all-to-all | bytes 4456448 | tf_op jit(solution)/shard_map/all_to_all | solution.py:26
  48.1 5.3 %conv.7 = bf16[8,288,128]{2,1,0:T(8,128)(2,1)} custom-call(bf16[8,1088,128]{2,1,0:T(8,128)(2,1)S(1)} %all_to_all.25.in_ref), custom_call_target="tpu_custom_call" | custom-call | tf_op jit(solution)/shard_map/conv/pallas_call | solution.py:349
  53.4 4.2 %all-to-all-start.4 = ((bf16[8,288,128]{2,1,0:T(8,128)(2,1)}), bf16[8,288,128]{2,1,0:T(8,128)(2,1)}, u32[]{:S(2)}, u32[]{:S(2)}) async-start(bf16[8,288,128]{2,1,0:T(8,128)(2,1)} %conv.7), calls=%async_computation.4 | async-start | bytes 1179648 | tf_op jit(solution)/shard_map/all_to_all | solution.py:26
  57.6 5.3 %conv.6 = bf16[8,288,128]{2,1,0:T(8,128)(2,1)} custom-call(bf16[8,1088,128]{2,1,0:T(8,128)(2,1)S(1)} %all_to_all.25.in_ref), custom_call_target="tpu_custom_call" | custom-call | tf_op jit(solution)/shard_map/conv/pallas_call | solution.py:349
  63.0 5.1 %all-to-all-done.4.in_ref = bf16[8,288,128]{2,1,0:T(8,128)(2,1)} async-done(((bf16[8,288,128]{2,1,0:T(8,128)(2,1)}), bf16[8,288,128]{2,1,0:T(8,128)(2,1)}, u32[]{:S(2)}, u32[]{:S(2)}) %all-to-all-start.4) | async-done | bytes 589856 | tf_op jit(solution)/shard_map/all_to_all | solution.py:26
  68.1 4.2 %all-to-all-start.3 = ((bf16[8,288,128]{2,1,0:T(8,128)(2,1)}), bf16[8,288,128]{2,1,0:T(8,128)(2,1)}, u32[]{:S(2)}, u32[]{:S(2)}) async-start(bf16[8,288,128]{2,1,0:T(8,128)(2,1)} %conv.6), calls=%async_computation.3 | async-start | bytes 1179648 | tf_op jit(solution)/shard_map/all_to_all | solution.py:26
  72.3 5.3 %conv.5 = bf16[8,288,128]{2,1,0:T(8,128)(2,1)} custom-call(bf16[8,1088,128]{2,1,0:T(8,128)(2,1)S(1)} %all_to_all.25.in_ref), custom_call_target="tpu_custom_call" | custom-call | tf_op jit(solution)/shard_map/conv/pallas_call | solution.py:349
  77.6 5.1 %all-to-all-done.3.in_ref = bf16[8,288,128]{2,1,0:T(8,128)(2,1)} async-done(((bf16[8,288,128]{2,1,0:T(8,128)(2,1)}), bf16[8,288,128]{2,1,0:T(8,128)(2,1)}, u32[]{:S(2)}, u32[]{:S(2)}) %all-to-all-start.3) | async-done | bytes 589856 | tf_op jit(solution)/shard_map/all_to_all | solution.py:26
  82.7 4.2 %all-to-all-start.2 = ((bf16[8,288,128]{2,1,0:T(8,128)(2,1)}), bf16[8,288,128]{2,1,0:T(8,128)(2,1)}, u32[]{:S(2)}, u32[]{:S(2)}) async-start(bf16[8,288,128]{2,1,0:T(8,128)(2,1)} %conv.5), calls=%async_computation.2 | async-start | bytes 1179648 | tf_op jit(solution)/shard_map/all_to_all | solution.py:26
  88.2 5.3 %conv.4 = bf16[8,288,128]{2,1,0:T(8,128)(2,1)} custom-call(bf16[8,1088,128]{2,1,0:T(8,128)(2,1)S(1)} %all_to_all.25.in_ref), custom_call_target="tpu_custom_call" | custom-call | tf_op jit(solution)/shard_map/conv/pallas_call | solution.py:349
  93.5 3.8 %all-to-all-done.2.in_ref = bf16[8,288,128]{2,1,0:T(8,128)(2,1)} async-done(((bf16[8,288,128]{2,1,0:T(8,128)(2,1)}), bf16[8,288,128]{2,1,0:T(8,128)(2,1)}, u32[]{:S(2)}, u32[]{:S(2)}) %all-to-all-start.2) | async-done | bytes 589856 | tf_op jit(solution)/shard_map/all_to_all | solution.py:26
  97.3 3.5 %all-to-all-start.1 = ((bf16[8,288,128]{2,1,0:T(8,128)(2,1)}), bf16[8,288,128]{2,1,0:T(8,128)(2,1)S(1)}, u32[]{:S(2)}, u32[]{:S(2)}) async-start(bf16[8,288,128]{2,1,0:T(8,128)(2,1)} %conv.4), calls=%async_computation.1 | async-start | bytes 1179648 | tf_op jit(solution)/shard_map/all_to_all | solution.py:26
  104.6 3.6 %finish.4 = (bf16[128,4096]{1,0:T(8,128)(2,1)}, bf16[272,1024]{1,0:T(8,128)(2,1)}, f32[9,1,4096]{2,1,0:T(1,128)}, f32[256,128]{1,0:T(8,128)}) custom-call(bf16[128,4096]{1,0:T(8,128)(2,1)} %bitcast.31, bf16[128,4096]{1,0:T(8,128)(2,1)} %bitcast.15, bf16[128,4096]{1,0:T(8,128)(2,1)} %bitcast.24, bf16[128,4096]{1,0:T(8,128)(2,1)} %bitcast.37, ...), custom_call_target="tpu_custom_call" | custom-call | tf_op jit(solution)/shard_map/finish/pallas_call | solution.py:369
  108.2 3.6 %finish.5 = (bf16[128,4096]{1,0:T(8,128)(2,1)}, bf16[272,1024]{1,0:T(8,128)(2,1)}, f32[9,1,4096]{2,1,0:T(1,128)}, f32[256,128]{1,0:T(8,128)}) custom-call(bf16[128,4096]{1,0:T(8,128)(2,1)} %bitcast.32, bf16[128,4096]{1,0:T(8,128)(2,1)} %bitcast.16, bf16[128,4096]{1,0:T(8,128)(2,1)} %bitcast.25, ...), custom_call_target="tpu_custom_call", output_to_operand_aliasing={{0}: (8, {}), {2}: (9, {}), {3}: (10, {})} | custom-call | tf_op jit(solution)/shard_map/finish/pallas_call | solution.py:369
  111.8 3.6 %finish.6 = (bf16[128,4096]{1,0:T(8,128)(2,1)}, bf16[272,1024]{1,0:T(8,128)(2,1)}, f32[9,1,4096]{2,1,0:T(1,128)}, f32[256,128]{1,0:T(8,128)}) custom-call(bf16[128,4096]{1,0:T(8,128)(2,1)} %bitcast.33, bf16[128,4096]{1,0:T(8,128)(2,1)} %bitcast.17, bf16[128,4096]{1,0:T(8,128)(2,1)} %bitcast.26, ...), custom_call_target="tpu_custom_call", output_to_operand_aliasing={{0}: (8, {}), {2}: (9, {}), {3}: (10, {})} | custom-call | tf_op jit(solution)/shard_map/finish/pallas_call | solution.py:369
  116.2 3.6 %finish.7 = (bf16[128,4096]{1,0:T(8,128)(2,1)}, bf16[272,1024]{1,0:T(8,128)(2,1)}, f32[9,1,4096]{2,1,0:T(1,128)}, f32[256,128]{1,0:T(8,128)}) custom-call(bf16[128,4096]{1,0:T(8,128)(2,1)} %bitcast.34, bf16[128,4096]{1,0:T(8,128)(2,1)} %bitcast.18, bf16[128,4096]{1,0:T(8,128)(2,1)} %bitcast.27, ...), custom_call_target="tpu_custom_call", output_to_operand_aliasing={{0}: (8, {}), {2}: (9, {}), {3}: (10, {})} | custom-call | tf_op jit(solution)/shard_map/finish/pallas_call | solution.py:369
  119.8 7.1 %collective-permute-start.11 = (f32[9,1,4096]{2,1,0:T(1,128)}, f32[9,1,4096]{2,1,0:T(1,128)S(1)}, u32[]{:S(2)}, u32[]{:S(2)}) collective-permute-start(f32[9,1,4096]{2,1,0:T(1,128)} %get-tuple-element.39), channel_id=1, source_target_pairs={{0,4},{4,0},{8,12},{12,8},{16,20},{20,16},{24,28},{28,24},{1,5},{5... | collective-permute-start | bytes 442376 | tf_op jit(solution)/shard_map/ppermute | solution.py:291
  131.6 3.7 %collective-permute-done.12 = f32[9,1,4096]{2,1,0:T(1,128)S(1)} collective-permute-done((f32[9,1,4096]{2,1,0:T(1,128)S(1)}, f32[9,1,4096]{2,1,0:T(1,128)S(1)}, u32[]{:S(2)}, u32[]{:S(2)}) %collective-permute-start.12) | collective-permute-done | bytes 147488 | tf_op jit(solution)/shard_map/ppermute | solution.py:291
  138.4 4.7 %collective-permute-done.4.before_ref = bf16[3,2,4096]{2,1,0:T(2,128)(2,1)S(1)} collective-permute-done((bf16[3,2,4096]{2,1,0:T(2,128)(2,1)S(1)}, bf16[3,2,4096]{2,1,0:T(2,128)(2,1)S(1)}, u32[]{:S(2)}, u32[]{:S(2)}) %collective-permute-start.4) | collective-permute-done | bytes 49184 | tf_op jit(solution)/shard_map/ppermute | solution.py:22
  144.3 4.7 %collective-permute-done.5.after_ref = bf16[3,2,4096]{2,1,0:T(2,128)(2,1)S(1)} collective-permute-done((bf16[3,2,4096]{2,1,0:T(2,128)(2,1)S(1)}, bf16[3,2,4096]{2,1,0:T(2,128)(2,1)S(1)}, u32[]{:S(2)}, u32[]{:S(2)}) %collective-permute-start.5) | collective-permute-done | bytes 49184 | tf_op jit(solution)/shard_map/ppermute | solution.py:22
  156.7 21.9 %collective-permute-done.10.late_ref = bf16[272,1024]{1,0:T(8,128)(2,1)} collective-permute-done((bf16[272,1024]{1,0:T(8,128)(2,1)}, bf16[272,1024]{1,0:T(8,128)(2,1)}, u32[]{:S(2)}, u32[]{:S(2)}) %collective-permute-start.10) | collective-permute-done | bytes 557088 | tf_op jit(solution)/shard_map/ppermute | solution.py:22
  184.8 5.8 %collective-permute-done.8.late_ref = bf16[272,1024]{1,0:T(8,128)(2,1)} collective-permute-done((bf16[272,1024]{1,0:T(8,128)(2,1)}, bf16[272,1024]{1,0:T(8,128)(2,1)}, u32[]{:S(2)}, u32[]{:S(2)}) %collective-permute-start.8) | collective-permute-done | bytes 557088 | tf_op jit(solution)/shard_map/ppermute | solution.py:22
  193.2 5.2 %collective-permute-done.7.late_ref = bf16[272,1024]{1,0:T(8,128)(2,1)S(1)} collective-permute-done((bf16[272,1024]{1,0:T(8,128)(2,1)}, bf16[272,1024]{1,0:T(8,128)(2,1)S(1)}, u32[]{:S(2)}, u32[]{:S(2)}) %collective-permute-start.7) | collective-permute-done | bytes 557088 | tf_op jit(solution)/shard_map/ppermute | solution.py:22
  (59 shorter events, 40.4 us)
Async XLA Ops:
  2.3 3.5 %collective-permute-start = (bf16[3,2,4096]{2,1,0:T(2,128)(2,1)}, bf16[3,2,4096]{2,1,0:T(2,128)(2,1)S(1)}, u32[]{:S(2)}, u32[]{:S(2)}) collective-permute-start(bf16[3,2,4096]{2,1,0:T(2,128)(2,1)} %get-tuple-element.22), channel_id=1, source_target_pairs={{0,4},{4,8},{8,12},{12,16},{16,20},{20,24},{24,28},{1,5},{5,9},{9,... | collective-permute-start | bytes 147464 | tf_op jit(solution)/shard_map/ppermute | solution.py:22
  53.4 14.6 %all-to-all-start.4 = ((bf16[8,288,128]{2,1,0:T(8,128)(2,1)}), bf16[8,288,128]{2,1,0:T(8,128)(2,1)}, u32[]{:S(2)}, u32[]{:S(2)}) async-start(bf16[8,288,128]{2,1,0:T(8,128)(2,1)} %conv.7), calls=%async_computation.4 | async-start | bytes 1179648 | tf_op jit(solution)/shard_map/all_to_all | solution.py:26
  63.0 23.9 %copy-start = (bf16[1,128,4096]{2,1,0:T(8,128)(2,1)S(1)}, bf16[1,128,4096]{2,1,0:T(8,128)(2,1)}, u32[]{:S(2)}) copy-start(bf16[1,128,4096]{2,1,0:T(8,128)(2,1)} %param.7) | copy-start | bytes 3145732
  68.1 14.6 %all-to-all-start.3 = ((bf16[8,288,128]{2,1,0:T(8,128)(2,1)}), bf16[8,288,128]{2,1,0:T(8,128)(2,1)}, u32[]{:S(2)}, u32[]{:S(2)}) async-start(bf16[8,288,128]{2,1,0:T(8,128)(2,1)} %conv.6), calls=%async_computation.3 | async-start | bytes 1179648 | tf_op jit(solution)/shard_map/all_to_all | solution.py:26
  77.6 23.3 %copy-start.13 = (bf16[3,2,4096]{2,1,0:T(2,128)(2,1)S(1)}, bf16[3,2,4096]{2,1,0:T(2,128)(2,1)}, u32[]{:S(2)}) copy-start(bf16[3,2,4096]{2,1,0:T(2,128)(2,1)} %get-tuple-element.23) | copy-start | bytes 147460
  82.7 14.6 %all-to-all-start.2 = ((bf16[8,288,128]{2,1,0:T(8,128)(2,1)}), bf16[8,288,128]{2,1,0:T(8,128)(2,1)}, u32[]{:S(2)}, u32[]{:S(2)}) async-start(bf16[8,288,128]{2,1,0:T(8,128)(2,1)} %conv.5), calls=%async_computation.2 | async-start | bytes 1179648 | tf_op jit(solution)/shard_map/all_to_all | solution.py:26
  86.9 64.7 %collective-permute-start.2 = (bf16[128,4096]{1,0:T(8,128)(2,1)S(1)}, bf16[128,4096]{1,0:T(8,128)(2,1)}, u32[]{:S(2)}, u32[]{:S(2)}) collective-permute-start(bf16[128,4096]{1,0:T(8,128)(2,1)S(1)} %bitcast.19), channel_id=1, source_target_pairs={{1,0},{2,1},{3,2},{5,4},{6,5},{7,6},{9,8},{10,9},{11,10},{13,12},{... | collective-permute-start | bytes 3145736 | tf_op jit(solution)/shard_map/ppermute | solution.py:22
  97.3 18.1 %all-to-all-start.1 = ((bf16[8,288,128]{2,1,0:T(8,128)(2,1)}), bf16[8,288,128]{2,1,0:T(8,128)(2,1)S(1)}, u32[]{:S(2)}, u32[]{:S(2)}) async-start(bf16[8,288,128]{2,1,0:T(8,128)(2,1)} %conv.4), calls=%async_computation.1 | async-start | bytes 1179648 | tf_op jit(solution)/shard_map/all_to_all | solution.py:26
  100.9 3.1 %collective-permute-start.1 = (bf16[3,2,4096]{2,1,0:T(2,128)(2,1)S(1)}, bf16[3,2,4096]{2,1,0:T(2,128)(2,1)S(1)}, u32[]{:S(2)}, u32[]{:S(2)}) collective-permute-start(bf16[3,2,4096]{2,1,0:T(2,128)(2,1)S(1)} %copy-done.13), channel_id=1, source_target_pairs={{4,0},{8,4},{12,8},{16,12},{20,16},{24,20},{28,24},{5,1},{9,5},{13... | collective-permute-start | bytes 147464 | tf_op jit(solution)/shard_map/ppermute | solution.py:22
  102.2 54.6 %collective-permute-start.3 = (bf16[128,4096]{1,0:T(8,128)(2,1)}, bf16[128,4096]{1,0:T(8,128)(2,1)S(1)}, u32[]{:S(2)}, u32[]{:S(2)}) collective-permute-start(bf16[128,4096]{1,0:T(8,128)(2,1)} %bitcast.23), channel_id=1, source_target_pairs={{1,0},{2,1},{3,2},{5,4},{6,5},{7,6},{9,8},{10,9},{11,10},{13,12},{... | collective-permute-start | bytes 3145736 | tf_op jit(solution)/shard_map/ppermute | solution.py:22
  116.2 26.8 %copy-start.8 = (bf16[3,2,4096]{2,1,0:T(2,128)(2,1)S(1)}, bf16[3,2,4096]{2,1,0:T(2,128)(2,1)}, u32[]{:S(2)}) copy-start(bf16[3,2,4096]{2,1,0:T(2,128)(2,1)} %copy-done.7) | copy-start | bytes 147460
  119.8 8.3 %collective-permute-start.11 = (f32[9,1,4096]{2,1,0:T(1,128)}, f32[9,1,4096]{2,1,0:T(1,128)S(1)}, u32[]{:S(2)}, u32[]{:S(2)}) collective-permute-start(f32[9,1,4096]{2,1,0:T(1,128)} %get-tuple-element.39), channel_id=1, source_target_pairs={{0,4},{4,0},{8,12},{12,8},{16,20},{20,16},{24,28},{28,24},{1,5},{5... | collective-permute-start | bytes 442376 | tf_op jit(solution)/shard_map/ppermute | solution.py:291
  129.2 6.2 %collective-permute-start.12 = (f32[9,1,4096]{2,1,0:T(1,128)S(1)}, f32[9,1,4096]{2,1,0:T(1,128)S(1)}, u32[]{:S(2)}, u32[]{:S(2)}) collective-permute-start(f32[9,1,4096]{2,1,0:T(1,128)S(1)} %add.9), channel_id=1, source_target_pairs={{0,8},{4,12},{8,0},{12,4},{16,24},{20,28},{24,16},{28,20},{1,9},{5... | collective-permute-start | bytes 442376 | tf_op jit(solution)/shard_map/ppermute | solution.py:291
  130.3 20.0 %collective-permute-start.6 = (f32[9,1,4096]{2,1,0:T(1,128)S(1)}, f32[9,1,4096]{2,1,0:T(1,128)S(1)}, u32[]{:S(2)}, u32[]{:S(2)}) collective-permute-start(f32[9,1,4096]{2,1,0:T(1,128)S(1)} %bitcast.47), channel_id=1, source_target_pairs={{1,0},{2,1},{3,2},{5,4},{6,5},{7,6},{9,8},{10,9},{11,10},{13,12},{... | collective-permute-start | bytes 442376 | tf_op jit(solution)/shard_map/ppermute | solution.py:22
  135.5 17.4 %collective-permute-start.13 = (f32[9,1,4096]{2,1,0:T(1,128)S(1)}, f32[9,1,4096]{2,1,0:T(1,128)S(1)}, u32[]{:S(2)}, u32[]{:S(2)}) collective-permute-start(f32[9,1,4096]{2,1,0:T(1,128)S(1)} %add.10), channel_id=1, source_target_pairs={{0,16},{4,20},{8,24},{12,28},{16,0},{20,4},{24,8},{28,12},{1,17},{... | collective-permute-start | bytes 442376 | tf_op jit(solution)/shard_map/ppermute | solution.py:291
  137.1 6.0 %collective-permute-start.4 = (bf16[3,2,4096]{2,1,0:T(2,128)(2,1)S(1)}, bf16[3,2,4096]{2,1,0:T(2,128)(2,1)S(1)}, u32[]{:S(2)}, u32[]{:S(2)}) collective-permute-start(bf16[3,2,4096]{2,1,0:T(2,128)(2,1)S(1)} %copy-done.6), channel_id=1, source_target_pairs={{1,0},{2,1},{3,2},{5,4},{6,5},{7,6},{9,8},{10,9},{11,10},{13,12},{... | collective-permute-start | bytes 147464 | tf_op jit(solution)/shard_map/ppermute | solution.py:22
  143.1 35.6 %copy-start.9 = (bf16[3,2,4096]{2,1,0:T(2,128)(2,1)}, bf16[3,2,4096]{2,1,0:T(2,128)(2,1)S(1)}, u32[]{:S(2)}) copy-start(bf16[3,2,4096]{2,1,0:T(2,128)(2,1)S(1)} %collective-permute-done.4.before_ref) | copy-start | bytes 147460
  143.1 6.0 %collective-permute-start.5 = (bf16[3,2,4096]{2,1,0:T(2,128)(2,1)S(1)}, bf16[3,2,4096]{2,1,0:T(2,128)(2,1)S(1)}, u32[]{:S(2)}, u32[]{:S(2)}) collective-permute-start(bf16[3,2,4096]{2,1,0:T(2,128)(2,1)S(1)} %copy-done.8), channel_id=1, source_target_pairs={{1,0},{2,1},{3,2},{5,4},{6,5},{7,6},{9,8},{10,9},{11,10},{13,12},{... | collective-permute-start | bytes 147464 | tf_op jit(solution)/shard_map/ppermute | solution.py:22
  149.0 29.6 %copy-start.10 = (bf16[3,2,4096]{2,1,0:T(2,128)(2,1)}, bf16[3,2,4096]{2,1,0:T(2,128)(2,1)S(1)}, u32[]{:S(2)}) copy-start(bf16[3,2,4096]{2,1,0:T(2,128)(2,1)S(1)} %collective-permute-done.5.after_ref) | copy-start | bytes 147460
  149.0 32.3 %collective-permute-start.9 = (bf16[272,1024]{1,0:T(8,128)(2,1)}, bf16[272,1024]{1,0:T(8,128)(2,1)S(1)}, u32[]{:S(2)}, u32[]{:S(2)}) collective-permute-start(bf16[272,1024]{1,0:T(8,128)(2,1)} %get-tuple-element.36), channel_id=1, source_target_pairs={{1,0},{2,1},{3,2},{5,4},{6,5},{7,6},{9,8},{10,9},{11,10},{13,12},{... | collective-permute-start | bytes 1671176 | tf_op jit(solution)/shard_map/ppermute | solution.py:22
  150.3 28.3 %copy-start.4 = (f32[9,1,4096]{2,1,0:T(1,128)}, f32[9,1,4096]{2,1,0:T(1,128)S(1)}, u32[]{:S(2)}) copy-start(f32[9,1,4096]{2,1,0:T(1,128)S(1)} %collective-permute-done.6.taps_ref) | copy-start | bytes 442372
  150.3 28.3 %collective-permute-start.10 = (bf16[272,1024]{1,0:T(8,128)(2,1)}, bf16[272,1024]{1,0:T(8,128)(2,1)}, u32[]{:S(2)}, u32[]{:S(2)}) collective-permute-start(bf16[272,1024]{1,0:T(8,128)(2,1)} %get-tuple-element.37), channel_id=1, source_target_pairs={{1,0},{2,1},{3,2},{5,4},{6,5},{7,6},{9,8},{10,9},{11,10},{13,12},{... | collective-permute-start | bytes 1671176 | tf_op jit(solution)/shard_map/ppermute | solution.py:22
  151.7 38.9 %collective-permute-start.8 = (bf16[272,1024]{1,0:T(8,128)(2,1)}, bf16[272,1024]{1,0:T(8,128)(2,1)}, u32[]{:S(2)}, u32[]{:S(2)}) collective-permute-start(bf16[272,1024]{1,0:T(8,128)(2,1)} %get-tuple-element.35), channel_id=1, source_target_pairs={{1,0},{2,1},{3,2},{5,4},{6,5},{7,6},{9,8},{10,9},{11,10},{13,12},{... | collective-permute-start | bytes 1671176 | tf_op jit(solution)/shard_map/ppermute | solution.py:22
  153.0 45.4 %collective-permute-start.7 = (bf16[272,1024]{1,0:T(8,128)(2,1)}, bf16[272,1024]{1,0:T(8,128)(2,1)S(1)}, u32[]{:S(2)}, u32[]{:S(2)}) collective-permute-start(bf16[272,1024]{1,0:T(8,128)(2,1)} %get-tuple-element.34), channel_id=1, source_target_pairs={{1,0},{2,1},{3,2},{5,4},{6,5},{7,6},{9,8},{10,9},{11,10},{13,12},{... | collective-permute-start | bytes 1671176 | tf_op jit(solution)/shard_map/ppermute | solution.py:22
  (8 other events, 60.6 us)

commit v4 on v3

--- a/solution.py
+++ b/solution.py
@@ -11,7 +11,8 @@
 
 F32 = jnp.float32
 BF16 = jnp.bfloat16
-SPAN = 4
+FINISH_SPAN = 4
+APPLY_SPAN = 4
 TILE = 16
 LANES = 128
 
@@ -81,31 +82,42 @@
     return weighted(taps, branch, new, one, last)
 
 
-def send_kernel(query_ref, key_ref, value_ref, grad_ref, before_ref, taps_ref, filter_ref, out_ref, held):
-    seq, _, _ = out_ref.shape
+def partner(rank, step, count, sign):
+    if count & (count - 1):
+        return lax.rem(rank + sign * step + count, jnp.int32(count))
+    return rank ^ step
+
+
+def send_kernel(
+    first_chunk, chunks, spread, rank_ref, query_ref, key_ref, value_ref, grad_ref, before_ref, taps_ref, filter_ref,
+    *refs,
+):
+    outs, held = refs[:-1], refs[-1]
+    seq = query_ref.shape[1] // LANES
     all_groups = filter_ref.shape[1]
-    count = all_groups // pl.num_programs(0)
+    count = all_groups // chunks
     groups = count // seq
     unit = identity(LANES)
-    for d in range(seq):
-        cols = pl.ds(d * LANES, LANES)
+    rounded = filter_ref[...].astype(BF16)
+    row = grid_index((TILE, all_groups), 0)
+    column = grid_index((TILE, all_groups), 1)
+    for step in range(seq):
+        d = partner(rank_ref[0], step, seq, 1) if spread else step
+        out = outs[step] if spread else outs[0].at[step]
+        cols = pl.ds(pl.multiple_of(d * LANES, LANES) if spread else d * LANES, LANES)
         taps = taps_ref[:, 0, cols]
         feats = []
         for branch, ref in enumerate((query_ref, key_ref, value_ref)):
             x = ref[:, cols].astype(F32)
-            one, two = delayed(x, before_ref[branch, :, cols].astype(F32), held.at[d % 2, branch])
+            one, two = delayed(x, before_ref[branch, :, cols].astype(F32), held.at[step % 2, branch])
             feats.append(weighted(taps, branch, x, one, two))
         product = (feats[1] * feats[2]).astype(BF16)
         scaled = (grad_ref[:, cols].astype(F32) * feats[0]).astype(BF16)
-        out_ref[d, pl.ds(0, LANES), :] = dot_nt(unit, product).astype(BF16)
-        out_ref[d, pl.ds(LANES, LANES), :] = dot_nt(unit, scaled).astype(BF16)
-    shape = (TILE, all_groups)
-    rounded = filter_ref[...].astype(BF16)
-    for d in range(seq):
-        row = grid_index(shape, 0)
-        wanted = pl.program_id(0) * count + d * groups + row
-        pick = ((row < groups) & (grid_index(shape, 1) == wanted)).astype(F32).astype(BF16)
-        out_ref[d, pl.ds(2 * LANES, TILE), :] = dot_nt(pick, rounded).astype(BF16)
+        out[pl.ds(0, LANES), :] = dot_nt(unit, product).astype(BF16)
+        out[pl.ds(LANES, LANES), :] = dot_nt(unit, scaled).astype(BF16)
+        wanted = (first_chunk + pl.program_id(0)) * count + d * groups + row
+        pick = ((row < groups) & (column == wanted)).astype(F32).astype(BF16)
+        out[pl.ds(2 * LANES, TILE), :] = dot_nt(pick, rounded).astype(BF16)
 
 
 def toeplitz_blocks(lines):
@@ -150,16 +162,24 @@
     ]
 
 
-def conv_kernel(groups, chunk, scale, in_ref, out_ref, corr, taps, even_taps, odd_taps, even_cross, odd_cross):
+def conv_kernel(groups, chunk, count, scale, *refs):
+    if chunk is None:
+        in_ref = refs[0]
+        refs = refs[1:]
+    else:
+        in_ref = refs[-1]
+        for step in range(count):
+            in_ref[partner(refs[0][0], step, count, -1)] = refs[1 + step][...]
+        refs = refs[1 + count : -1]
+    out_ref, corr, taps, even_taps, odd_taps, even_cross, odd_cross = refs
     blocks = in_ref.shape[0]
     wide = LANES // groups
     rows = blocks * wide
-    start = chunk * (2 * LANES + TILE)
     lane = grid_index((LANES, LANES), 1)
     sub = grid_index((LANES, LANES), 0)
     flipped = (sub // 8) * 8 + 7 - sub % 8
     flip = (lane == flipped).astype(F32).astype(BF16)
-    taps[...] = in_ref[:, pl.ds(start + 2 * LANES, TILE), :].astype(F32)
+    taps[...] = in_ref[:, pl.ds(2 * LANES, TILE), :].astype(F32)
     odd_cross[...] = jnp.zeros(odd_cross.shape, F32)
 
     def spread(g, table):
@@ -169,8 +189,8 @@
 
     def multiply(g, table, cross):
         at = pl.multiple_of(g * wide, wide)
-        first = in_ref[:, pl.ds(start + at, wide), :].reshape(rows, LANES)
-        second = in_ref[:, pl.ds(start + LANES + at, wide), :].reshape(rows, LANES)
+        first = in_ref[:, pl.ds(at, wide), :].reshape(rows, LANES)
+        second = in_ref[:, pl.ds(LANES + at, wide), :].reshape(rows, LANES)
         shifted, ahead = [first], [second]
         for k in range(1, blocks):
             gap = jnp.zeros((wide * k, LANES), BF16)
@@ -256,31 +276,32 @@
         tap_lines(back * weighted(taps, 2, *value_raw), key_raw)
         tap_lines(back * weighted(taps, 1, *key_raw), value_raw)
         late_ref[pl.ds(rows, rows), cols] = back.astype(BF16)
-        tail = jnp.concatenate([edge[2:4], jnp.zeros((TILE - 2, LANES), F32)], axis=0)
-        late_ref[pl.ds(2 * rows, TILE), cols] = tail.astype(BF16)
+        tail = jnp.concatenate([edge[2:4], jnp.zeros((6, LANES), F32)], axis=0)
+        late_ref[pl.ds(2 * rows, 8), cols] = tail.astype(BF16)
         for index, line in enumerate(lines):
             sums_ref[index, :, cols] = line
         pair = in_ref[part, pl.ds(2 * LANES + TILE, 2 * groups), :].astype(F32)
         corr_ref[pl.ds(part * groups, groups), :] = pair[:groups] + pair[groups:]
 
 
-def apply_kernel(has_old, key_ref, value_ref, before_ref, after_ref, taps_ref, late_ref, *refs):
+def apply_kernel(has_old, key_ref, value_ref, edges_ref, taps_ref, late_ref, *refs):
     out_ref, held = refs[1:] if has_old else refs
     rows, width = key_ref.shape
     for part in range(width // LANES):
         cols = pl.ds(part * LANES, LANES)
         taps = taps_ref[:, 0, cols]
         back = late_ref[pl.ds(rows, rows), cols].astype(F32)
-        edge = late_ref[pl.ds(2 * rows, TILE), cols].astype(F32)[0:2]
+        edge = late_ref[pl.ds(2 * rows, 8), cols].astype(F32)[0:2]
         out_ref[0, :, cols] = late_ref[pl.ds(0, rows), cols]
-        for branch, other, ref in ((1, 2, value_ref), (2, 1, key_ref)):
+        for branch, ref in ((0, value_ref), (1, key_ref)):
+            other = 1 - branch
             x = ref[:, cols].astype(F32)
-            one, two = delayed(x, before_ref[other, :, cols].astype(F32), held.at[part % 2, branch - 1])
+            one, two = delayed(x, edges_ref[other, :, cols].astype(F32), held.at[part % 2, branch])
             value = back * weighted(taps, other, x, one, two)
-            new = after_ref[other - 1, :, cols].astype(F32)
+            new = edges_ref[2 + other, :, cols].astype(F32)
             follow = edge * next_featured(taps, other, x, new)
-            one, two = advanced(value, follow, held.at[part % 2, branch + 1])
-            out_ref[branch, :, cols] = weighted(taps, branch, value, one, two).astype(BF16)
+            one, two = advanced(value, follow, held.at[part % 2, branch + 2])
+            out_ref[branch + 1, :, cols] = weighted(taps, branch, value, one, two).astype(BF16)
 
 
 def summed(x, axis):
@@ -290,6 +311,10 @@
     for bit in range(count.bit_length() - 1):
         x = x + lax.ppermute(x, axis, [(i, i ^ (1 << bit)) for i in range(count)])
     return x
+
+
+def batches(chunks):
+    return [(0, 1), (1, chunks)] if chunks > 1 else [(0, 1)]
 
 
 def layer_step(query_in, key_in, value_in, grad_out, long_filter, short_taps):
@@ -303,8 +328,10 @@
     own_groups = LANES // wide
     height = 2 * LANES + TILE
     back_height = height + 2 * own_groups
-    span = math.gcd(SPAN, seq)
+    span = math.gcd(FINISH_SPAN, seq)
     steps = seq // span
+    last_span = math.gcd(APPLY_SPAN, seq)
+    last_steps = seq // last_span
     query, key, value, grad = query_in[0], key_in[0], value_in[0], grad_out[0]
     taps = short_taps[0].reshape(9, 1, width)
     low = pl.BlockSpec((8, width), lambda i: (rows // 8 - 1, 0))
@@ -321,49 +348,72 @@
     before = passed_along(last, "seq", 1)
     after = passed_along(top, "seq", -1)
 
-    main = pl.BlockSpec((rows, across), lambda c: (0, c))
-    sent = pl.pallas_call(
-        send_kernel,
-        grid=(chunks,),
-        in_specs=[
-            main, main, main, main,
-            pl.BlockSpec((3, 2, across), lambda c: (0, 0, c)),
-            pl.BlockSpec((9, 1, across), lambda c: (0, 0, c)),
-            pl.BlockSpec((rows, groups), lambda c: (0, 0)),
-        ],
-        out_specs=pl.BlockSpec((seq, height, rows), lambda c: (0, c, 0)),
-        out_shape=jax.ShapeDtypeStruct((seq, chunks * height, rows), BF16),
-        scratch_shapes=[pltpu.VMEM((2, 3, rows + 8, LANES), F32)],
-        name="send",
-    )(query, key, value, grad, before, taps, long_filter[0])
-    arrived = exchange(sent)
+    rank = lax.axis_index("seq").astype(jnp.int32).reshape(1)
+    scalar = pl.BlockSpec(memory_space=pltpu.SMEM)
+    arrived = []
+    for part, (low, high) in enumerate(batches(chunks)):
+        main = pl.BlockSpec((rows, across), lambda c, low=low: (0, low + c))
+        if part:
+            out_specs = [pl.BlockSpec((height, rows), lambda c: (c, 0))] * seq
+            out_shape = [jax.ShapeDtypeStruct(((high - low) * height, rows), BF16)] * seq
+        else:
+            out_specs = [pl.BlockSpec((seq, height, rows), lambda c: (0, c, 0))]
+            out_shape = [jax.ShapeDtypeStruct((seq, height, rows), BF16)]
+        sent = pl.pallas_call(
+            functools.partial(send_kernel, low, chunks, part > 0),
+            grid=(high - low,),
+            in_specs=[
+                scalar, main, main, main, main,
+                pl.BlockSpec((3, 2, across), lambda c, low=low: (0, 0, low + c)),
+                pl.BlockSpec((9, 1, across), lambda c, low=low: (0, 0, low + c)),
+                pl.BlockSpec((rows, groups), lambda c: (0, 0)),
+            ],
+            out_specs=out_specs,
+            out_shape=out_shape,
+            scratch_shapes=[pltpu.VMEM((2, 3, rows + 8, LANES), F32)],
+            name="send",
+        )(rank, query, key, value, grad, before, taps, long_filter[0])
+        if not part:
+            arrived.append((None, (exchange(sent[0]),)))
+            continue
+        there = [sent[0]]
+        for step in range(1, seq):
+            pairs = [(i, i ^ step if seq & (seq - 1) == 0 else (i + step) % seq) for i in range(seq)]
+            there.append(lax.ppermute(sent[step], "seq", pairs))
+        arrived += [(chunk, (rank, *there)) for chunk in range(high - low)]
 
     early = {}
-    for name, array in (
-        ("key", key), ("value", value), ("before", before), ("after", after), ("taps", taps),
-    ):
+    edges = jnp.concatenate([before[1:], after[:2]], axis=0)
+    for name, array in (("key", key), ("value", value), ("edges", edges), ("taps", taps[3:])):
         early[name] = passed_along(array, "pipe", -1)
 
     layer, passed, tap_sums, corr = None, None, None, None
     for chunk in range(chunks):
+        place, there = arrived[chunk]
         returned = pl.pallas_call(
-            functools.partial(conv_kernel, own_groups, chunk, 1.0 / math.sqrt(total_rows * wide)),
-            in_specs=[pl.BlockSpec(memory_space=pltpu.VMEM)],
-            out_specs=pl.BlockSpec(memory_space=pltpu.VMEM),
+            functools.partial(conv_kernel, own_groups, place, seq, 1.0 / math.sqrt(total_rows * wide)),
+            grid=(1,),
+            in_specs=[pl.BlockSpec((seq, height, rows), lambda i: (0, 0, 0))]
+            if place is None
+            else [scalar] + [pl.BlockSpec((height, rows), lambda i, place=place: (place, 0))] * seq,
+            out_specs=pl.BlockSpec((seq, back_height, rows), lambda i: (0, 0, 0)),
             out_shape=jax.ShapeDtypeStruct((seq, back_height, rows), BF16),
             scratch_shapes=[pltpu.VMEM((seq, own_groups, LANES), F32), pltpu.VMEM((seq, TILE, LANES), F32)]
             + [pltpu.VMEM((LANES, total_rows), BF16)] * 2
-            + [pltpu.VMEM((LANES, total_rows), F32)] * 2,
+            + [pltpu.VMEM((LANES, total_rows), F32)] * 2
+            + [pltpu.VMEM((seq, height, LANES), BF16)] * (place is not None),
             name="conv",
             compiler_params=pltpu.CompilerParams(vmem_limit_bytes=24 * 2**20),
-        )(arrived)
+        )(*there)
         back = exchange(returned)
         at = lambda i, chunk=chunk: (0, chunk * steps + i)
         at3 = lambda i, chunk=chunk: (0, 0, chunk * steps + i)
+        last = lambda i, chunk=chunk: (0, chunk * last_steps + i)
+        last3 = lambda i, chunk=chunk: (0, 0, chunk * last_steps + i)
         main = pl.BlockSpec((rows, span * LANES), at)
         edge = pl.BlockSpec((3, 2, span * LANES), at3)
         tap_spec = pl.BlockSpec((9, 1, span * LANES), at3)
-        here = pl.BlockSpec((2 * rows + TILE, span * LANES), lambda i: (0, i))
+        here = pl.BlockSpec((2 * rows + 8, span * LANES), lambda i: (0, i))
         has_old = layer is not None
         old = [pl.BlockSpec(memory_space=pl.ANY)] * has_old
         layer, late, tap_sums, corr = pl.pallas_call(
@@ -380,7 +430,7 @@
             ],
             out_shape=[
                 jax.ShapeDtypeStruct((rows, width), BF16),
-                jax.ShapeDtypeStruct((2 * rows + TILE, across), BF16),
+                jax.ShapeDtypeStruct((2 * rows + 8, across), BF16),
                 jax.ShapeDtypeStruct((9, 1, width), F32),
                 jax.ShapeDtypeStruct((groups, rows), F32),
             ],
@@ -391,15 +441,23 @@
         late = passed_along(late, "pipe", -1)
         passed = pl.pallas_call(
             functools.partial(apply_kernel, has_old),
-            grid=(steps,),
-            in_specs=[main, main, edge, edge, tap_spec, here] + old,
-            out_specs=pl.BlockSpec((3, rows, span * LANES), at3),
+            grid=(last_steps,),
+            in_specs=[
+                pl.BlockSpec((rows, last_span * LANES), last),
+                pl.BlockSpec((rows, last_span * LANES), last),
+                pl.BlockSpec((4, 2, last_span * LANES), last3),
+                pl.BlockSpec((6, 1, last_span * LANES), last3),
+                pl.BlockSpec((2 * rows + 8, last_span * LANES), lambda i: (0, i)),
+            ]
+            + old,
+            out_specs=pl.BlockSpec((3, rows, last_span * LANES), last3),
             out_shape=jax.ShapeDtypeStruct((3, rows, width), BF16),
-            input_output_aliases={6: 0} if has_old else {},
+            input_output_aliases={5: 0} if has_old else {},
             scratch_shapes=[pltpu.VMEM((2, 4, rows + 8, LANES), F32)],
             name="apply",
+            compiler_params=pltpu.CompilerParams(vmem_limit_bytes=24 * 2**20),
         )(
-            early["key"], early["value"], early["before"], early["after"], early["taps"], late,
+            early["key"], early["value"], early["edges"], early["taps"], late,
             *([passed] * has_old),
         )
 

time: 203 us -> 209 us (1.030)
  blocking collectives: 35.3 us -> 0 us
  waiting for transfers between devices: 62.8 us -> 93 us
  starting transfers between devices: 41.2 us -> 52.2 us
    all_to_all x1 -> x0, blocking collectives: 35.3 us -> none  [exchange(): return lax.all_to_all(x, 'seq', split_axis=0, concat_axis=0, tiled=True)]
    ppermute x0 -> x7, waiting for transfers between devices: none -> 15.6 us  [layer_step(): there.append(lax.ppermute(sent[step], 'seq', pairs))]
    ppermute x11 -> x10, waiting for transfers between devices: 43.9 us -> 58.7 us  [passed_along(): return lax.ppermute(x, axis, pairs)]
    ppermute x0 -> x7, starting transfers between devices: none -> 7.25 us  [layer_step(): there.append(lax.ppermute(sent[step], 'seq', pairs))]
    all_to_all x4 -> x5, starting transfers between devices: 16.1 us -> 22.4 us  [exchange(): return lax.all_to_all(x, 'seq', split_axis=0, concat_axis=0, tiled=True)]
    ppermute x11 -> x10, starting transfers between devices: 15.3 us -> 14 us  [passed_along(): return lax.ppermute(x, axis, pairs)]
    all_to_all x4 -> x5, waiting for transfers between devices: 14 us -> 15.1 us  [exchange(): return lax.all_to_all(x, 'seq', split_axis=0, concat_axis=0, tiled=True)]
    pallas_call x9 -> x10, Pallas kernels: 38.3 us -> 37.2 us  [the longest x4 21.4 us: layer_step(): pl.pallas_call(functools.partial(conv_kernel, own_groups, place, seq, 1.0...]
  transfers between devices with their start and end apart: 18 -> 25, of which waited for: 12 -> 15; matrix products, arithmetic and copies ran while one was open for 2% -> 2% of each run, Pallas kernels for 19% -> 20%
where the time goes in v4:
time: 209 us; the launch traced here: 208 us
  waiting for transfers between devices  93 us (44%)
  Pallas kernels  53.1 us (25%)
  starting transfers between devices  52.2 us (25%)
  local copies, waits for them, and re-layouts  5.33 us (3%)
  other arithmetic  3.03 us (1%)
    ppermute x10, waiting for transfers between devices, passed_along(): return lax.ppermute(x, axis, pairs)  58.7 us
    all_to_all x5, starting transfers between devices, exchange(): return lax.all_to_all(x, 'seq', split_axis=0, concat_axis=0, tiled=True)  22.4 us
    pallas_call x4, Pallas kernels, layer_step(): pl.pallas_call(functools.partial(conv_kernel, own_groups, place, seq, 1.0...  21.4 us
    ppermute x7, waiting for transfers between devices, layer_step(): there.append(lax.ppermute(sent[step], 'seq', pairs))  15.6 us
    all_to_all x5, waiting for transfers between devices, exchange(): return lax.all_to_all(x, 'seq', split_axis=0, concat_axis=0, tiled=True)  15.1 us
    pallas_call x4, Pallas kernels, layer_step(): pl.pallas_call(functools.partial(finish_kernel, 1.0 / math.sqrt(total_row...  14.3 us
    ppermute x10, starting transfers between devices, passed_along(): return lax.ppermute(x, axis, pairs)  14 us
    ppermute x3, starting transfers between devices, summed(): x = x + lax.ppermute(x, axis, [(i, i ^ 1 << bit) for i in range(count)])  8.5 us
  transfers between devices with their start and end apart: 25, of which 15 were waited for; matrix products, arithmetic and copies ran while one was open for 2% of the time, Pallas kernels for 20%

profile of v4, /device:TPU:0, one launch (start us, length us, event | category | flops | bytes accessed | tf_op | source)
XLA Modules:
  0.0 207.5 jit_solution(10247032128951270246)
XLA Ops:
  9.1 7.3 %all-to-all-start.3 = ((bf16[8,272,128]{2,1,0:T(8,128)(2,1)}), bf16[8,272,128]{2,1,0:T(8,128)(2,1)S(1)}, u32[]{:S(2)}, u32[]{:S(2)}) async-start(bf16[8,272,128]{2,1,0:T(8,128)(2,1)} %send.3), calls=%async_computation.3 | async-start | bytes 1114112 | tf_op jit(solution)/shard_map/all_to_all | solution.py:27
  16.5 4.9 %send.2 = (bf16[816,128]{1,0:T(8,128)(2,1)}, bf16[816,128]{1,0:T(8,128)(2,1)}, bf16[816,128]{1,0:T(8,128)(2,1)}, bf16[816,128]{1,0:T(8,128)(2,1)}, bf16[816,128]...) custom-call(s32[1]{0:T(128)} %bitcast.5.rank_ref.refs_0_, ...), custom_call_target="tpu_custom_call" | custom-call | tf_op jit(solution)/shard_map/send/pallas_call | solution.py:362
  34.0 10.2 %collective-permute-done.6.refs_6_ = bf16[816,128]{1,0:T(8,128)(2,1)S(1)} collective-permute-done((bf16[816,128]{1,0:T(8,128)(2,1)}, bf16[816,128]{1,0:T(8,128)(2,1)S(1)}, u32[]{:S(2)}, u32[]{:S(2)}) %collective-permute-start.6) | collective-permute-done | bytes 208928 | tf_op jit(solution)/shard_map/ppermute | solution.py:382
  45.2 5.4 %conv.6 = bf16[8,288,128]{2,1,0:T(8,128)(2,1)} custom-call(s32[1]{0:T(128)} %bitcast.5.rank_ref.refs_0_, bf16[816,128]{1,0:T(8,128)(2,1)S(1)} %copy-done, bf16[816,128]{1,0:T(8,128)(2,1)S(1)} %collective-permute-done.2.refs_2_, bf16[816,128]{1,0:T(8,128)(2,1)S(1)} %collective-permute-done.3.refs_3_, bf16[816,128]{1,0:T(8,128)(2,1)S(1)} %collective-permute-done.4.refs_4_, ...), custom_call_target="tpu_custom_call" | custom-call | tf_op jit(solution)/shard_map/conv/pallas_call | solution.py:393
  50.6 3.8 %all-to-all-start.2 = ((bf16[8,288,128]{2,1,0:T(8,128)(2,1)}), bf16[8,288,128]{2,1,0:T(8,128)(2,1)S(1)}, u32[]{:S(2)}, u32[]{:S(2)}) async-start(bf16[8,288,128]{2,1,0:T(8,128)(2,1)} %conv.6), calls=%async_computation.2 | async-start | bytes 1179648 | tf_op jit(solution)/shard_map/all_to_all | solution.py:27
  54.4 5.4 %conv.5 = bf16[8,288,128]{2,1,0:T(8,128)(2,1)} custom-call(s32[1]{0:T(128)} %bitcast.5.rank_ref.refs_0_, bf16[816,128]{1,0:T(8,128)(2,1)S(1)} %copy-done.1, bf16[816,128]{1,0:T(8,128)(2,1)S(1)} %collective-permute-done.2.refs_2_, bf16[816,128]{1,0:T(8,128)(2,1)S(1)} %collective-permute-done.3.refs_3_, bf16[816,128]{1,0:T(8,128)(2,1)S(1)} %collective-permute-done.4.refs_4_, ...), custom_call_target="tpu_custom_call" | custom-call | tf_op jit(solution)/shard_map/conv/pallas_call | solution.py:393
  59.8 5.0 %all-to-all-done.2.in_ref = bf16[8,288,128]{2,1,0:T(8,128)(2,1)S(1)} async-done(((bf16[8,288,128]{2,1,0:T(8,128)(2,1)}), bf16[8,288,128]{2,1,0:T(8,128)(2,1)S(1)}, u32[]{:S(2)}, u32[]{:S(2)}) %all-to-all-start.2) | async-done | bytes 589856 | tf_op jit(solution)/shard_map/all_to_all | solution.py:27
  64.8 3.5 %all-to-all-start.1 = ((bf16[8,288,128]{2,1,0:T(8,128)(2,1)}), bf16[8,288,128]{2,1,0:T(8,128)(2,1)S(1)}, u32[]{:S(2)}, u32[]{:S(2)}) async-start(bf16[8,288,128]{2,1,0:T(8,128)(2,1)} %conv.5), calls=%async_computation.1 | async-start | bytes 1179648 | tf_op jit(solution)/shard_map/all_to_all | solution.py:27
  68.4 5.3 %conv.7 = bf16[8,288,128]{2,1,0:T(8,128)(2,1)} custom-call(bf16[8,272,128]{2,1,0:T(8,128)(2,1)S(1)} %all-to-all-done.3.refs_0_), custom_call_target="tpu_custom_call" | custom-call | tf_op jit(solution)/shard_map/conv/pallas_call | solution.py:393
  73.7 5.0 %all-to-all-done.1.in_ref = bf16[8,288,128]{2,1,0:T(8,128)(2,1)S(1)} async-done(((bf16[8,288,128]{2,1,0:T(8,128)(2,1)}), bf16[8,288,128]{2,1,0:T(8,128)(2,1)S(1)}, u32[]{:S(2)}, u32[]{:S(2)}) %all-to-all-start.1) | async-done | bytes 589856 | tf_op jit(solution)/shard_map/all_to_all | solution.py:27
  78.7 4.2 %all-to-all-start.4 = ((bf16[8,288,128]{2,1,0:T(8,128)(2,1)}), bf16[8,288,128]{2,1,0:T(8,128)(2,1)}, u32[]{:S(2)}, u32[]{:S(2)}) async-start(bf16[8,288,128]{2,1,0:T(8,128)(2,1)} %conv.7), calls=%async_computation.4 | async-start | bytes 1179648 | tf_op jit(solution)/shard_map/all_to_all | solution.py:27
  82.9 5.4 %conv.4 = bf16[8,288,128]{2,1,0:T(8,128)(2,1)} custom-call(s32[1]{0:T(128)} %bitcast.5.rank_ref.refs_0_, bf16[816,128]{1,0:T(8,128)(2,1)S(1)} %copy-done.1, bf16[816,128]{1,0:T(8,128)(2,1)S(1)} %collective-permute-done.2.refs_2_, bf16[816,128]{1,0:T(8,128)(2,1)S(1)} %collective-permute-done.3.refs_3_, bf16[816,128]{1,0:T(8,128)(2,1)S(1)} %collective-permute-done.4.refs_4_, ...), custom_call_target="tpu_custom_call" | custom-call | tf_op jit(solution)/shard_map/conv/pallas_call | solution.py:393
  88.3 5.1 %all-to-all-done.4.in_ref = bf16[8,288,128]{2,1,0:T(8,128)(2,1)} async-done(((bf16[8,288,128]{2,1,0:T(8,128)(2,1)}), bf16[8,288,128]{2,1,0:T(8,128)(2,1)}, u32[]{:S(2)}, u32[]{:S(2)}) %all-to-all-start.4) | async-done | bytes 589856 | tf_op jit(solution)/shard_map/all_to_all | solution.py:27
  93.3 3.5 %all-to-all-start = ((bf16[8,288,128]{2,1,0:T(8,128)(2,1)}), bf16[8,288,128]{2,1,0:T(8,128)(2,1)S(1)}, u32[]{:S(2)}, u32[]{:S(2)}) async-start(bf16[8,288,128]{2,1,0:T(8,128)(2,1)} %conv.4), calls=%async_computation | async-start | bytes 1179648 | tf_op jit(solution)/shard_map/all_to_all | solution.py:27
  101.9 3.6 %finish.4 = (bf16[128,4096]{1,0:T(8,128)(2,1)}, bf16[264,1024]{1,0:T(8,128)(2,1)}, f32[9,1,4096]{2,1,0:T(1,128)}, f32[256,128]{1,0:T(8,128)}) custom-call(bf16[128,4096]{1,0:T(8,128)(2,1)} %bitcast.17, bf16[128,4096]{1,0:T(8,128)(2,1)} %bitcast.1.key_ref.key_top, bf16[128,4096]{1,0:T(8,128)(2,1)} %bitcast.2.value_ref.value_top, bf16[128,4096]{1,0:T(8,128)(2,1)} %bitcast.24, ...), custom_call_target="tpu_custom_call" | custom-call | tf_op jit(solution)/shard_map/finish/pallas_call | solution.py:419
  105.5 3.6 %finish.5 = (bf16[128,4096]{1,0:T(8,128)(2,1)}, bf16[264,1024]{1,0:T(8,128)(2,1)}, f32[9,1,4096]{2,1,0:T(1,128)}, f32[256,128]{1,0:T(8,128)}) custom-call(bf16[128,4096]{1,0:T(8,128)(2,1)} %bitcast.18, bf16[128,4096]{1,0:T(8,128)(2,1)} %bitcast.1.key_ref.key_top, ...), custom_call_target="tpu_custom_call", output_to_operand_aliasing={{0}: (8, {}), {2}: (9, {}), {3}: (10, {})} | custom-call | tf_op jit(solution)/shard_map/finish/pallas_call | solution.py:419
  109.1 3.6 %finish.6 = (bf16[128,4096]{1,0:T(8,128)(2,1)}, bf16[264,1024]{1,0:T(8,128)(2,1)}, f32[9,1,4096]{2,1,0:T(1,128)}, f32[256,128]{1,0:T(8,128)}) custom-call(bf16[128,4096]{1,0:T(8,128)(2,1)} %bitcast.19, bf16[128,4096]{1,0:T(8,128)(2,1)} %bitcast.1.key_ref.key_top, ...), custom_call_target="tpu_custom_call", output_to_operand_aliasing={{0}: (8, {}), {2}: (9, {}), {3}: (10, {})} | custom-call | tf_op jit(solution)/shard_map/finish/pallas_call | solution.py:419
  113.5 3.6 %finish.7 = (bf16[128,4096]{1,0:T(8,128)(2,1)}, bf16[264,1024]{1,0:T(8,128)(2,1)}, f32[9,1,4096]{2,1,0:T(1,128)}, f32[256,128]{1,0:T(8,128)}) custom-call(bf16[128,4096]{1,0:T(8,128)(2,1)} %bitcast.20, bf16[128,4096]{1,0:T(8,128)(2,1)} %bitcast.1.key_ref.key_top, ...), custom_call_target="tpu_custom_call", output_to_operand_aliasing={{0}: (8, {}), {2}: (9, {}), {3}: (10, {})} | custom-call | tf_op jit(solution)/shard_map/finish/pallas_call | solution.py:419
  117.1 5.7 %collective-permute-start.17 = (f32[9,1,4096]{2,1,0:T(1,128)}, f32[9,1,4096]{2,1,0:T(1,128)S(1)}, u32[]{:S(2)}, u32[]{:S(2)}) collective-permute-start(f32[9,1,4096]{2,1,0:T(1,128)} %get-tuple-element.55), channel_id=1, source_target_pairs={{0,4},{4,0},{8,12},{12,8},{16,20},{20,16},{24,28},{28,24},{1,5},{5... | collective-permute-start | bytes 442376 | tf_op jit(solution)/shard_map/ppermute | solution.py:312
  134.4 22.0 %collective-permute-done.12.taps_ref = f32[6,1,4096]{2,1,0:T(1,128)S(1)} collective-permute-done((f32[6,1,4096]{2,1,0:T(1,128)S(1)}, f32[6,1,4096]{2,1,0:T(1,128)S(1)}, u32[]{:S(2)}, u32[]{:S(2)}) %collective-permute-start.12) | collective-permute-done | bytes 98336 | tf_op jit(solution)/shard_map/ppermute | solution.py:23
  165.7 8.0 %collective-permute-done.16.late_ref = bf16[264,1024]{1,0:T(8,128)(2,1)S(1)} collective-permute-done((bf16[264,1024]{1,0:T(8,128)(2,1)}, bf16[264,1024]{1,0:T(8,128)(2,1)S(1)}, u32[]{:S(2)}, u32[]{:S(2)}) %collective-permute-start.16) | collective-permute-done | bytes 540704 | tf_op jit(solution)/shard_map/ppermute | solution.py:23
  175.2 10.1 %collective-permute-done.15.late_ref = bf16[264,1024]{1,0:T(8,128)(2,1)} collective-permute-done((bf16[264,1024]{1,0:T(8,128)(2,1)}, bf16[264,1024]{1,0:T(8,128)(2,1)}, u32[]{:S(2)}, u32[]{:S(2)}) %collective-permute-start.15) | collective-permute-done | bytes 540704 | tf_op jit(solution)/shard_map/ppermute | solution.py:23
  187.8 9.1 %collective-permute-done.14.late_ref = bf16[264,1024]{1,0:T(8,128)(2,1)} collective-permute-done((bf16[264,1024]{1,0:T(8,128)(2,1)}, bf16[264,1024]{1,0:T(8,128)(2,1)}, u32[]{:S(2)}, u32[]{:S(2)}) %collective-permute-start.14) | collective-permute-done | bytes 540704 | tf_op jit(solution)/shard_map/ppermute | solution.py:23
  199.4 6.6 %collective-permute-done.13.late_ref = bf16[264,1024]{1,0:T(8,128)(2,1)S(1)} collective-permute-done((bf16[264,1024]{1,0:T(8,128)(2,1)}, bf16[264,1024]{1,0:T(8,128)(2,1)S(1)}, u32[]{:S(2)}, u32[]{:S(2)}) %collective-permute-start.13) | collective-permute-done | bytes 540704 | tf_op jit(solution)/shard_map/ppermute | solution.py:23
  (71 shorter events, 56.7 us)
Async XLA Ops:
  2.3 3.5 %collective-permute-start = (bf16[3,2,4096]{2,1,0:T(2,128)(2,1)}, bf16[3,2,4096]{2,1,0:T(2,128)(2,1)S(1)}, u32[]{:S(2)}, u32[]{:S(2)}) collective-permute-start(bf16[3,2,4096]{2,1,0:T(2,128)(2,1)} %get-tuple-element.30), channel_id=1, source_target_pairs={{0,4},{4,8},{8,12},{12,16},{16,20},{20,24},{24,28},{1,5},{5,9},{9,... | collective-permute-start | bytes 147464 | tf_op jit(solution)/shard_map/ppermute | solution.py:23
  9.1 41.4 %all-to-all-start.3 = ((bf16[8,272,128]{2,1,0:T(8,128)(2,1)}), bf16[8,272,128]{2,1,0:T(8,128)(2,1)S(1)}, u32[]{:S(2)}, u32[]{:S(2)}) async-start(bf16[8,272,128]{2,1,0:T(8,128)(2,1)} %send.3), calls=%async_computation.3 | async-start | bytes 1114112 | tf_op jit(solution)/shard_map/all_to_all | solution.py:27
  21.4 4.1 %collective-permute-start.2 = (bf16[816,128]{1,0:T(8,128)(2,1)}, bf16[816,128]{1,0:T(8,128)(2,1)S(1)}, u32[]{:S(2)}, u32[]{:S(2)}) collective-permute-start(bf16[816,128]{1,0:T(8,128)(2,1)} %get-tuple-element.33), channel_id=1, source_target_pairs={{0,4},{4,0},{8,12},{12,8},{16,20},{20,16},{24,28},{28,24},{1,5},{5... | collective-permute-start | bytes 626696 | tf_op jit(solution)/shard_map/ppermute | solution.py:382
  22.0 8.7 %collective-permute-start.3 = (bf16[816,128]{1,0:T(8,128)(2,1)}, bf16[816,128]{1,0:T(8,128)(2,1)S(1)}, u32[]{:S(2)}, u32[]{:S(2)}) collective-permute-start(bf16[816,128]{1,0:T(8,128)(2,1)} %get-tuple-element.34), channel_id=1, source_target_pairs={{0,8},{4,12},{8,0},{12,4},{16,24},{20,28},{24,16},{28,20},{1,9},{5... | collective-permute-start | bytes 626696 | tf_op jit(solution)/shard_map/ppermute | solution.py:382
  23.6 10.4 %collective-permute-start.4 = (bf16[816,128]{1,0:T(8,128)(2,1)}, bf16[816,128]{1,0:T(8,128)(2,1)S(1)}, u32[]{:S(2)}, u32[]{:S(2)}) collective-permute-start(bf16[816,128]{1,0:T(8,128)(2,1)} %get-tuple-element.35), channel_id=1, source_target_pairs={{0,12},{4,8},{8,4},{12,0},{16,28},{20,24},{24,20},{28,16},{1,13},{... | collective-permute-start | bytes 626696 | tf_op jit(solution)/shard_map/ppermute | solution.py:382
  23.6 10.4 %collective-permute-start.5 = (bf16[816,128]{1,0:T(8,128)(2,1)}, bf16[816,128]{1,0:T(8,128)(2,1)S(1)}, u32[]{:S(2)}, u32[]{:S(2)}) collective-permute-start(bf16[816,128]{1,0:T(8,128)(2,1)} %get-tuple-element.36), channel_id=1, source_target_pairs={{0,16},{4,20},{8,24},{12,28},{16,0},{20,4},{24,8},{28,12},{1,17},{... | collective-permute-start | bytes 626696 | tf_op jit(solution)/shard_map/ppermute | solution.py:382
  25.6 18.7 %collective-permute-start.6 = (bf16[816,128]{1,0:T(8,128)(2,1)}, bf16[816,128]{1,0:T(8,128)(2,1)S(1)}, u32[]{:S(2)}, u32[]{:S(2)}) collective-permute-start(bf16[816,128]{1,0:T(8,128)(2,1)} %get-tuple-element.37), channel_id=1, source_target_pairs={{0,20},{4,16},{8,28},{12,24},{16,4},{20,0},{24,12},{28,8},{1,21},{... | collective-permute-start | bytes 626696 | tf_op jit(solution)/shard_map/ppermute | solution.py:382
  25.6 18.7 %collective-permute-start.7 = (bf16[816,128]{1,0:T(8,128)(2,1)}, bf16[816,128]{1,0:T(8,128)(2,1)S(1)}, u32[]{:S(2)}, u32[]{:S(2)}) collective-permute-start(bf16[816,128]{1,0:T(8,128)(2,1)} %get-tuple-element.38), channel_id=1, source_target_pairs={{0,24},{4,28},{8,16},{12,20},{16,8},{20,12},{24,0},{28,4},{1,25},{... | collective-permute-start | bytes 626696 | tf_op jit(solution)/shard_map/ppermute | solution.py:382
  30.7 13.6 %collective-permute-start.8 = (bf16[816,128]{1,0:T(8,128)(2,1)}, bf16[816,128]{1,0:T(8,128)(2,1)S(1)}, u32[]{:S(2)}, u32[]{:S(2)}) collective-permute-start(bf16[816,128]{1,0:T(8,128)(2,1)} %get-tuple-element.39), channel_id=1, source_target_pairs={{0,28},{4,24},{8,20},{12,16},{16,12},{20,8},{24,4},{28,0},{1,29},{... | collective-permute-start | bytes 626696 | tf_op jit(solution)/shard_map/ppermute | solution.py:382
  50.6 14.2 %all-to-all-start.2 = ((bf16[8,288,128]{2,1,0:T(8,128)(2,1)}), bf16[8,288,128]{2,1,0:T(8,128)(2,1)S(1)}, u32[]{:S(2)}, u32[]{:S(2)}) async-start(bf16[8,288,128]{2,1,0:T(8,128)(2,1)} %conv.6), calls=%async_computation.2 | async-start | bytes 1179648 | tf_op jit(solution)/shard_map/all_to_all | solution.py:27
  64.8 13.9 %all-to-all-start.1 = ((bf16[8,288,128]{2,1,0:T(8,128)(2,1)}), bf16[8,288,128]{2,1,0:T(8,128)(2,1)S(1)}, u32[]{:S(2)}, u32[]{:S(2)}) async-start(bf16[8,288,128]{2,1,0:T(8,128)(2,1)} %conv.5), calls=%async_computation.1 | async-start | bytes 1179648 | tf_op jit(solution)/shard_map/all_to_all | solution.py:27
  78.7 14.6 %all-to-all-start.4 = ((bf16[8,288,128]{2,1,0:T(8,128)(2,1)}), bf16[8,288,128]{2,1,0:T(8,128)(2,1)}, u32[]{:S(2)}, u32[]{:S(2)}) async-start(bf16[8,288,128]{2,1,0:T(8,128)(2,1)} %conv.7), calls=%async_computation.4 | async-start | bytes 1179648 | tf_op jit(solution)/shard_map/all_to_all | solution.py:27
  93.3 19.4 %all-to-all-start = ((bf16[8,288,128]{2,1,0:T(8,128)(2,1)}), bf16[8,288,128]{2,1,0:T(8,128)(2,1)S(1)}, u32[]{:S(2)}, u32[]{:S(2)}) async-start(bf16[8,288,128]{2,1,0:T(8,128)(2,1)} %conv.4), calls=%async_computation | async-start | bytes 1179648 | tf_op jit(solution)/shard_map/all_to_all | solution.py:27
  96.9 62.1 %collective-permute-start.9 = (bf16[128,4096]{1,0:T(8,128)(2,1)}, bf16[128,4096]{1,0:T(8,128)(2,1)S(1)}, u32[]{:S(2)}, u32[]{:S(2)}) collective-permute-start(bf16[128,4096]{1,0:T(8,128)(2,1)} %bitcast.1.key_ref.key_top), channel_id=1, source_target_pairs={{1,0},{2,1},{3,2},{5,4},{6,5},{7,6},{9,8},{10,9},{11,10},{13,12},{... | collective-permute-start | bytes 3145736 | tf_op jit(solution)/shard_map/ppermute | solution.py:23
  117.1 6.9 %collective-permute-start.17 = (f32[9,1,4096]{2,1,0:T(1,128)}, f32[9,1,4096]{2,1,0:T(1,128)S(1)}, u32[]{:S(2)}, u32[]{:S(2)}) collective-permute-start(f32[9,1,4096]{2,1,0:T(1,128)} %get-tuple-element.55), channel_id=1, source_target_pairs={{0,4},{4,0},{8,12},{12,8},{16,20},{20,16},{24,28},{28,24},{1,5},{5... | collective-permute-start | bytes 442376 | tf_op jit(solution)/shard_map/ppermute | solution.py:312
  125.1 6.2 %collective-permute-start.18 = (f32[9,1,4096]{2,1,0:T(1,128)S(1)}, f32[9,1,4096]{2,1,0:T(1,128)S(1)}, u32[]{:S(2)}, u32[]{:S(2)}) collective-permute-start(f32[9,1,4096]{2,1,0:T(1,128)S(1)} %add.9), channel_id=1, source_target_pairs={{0,8},{4,12},{8,0},{12,4},{16,24},{20,28},{24,16},{28,20},{1,9},{5... | collective-permute-start | bytes 442376 | tf_op jit(solution)/shard_map/ppermute | solution.py:312
  126.3 39.3 %collective-permute-start.10 = (bf16[128,4096]{1,0:T(8,128)(2,1)}, bf16[128,4096]{1,0:T(8,128)(2,1)S(1)}, u32[]{:S(2)}, u32[]{:S(2)}) collective-permute-start(bf16[128,4096]{1,0:T(8,128)(2,1)} %bitcast.2.value_ref.value_top), channel_id=1, source_target_pairs={{1,0},{2,1},{3,2},{5,4},{6,5},{7,6},{9,8},{10,9},{11,10},{13,12},{... | collective-permute-start | bytes 3145736 | tf_op jit(solution)/shard_map/ppermute | solution.py:23
  127.7 28.7 %collective-permute-start.12 = (f32[6,1,4096]{2,1,0:T(1,128)S(1)}, f32[6,1,4096]{2,1,0:T(1,128)S(1)}, u32[]{:S(2)}, u32[]{:S(2)}) collective-permute-start(f32[6,1,4096]{2,1,0:T(1,128)S(1)} %bitcast.40), channel_id=1, source_target_pairs={{1,0},{2,1},{3,2},{5,4},{6,5},{7,6},{9,8},{10,9},{11,10},{13,12},{... | collective-permute-start | bytes 294920 | tf_op jit(solution)/shard_map/ppermute | solution.py:23
  131.4 28.9 %collective-permute-start.19 = (f32[9,1,4096]{2,1,0:T(1,128)S(1)}, f32[9,1,4096]{2,1,0:T(1,128)S(1)}, u32[]{:S(2)}, u32[]{:S(2)}) collective-permute-start(f32[9,1,4096]{2,1,0:T(1,128)S(1)} %add.10), channel_id=1, source_target_pairs={{0,16},{4,20},{8,24},{12,28},{16,0},{20,4},{24,8},{28,12},{1,17},{... | collective-permute-start | bytes 442376 | tf_op jit(solution)/shard_map/ppermute | solution.py:312
  133.1 24.6 %collective-permute-start.11 = (bf16[4,2,4096]{2,1,0:T(2,128)(2,1)S(1)}, bf16[4,2,4096]{2,1,0:T(2,128)(2,1)S(1)}, u32[]{:S(2)}, u32[]{:S(2)}) collective-permute-start(bf16[4,2,4096]{2,1,0:T(2,128)(2,1)S(1)} %pad_maximum_fusion), channel_id=1, source_target_pairs={{1,0},{2,1},{3,2},{5,4},{6,5},{7,6},{9,8},{10,9},{11,10},{13,12},{... | collective-permute-start | bytes 196616 | tf_op jit(solution)/shard_map/ppermute | solution.py:23
  156.4 17.2 %collective-permute-start.16 = (bf16[264,1024]{1,0:T(8,128)(2,1)}, bf16[264,1024]{1,0:T(8,128)(2,1)S(1)}, u32[]{:S(2)}, u32[]{:S(2)}) collective-permute-start(bf16[264,1024]{1,0:T(8,128)(2,1)} %get-tuple-element.53), channel_id=1, source_target_pairs={{1,0},{2,1},{3,2},{5,4},{6,5},{7,6},{9,8},{10,9},{11,10},{13,12},{... | collective-permute-start | bytes 1622024 | tf_op jit(solution)/shard_map/ppermute | solution.py:23
  157.7 27.6 %collective-permute-start.15 = (bf16[264,1024]{1,0:T(8,128)(2,1)}, bf16[264,1024]{1,0:T(8,128)(2,1)}, u32[]{:S(2)}, u32[]{:S(2)}) collective-permute-start(bf16[264,1024]{1,0:T(8,128)(2,1)} %get-tuple-element.52), channel_id=1, source_target_pairs={{1,0},{2,1},{3,2},{5,4},{6,5},{7,6},{9,8},{10,9},{11,10},{13,12},{... | collective-permute-start | bytes 1622024 | tf_op jit(solution)/shard_map/ppermute | solution.py:23
  159.0 37.9 %collective-permute-start.14 = (bf16[264,1024]{1,0:T(8,128)(2,1)}, bf16[264,1024]{1,0:T(8,128)(2,1)}, u32[]{:S(2)}, u32[]{:S(2)}) collective-permute-start(bf16[264,1024]{1,0:T(8,128)(2,1)} %get-tuple-element.51), channel_id=1, source_target_pairs={{1,0},{2,1},{3,2},{5,4},{6,5},{7,6},{9,8},{10,9},{11,10},{13,12},{... | collective-permute-start | bytes 1622024 | tf_op jit(solution)/shard_map/ppermute | solution.py:23
  161.0 45.0 %collective-permute-start.13 = (bf16[264,1024]{1,0:T(8,128)(2,1)}, bf16[264,1024]{1,0:T(8,128)(2,1)S(1)}, u32[]{:S(2)}, u32[]{:S(2)}) collective-permute-start(bf16[264,1024]{1,0:T(8,128)(2,1)} %get-tuple-element.50), channel_id=1, source_target_pairs={{1,0},{2,1},{3,2},{5,4},{6,5},{7,6},{9,8},{10,9},{11,10},{13,12},{... | collective-permute-start | bytes 1622024 | tf_op jit(solution)/shard_map/ppermute | solution.py:23
  (13 other events, 154.2 us)

commit v5 on v4

--- a/solution.py
+++ b/solution.py
@@ -332,7 +332,9 @@
     steps = seq // span
     last_span = math.gcd(APPLY_SPAN, seq)
     last_steps = seq // last_span
-    query, key, value, grad = query_in[0], key_in[0], value_in[0], grad_out[0]
+    query, key, value, grad = (
+        pltpu.with_memory_space_constraint(x[0], pltpu.HBM) for x in (query_in, key_in, value_in, grad_out)
+    )
     taps = short_taps[0].reshape(9, 1, width)
     low = pl.BlockSpec((8, width), lambda i: (rows // 8 - 1, 0))
     high = pl.BlockSpec((8, width), lambda i: (0, 0))
@@ -344,6 +346,7 @@
         out_specs=[two_rows, two_rows],
         out_shape=[jax.ShapeDtypeStruct((3, 2, width), BF16)] * 2,
         name="edges",
+        compiler_params=pltpu.CompilerParams(vmem_limit_bytes=32 * 2**20),
     )(query, key, value, key, value, grad)
     before = passed_along(last, "seq", 1)
     after = passed_along(top, "seq", -1)
@@ -372,6 +375,7 @@
             out_shape=out_shape,
             scratch_shapes=[pltpu.VMEM((2, 3, rows + 8, LANES), F32)],
             name="send",
+            compiler_params=pltpu.CompilerParams(vmem_limit_bytes=32 * 2**20),
         )(rank, query, key, value, grad, before, taps, long_filter[0])
         if not part:
             arrived.append((None, (exchange(sent[0]),)))
@@ -437,6 +441,7 @@
             input_output_aliases={8: 0, 9: 2, 10: 3} if has_old else {},
             scratch_shapes=[pltpu.VMEM((2, 4, rows + 8, LANES), F32)],
             name="finish",
+            compiler_params=pltpu.CompilerParams(vmem_limit_bytes=32 * 2**20),
         )(query, key, value, grad, before, after, taps, back, *([layer, tap_sums, corr] if has_old else []))
         late = passed_along(late, "pipe", -1)
         passed = pl.pallas_call(

time: 209 us -> 202 us (0.967)
    all_to_all x5, waiting for transfers between devices: 15.1 us -> 11.3 us  [exchange(): return lax.all_to_all(x, 'seq', split_axis=0, concat_axis=0, tiled=True)]
    unnamed x21 -> x27, local copies, waits for them, and re-layouts: 5.32 us -> 4.51 us
  transfers between devices with their start and end apart: 25 -> 25, of which waited for: 15 -> 16; matrix products, arithmetic and copies ran while one was open for 2% -> 1% of each run, Pallas kernels for 20% -> 21%
where the time goes in v5:
time: 202 us; the launch traced here: 201 us
  waiting for transfers between devices  91.1 us (45%)
  Pallas kernels  52.4 us (26%)
  starting transfers between devices  50.7 us (25%)
  local copies, waits for them, and re-layouts  4.57 us (2%)
    ppermute x10, waiting for transfers between devices, passed_along(): return lax.ppermute(x, axis, pairs)  59.8 us
    all_to_all x5, starting transfers between devices, exchange(): return lax.all_to_all(x, 'seq', split_axis=0, concat_axis=0, tiled=True)  21.5 us
    pallas_call x4, Pallas kernels, layer_step(): pl.pallas_call(functools.partial(conv_kernel, own_groups, place, seq, 1.0...  21.4 us
    ppermute x7, waiting for transfers between devices, layer_step(): there.append(lax.ppermute(sent[step], 'seq', pairs))  16.7 us
    ppermute x10, starting transfers between devices, passed_along(): return lax.ppermute(x, axis, pairs)  14 us
    pallas_call x4, Pallas kernels, layer_step(): pl.pallas_call(functools.partial(finish_kernel, 1.0 / math.sqrt(total_row...  13.4 us
    all_to_all x5, waiting for transfers between devices, exchange(): return lax.all_to_all(x, 'seq', split_axis=0, concat_axis=0, tiled=True)  11.3 us
    pallas_call x4, Pallas kernels, layer_step(): pl.pallas_call(functools.partial(apply_kernel, has_old), grid=(last_steps...  9.78 us
  transfers between devices with their start and end apart: 25, of which 16 were waited for; matrix products, arithmetic and copies ran while one was open for 1% of the time, Pallas kernels for 21%

profile of v5, /device:TPU:0, one launch (start us, length us, event | category | flops | bytes accessed | tf_op | source)
XLA Modules:
  0.0 200.8 jit_solution(9394495217802653713)
XLA Ops:
  7.7 7.3 %all-to-all-start.3 = ((bf16[8,272,128]{2,1,0:T(8,128)(2,1)}), bf16[8,272,128]{2,1,0:T(8,128)(2,1)S(1)}, u32[]{:S(2)}, u32[]{:S(2)}) async-start(bf16[8,272,128]{2,1,0:T(8,128)(2,1)} %send.3), calls=%async_computation.3 | async-start | bytes 1114112 | tf_op jit(solution)/shard_map/all_to_all | solution.py:27
  15.1 4.0 %send.2 = (bf16[816,128]{1,0:T(8,128)(2,1)S(1)}, bf16[816,128]{1,0:T(8,128)(2,1)S(1)}, bf16[816,128]{1,0:T(8,128)(2,1)S(1)}, bf16[816,128]{1,0:T(8,128)(2,1)S(1)...) custom-call(s32[1]{0:T(128)} %bitcast.5.rank_ref.refs_0_, ...), custom_call_target="tpu_custom_call" | custom-call | tf_op jit(solution)/shard_map/send/pallas_call | solution.py:365
  25.7 3.6 %collective-permute-done.3.refs_3_ = bf16[816,128]{1,0:T(8,128)(2,1)S(1)} collective-permute-done((bf16[816,128]{1,0:T(8,128)(2,1)S(1)}, bf16[816,128]{1,0:T(8,128)(2,1)S(1)}, u32[]{:S(2)}, u32[]{:S(2)}) %collective-permute-start.3) | collective-permute-done | bytes 208928 | tf_op jit(solution)/shard_map/ppermute | solution.py:386
  29.4 3.2 %collective-permute-done.4.refs_4_ = bf16[816,128]{1,0:T(8,128)(2,1)S(1)} collective-permute-done((bf16[816,128]{1,0:T(8,128)(2,1)S(1)}, bf16[816,128]{1,0:T(8,128)(2,1)S(1)}, u32[]{:S(2)}, u32[]{:S(2)}) %collective-permute-start.4) | collective-permute-done | bytes 208928 | tf_op jit(solution)/shard_map/ppermute | solution.py:386
  32.6 9.1 %collective-permute-done.6.refs_6_ = bf16[816,128]{1,0:T(8,128)(2,1)S(1)} collective-permute-done((bf16[816,128]{1,0:T(8,128)(2,1)S(1)}, bf16[816,128]{1,0:T(8,128)(2,1)S(1)}, u32[]{:S(2)}, u32[]{:S(2)}) %collective-permute-start.6) | collective-permute-done | bytes 208928 | tf_op jit(solution)/shard_map/ppermute | solution.py:386
  42.5 5.4 %conv.6 = bf16[8,288,128]{2,1,0:T(8,128)(2,1)} custom-call(s32[1]{0:T(128)} %bitcast.5.rank_ref.refs_0_, bf16[816,128]{1,0:T(8,128)(2,1)S(1)} %get-tuple-element.32.refs_1_, bf16[816,128]{1,0:T(8,128)(2,1)S(1)} %collective-permute-done.2.refs_2_, bf16[816,128]{1,0:T(8,128)(2,1)S(1)} %collective-permute-done.3.refs_3_, ...), custom_call_target="tpu_custom_call" | custom-call | tf_op jit(solution)/shard_map/conv/pallas_call | solution.py:397
  47.8 3.5 %all-to-all-start.2 = ((bf16[8,288,128]{2,1,0:T(8,128)(2,1)}), bf16[8,288,128]{2,1,0:T(8,128)(2,1)S(1)}, u32[]{:S(2)}, u32[]{:S(2)}) async-start(bf16[8,288,128]{2,1,0:T(8,128)(2,1)} %conv.6), calls=%async_computation.2 | async-start | bytes 1179648 | tf_op jit(solution)/shard_map/all_to_all | solution.py:27
  51.4 5.4 %conv.5 = bf16[8,288,128]{2,1,0:T(8,128)(2,1)} custom-call(s32[1]{0:T(128)} %bitcast.5.rank_ref.refs_0_, bf16[816,128]{1,0:T(8,128)(2,1)S(1)} %get-tuple-element.32.refs_1_, bf16[816,128]{1,0:T(8,128)(2,1)S(1)} %collective-permute-done.2.refs_2_, bf16[816,128]{1,0:T(8,128)(2,1)S(1)} %collective-permute-done.3.refs_3_, ...), custom_call_target="tpu_custom_call" | custom-call | tf_op jit(solution)/shard_map/conv/pallas_call | solution.py:397
  56.7 5.0 %all-to-all-done.2.in_ref = bf16[8,288,128]{2,1,0:T(8,128)(2,1)S(1)} async-done(((bf16[8,288,128]{2,1,0:T(8,128)(2,1)}), bf16[8,288,128]{2,1,0:T(8,128)(2,1)S(1)}, u32[]{:S(2)}, u32[]{:S(2)}) %all-to-all-start.2) | async-done | bytes 589856 | tf_op jit(solution)/shard_map/all_to_all | solution.py:27
  61.7 3.6 %all-to-all-start.1 = ((bf16[8,288,128]{2,1,0:T(8,128)(2,1)}), bf16[8,288,128]{2,1,0:T(8,128)(2,1)S(1)}, u32[]{:S(2)}, u32[]{:S(2)}) async-start(bf16[8,288,128]{2,1,0:T(8,128)(2,1)} %conv.5), calls=%async_computation.1 | async-start | bytes 1179648 | tf_op jit(solution)/shard_map/all_to_all | solution.py:27
  65.3 5.3 %conv.7 = bf16[8,288,128]{2,1,0:T(8,128)(2,1)} custom-call(bf16[8,272,128]{2,1,0:T(8,128)(2,1)S(1)} %all-to-all-done.3.refs_0_), custom_call_target="tpu_custom_call" | custom-call | tf_op jit(solution)/shard_map/conv/pallas_call | solution.py:397
  70.6 5.0 %all-to-all-done.1.in_ref = bf16[8,288,128]{2,1,0:T(8,128)(2,1)S(1)} async-done(((bf16[8,288,128]{2,1,0:T(8,128)(2,1)}), bf16[8,288,128]{2,1,0:T(8,128)(2,1)S(1)}, u32[]{:S(2)}, u32[]{:S(2)}) %all-to-all-start.1) | async-done | bytes 589856 | tf_op jit(solution)/shard_map/all_to_all | solution.py:27
  75.7 3.5 %all-to-all-start.4 = ((bf16[8,288,128]{2,1,0:T(8,128)(2,1)}), bf16[8,288,128]{2,1,0:T(8,128)(2,1)S(1)}, u32[]{:S(2)}, u32[]{:S(2)}) async-start(bf16[8,288,128]{2,1,0:T(8,128)(2,1)} %conv.7), calls=%async_computation.4 | async-start | bytes 1179648 | tf_op jit(solution)/shard_map/all_to_all | solution.py:27
  82.9 5.4 %conv.4 = bf16[8,288,128]{2,1,0:T(8,128)(2,1)} custom-call(s32[1]{0:T(128)} %bitcast.5.rank_ref.refs_0_, bf16[816,128]{1,0:T(8,128)(2,1)S(1)} %get-tuple-element.32.refs_1_, bf16[816,128]{1,0:T(8,128)(2,1)S(1)} %collective-permute-done.2.refs_2_, bf16[816,128]{1,0:T(8,128)(2,1)S(1)} %collective-permute-done.3.refs_3_, ...), custom_call_target="tpu_custom_call" | custom-call | tf_op jit(solution)/shard_map/conv/pallas_call | solution.py:397
  89.5 3.5 %all-to-all-start = ((bf16[8,288,128]{2,1,0:T(8,128)(2,1)}), bf16[8,288,128]{2,1,0:T(8,128)(2,1)S(1)}, u32[]{:S(2)}, u32[]{:S(2)}) async-start(bf16[8,288,128]{2,1,0:T(8,128)(2,1)} %conv.4), calls=%async_computation | async-start | bytes 1179648 | tf_op jit(solution)/shard_map/all_to_all | solution.py:27
  100.8 3.4 %finish.5 = (bf16[128,4096]{1,0:T(8,128)(2,1)}, bf16[264,1024]{1,0:T(8,128)(2,1)}, f32[9,1,4096]{2,1,0:T(1,128)S(1)}, f32[256,128]{1,0:T(8,128)S(1)}) custom-call(bf16[128,4096]{1,0:T(8,128)(2,1)} %bitcast.36, bf16[128,4096]{1,0:T(8,128)(2,1)} %bitcast.29, ...), custom_call_target="tpu_custom_call", output_to_operand_aliasing={{0}: (8, {}), {2}: (9, {}), {3}: (10, {})} | custom-call | tf_op jit(solution)/shard_map/finish/pallas_call | solution.py:423
  104.1 3.2 %finish.6 = (bf16[128,4096]{1,0:T(8,128)(2,1)}, bf16[264,1024]{1,0:T(8,128)(2,1)S(1)}, f32[9,1,4096]{2,1,0:T(1,128)S(1)}, f32[256,128]{1,0:T(8,128)S(1)}) custom-call(bf16[128,4096]{1,0:T(8,128)(2,1)} %bitcast.37, bf16[128,4096]{1,0:T(8,128)(2,1)} %bitcast.30, ...), custom_call_target="tpu_custom_call", output_to_operand_aliasing={{0}: (8, {}), {2}: (9, {}), {3}: (10, {})} | custom-call | tf_op jit(solution)/shard_map/finish/pallas_call | solution.py:423
  107.4 3.6 %finish.7 = (bf16[128,4096]{1,0:T(8,128)(2,1)}, bf16[264,1024]{1,0:T(8,128)(2,1)}, f32[9,1,4096]{2,1,0:T(1,128)S(1)}, f32[256,128]{1,0:T(8,128)S(1)}) custom-call(bf16[128,4096]{1,0:T(8,128)(2,1)} %bitcast.38, bf16[128,4096]{1,0:T(8,128)(2,1)} %bitcast.31, ...), custom_call_target="tpu_custom_call", output_to_operand_aliasing={{0}: (8, {}), {2}: (9, {}), {3}: (10, {})} | custom-call | tf_op jit(solution)/shard_map/finish/pallas_call | solution.py:423
  110.9 5.8 %collective-permute-start.17 = (f32[9,1,4096]{2,1,0:T(1,128)S(1)}, f32[9,1,4096]{2,1,0:T(1,128)S(1)}, u32[]{:S(2)}, u32[]{:S(2)}) collective-permute-start(f32[9,1,4096]{2,1,0:T(1,128)S(1)} %get-tuple-element.55), channel_id=1, source_target_pairs={{0,4},{4,0},{8,12},{12,8},{16,20},{20,16},{24,28},{28,24},{1,5},{5... | collective-permute-start | bytes 442376 | tf_op jit(solution)/shard_map/ppermute | solution.py:312
  127.1 21.9 %collective-permute-done.12.taps_ref = f32[6,1,4096]{2,1,0:T(1,128)S(1)} collective-permute-done((f32[6,1,4096]{2,1,0:T(1,128)S(1)}, f32[6,1,4096]{2,1,0:T(1,128)S(1)}, u32[]{:S(2)}, u32[]{:S(2)}) %collective-permute-start.12) | collective-permute-done | bytes 98336 | tf_op jit(solution)/shard_map/ppermute | solution.py:23
  155.8 10.2 %collective-permute-done.16.late_ref = bf16[264,1024]{1,0:T(8,128)(2,1)S(1)} collective-permute-done((bf16[264,1024]{1,0:T(8,128)(2,1)S(1)}, bf16[264,1024]{1,0:T(8,128)(2,1)S(1)}, u32[]{:S(2)}, u32[]{:S(2)}) %collective-permute-start.16) | collective-permute-done | bytes 540704 | tf_op jit(solution)/shard_map/ppermute | solution.py:23
  168.5 9.1 %collective-permute-done.15.late_ref = bf16[264,1024]{1,0:T(8,128)(2,1)S(1)} collective-permute-done((bf16[264,1024]{1,0:T(8,128)(2,1)}, bf16[264,1024]{1,0:T(8,128)(2,1)S(1)}, u32[]{:S(2)}, u32[]{:S(2)}) %collective-permute-start.15) | collective-permute-done | bytes 540704 | tf_op jit(solution)/shard_map/ppermute | solution.py:23
  180.1 9.1 %collective-permute-done.14.late_ref = bf16[264,1024]{1,0:T(8,128)(2,1)S(1)} collective-permute-done((bf16[264,1024]{1,0:T(8,128)(2,1)}, bf16[264,1024]{1,0:T(8,128)(2,1)S(1)}, u32[]{:S(2)}, u32[]{:S(2)}) %collective-permute-start.14) | collective-permute-done | bytes 540704 | tf_op jit(solution)/shard_map/ppermute | solution.py:23
  191.7 6.7 %collective-permute-done.13.late_ref = bf16[264,1024]{1,0:T(8,128)(2,1)S(1)} collective-permute-done((bf16[264,1024]{1,0:T(8,128)(2,1)}, bf16[264,1024]{1,0:T(8,128)(2,1)S(1)}, u32[]{:S(2)}, u32[]{:S(2)}) %collective-permute-start.13) | collective-permute-done | bytes 540704 | tf_op jit(solution)/shard_map/ppermute | solution.py:23
  (75 shorter events, 54.1 us)
Async XLA Ops:
  1.7 3.3 %collective-permute-start = (bf16[3,2,4096]{2,1,0:T(2,128)(2,1)S(1)}, bf16[3,2,4096]{2,1,0:T(2,128)(2,1)S(1)}, u32[]{:S(2)}, u32[]{:S(2)}) collective-permute-start(bf16[3,2,4096]{2,1,0:T(2,128)(2,1)S(1)} %get-tuple-element.30), channel_id=1, source_target_pairs={{0,4},{4,8},{8,12},{12,16},{16,20},{20,24},{24,28},{1,5},{5,9},{9,... | collective-permute-start | bytes 147464 | tf_op jit(solution)/shard_map/ppermute | solution.py:23
  7.7 40.1 %all-to-all-start.3 = ((bf16[8,272,128]{2,1,0:T(8,128)(2,1)}), bf16[8,272,128]{2,1,0:T(8,128)(2,1)S(1)}, u32[]{:S(2)}, u32[]{:S(2)}) async-start(bf16[8,272,128]{2,1,0:T(8,128)(2,1)} %send.3), calls=%async_computation.3 | async-start | bytes 1114112 | tf_op jit(solution)/shard_map/all_to_all | solution.py:27
  19.1 4.1 %collective-permute-start.2 = (bf16[816,128]{1,0:T(8,128)(2,1)S(1)}, bf16[816,128]{1,0:T(8,128)(2,1)S(1)}, u32[]{:S(2)}, u32[]{:S(2)}) collective-permute-start(bf16[816,128]{1,0:T(8,128)(2,1)S(1)} %get-tuple-element.33), channel_id=1, source_target_pairs={{0,4},{4,0},{8,12},{12,8},{16,20},{20,16},{24,28},{28,24},{1,5},{5... | collective-permute-start | bytes 626696 | tf_op jit(solution)/shard_map/ppermute | solution.py:386
  19.7 9.6 %collective-permute-start.3 = (bf16[816,128]{1,0:T(8,128)(2,1)S(1)}, bf16[816,128]{1,0:T(8,128)(2,1)S(1)}, u32[]{:S(2)}, u32[]{:S(2)}) collective-permute-start(bf16[816,128]{1,0:T(8,128)(2,1)S(1)} %get-tuple-element.34), channel_id=1, source_target_pairs={{0,8},{4,12},{8,0},{12,4},{16,24},{20,28},{24,16},{28,20},{1,9},{5... | collective-permute-start | bytes 626696 | tf_op jit(solution)/shard_map/ppermute | solution.py:386
  21.3 11.3 %collective-permute-start.4 = (bf16[816,128]{1,0:T(8,128)(2,1)S(1)}, bf16[816,128]{1,0:T(8,128)(2,1)S(1)}, u32[]{:S(2)}, u32[]{:S(2)}) collective-permute-start(bf16[816,128]{1,0:T(8,128)(2,1)S(1)} %get-tuple-element.35), channel_id=1, source_target_pairs={{0,12},{4,8},{8,4},{12,0},{16,28},{20,24},{24,20},{28,16},{1,13},{... | collective-permute-start | bytes 626696 | tf_op jit(solution)/shard_map/ppermute | solution.py:386
  21.3 11.3 %collective-permute-start.5 = (bf16[816,128]{1,0:T(8,128)(2,1)S(1)}, bf16[816,128]{1,0:T(8,128)(2,1)S(1)}, u32[]{:S(2)}, u32[]{:S(2)}) collective-permute-start(bf16[816,128]{1,0:T(8,128)(2,1)S(1)} %get-tuple-element.36), channel_id=1, source_target_pairs={{0,16},{4,20},{8,24},{12,28},{16,0},{20,4},{24,8},{28,12},{1,17},{... | collective-permute-start | bytes 626696 | tf_op jit(solution)/shard_map/ppermute | solution.py:386
  23.2 18.4 %collective-permute-start.6 = (bf16[816,128]{1,0:T(8,128)(2,1)S(1)}, bf16[816,128]{1,0:T(8,128)(2,1)S(1)}, u32[]{:S(2)}, u32[]{:S(2)}) collective-permute-start(bf16[816,128]{1,0:T(8,128)(2,1)S(1)} %get-tuple-element.37), channel_id=1, source_target_pairs={{0,20},{4,16},{8,28},{12,24},{16,4},{20,0},{24,12},{28,8},{1,21},{... | collective-permute-start | bytes 626696 | tf_op jit(solution)/shard_map/ppermute | solution.py:386
  23.2 18.4 %collective-permute-start.7 = (bf16[816,128]{1,0:T(8,128)(2,1)S(1)}, bf16[816,128]{1,0:T(8,128)(2,1)S(1)}, u32[]{:S(2)}, u32[]{:S(2)}) collective-permute-start(bf16[816,128]{1,0:T(8,128)(2,1)S(1)} %get-tuple-element.38), channel_id=1, source_target_pairs={{0,24},{4,28},{8,16},{12,20},{16,8},{20,12},{24,0},{28,4},{1,25},{... | collective-permute-start | bytes 626696 | tf_op jit(solution)/shard_map/ppermute | solution.py:386
  29.3 13.2 %collective-permute-start.8 = (bf16[816,128]{1,0:T(8,128)(2,1)S(1)}, bf16[816,128]{1,0:T(8,128)(2,1)S(1)}, u32[]{:S(2)}, u32[]{:S(2)}) collective-permute-start(bf16[816,128]{1,0:T(8,128)(2,1)S(1)} %get-tuple-element.39), channel_id=1, source_target_pairs={{0,28},{4,24},{8,20},{12,16},{16,12},{20,8},{24,4},{28,0},{1,29},{... | collective-permute-start | bytes 626696 | tf_op jit(solution)/shard_map/ppermute | solution.py:386
  47.8 13.9 %all-to-all-start.2 = ((bf16[8,288,128]{2,1,0:T(8,128)(2,1)}), bf16[8,288,128]{2,1,0:T(8,128)(2,1)S(1)}, u32[]{:S(2)}, u32[]{:S(2)}) async-start(bf16[8,288,128]{2,1,0:T(8,128)(2,1)} %conv.6), calls=%async_computation.2 | async-start | bytes 1179648 | tf_op jit(solution)/shard_map/all_to_all | solution.py:27
  61.7 13.9 %all-to-all-start.1 = ((bf16[8,288,128]{2,1,0:T(8,128)(2,1)}), bf16[8,288,128]{2,1,0:T(8,128)(2,1)S(1)}, u32[]{:S(2)}, u32[]{:S(2)}) async-start(bf16[8,288,128]{2,1,0:T(8,128)(2,1)} %conv.5), calls=%async_computation.1 | async-start | bytes 1179648 | tf_op jit(solution)/shard_map/all_to_all | solution.py:27
  75.7 13.9 %all-to-all-start.4 = ((bf16[8,288,128]{2,1,0:T(8,128)(2,1)}), bf16[8,288,128]{2,1,0:T(8,128)(2,1)S(1)}, u32[]{:S(2)}, u32[]{:S(2)}) async-start(bf16[8,288,128]{2,1,0:T(8,128)(2,1)} %conv.7), calls=%async_computation.4 | async-start | bytes 1179648 | tf_op jit(solution)/shard_map/all_to_all | solution.py:27
  89.5 17.8 %all-to-all-start = ((bf16[8,288,128]{2,1,0:T(8,128)(2,1)}), bf16[8,288,128]{2,1,0:T(8,128)(2,1)S(1)}, u32[]{:S(2)}, u32[]{:S(2)}) async-start(bf16[8,288,128]{2,1,0:T(8,128)(2,1)} %conv.4), calls=%async_computation | async-start | bytes 1179648 | tf_op jit(solution)/shard_map/all_to_all | solution.py:27
  93.1 58.5 %collective-permute-start.9 = (bf16[128,4096]{1,0:T(8,128)(2,1)}, bf16[128,4096]{1,0:T(8,128)(2,1)}, u32[]{:S(2)}, u32[]{:S(2)}) collective-permute-start(bf16[128,4096]{1,0:T(8,128)(2,1)} %bitcast.27), channel_id=1, source_target_pairs={{1,0},{2,1},{3,2},{5,4},{6,5},{7,6},{9,8},{10,9},{11,10},{13,12},{... | collective-permute-start | bytes 3145736 | tf_op jit(solution)/shard_map/ppermute | solution.py:23
  110.9 6.8 %collective-permute-start.17 = (f32[9,1,4096]{2,1,0:T(1,128)S(1)}, f32[9,1,4096]{2,1,0:T(1,128)S(1)}, u32[]{:S(2)}, u32[]{:S(2)}) collective-permute-start(f32[9,1,4096]{2,1,0:T(1,128)S(1)} %get-tuple-element.55), channel_id=1, source_target_pairs={{0,4},{4,0},{8,12},{12,8},{16,20},{20,16},{24,28},{28,24},{1,5},{5... | collective-permute-start | bytes 442376 | tf_op jit(solution)/shard_map/ppermute | solution.py:312
  117.8 6.2 %collective-permute-start.18 = (f32[9,1,4096]{2,1,0:T(1,128)S(1)}, f32[9,1,4096]{2,1,0:T(1,128)S(1)}, u32[]{:S(2)}, u32[]{:S(2)}) collective-permute-start(f32[9,1,4096]{2,1,0:T(1,128)S(1)} %add.9), channel_id=1, source_target_pairs={{0,8},{4,12},{8,0},{12,4},{16,24},{20,28},{24,16},{28,20},{1,9},{5... | collective-permute-start | bytes 442376 | tf_op jit(solution)/shard_map/ppermute | solution.py:312
  119.0 36.8 %collective-permute-start.10 = (bf16[128,4096]{1,0:T(8,128)(2,1)}, bf16[128,4096]{1,0:T(8,128)(2,1)}, u32[]{:S(2)}, u32[]{:S(2)}) collective-permute-start(bf16[128,4096]{1,0:T(8,128)(2,1)} %bitcast.2.value_ref.value_top), channel_id=1, source_target_pairs={{1,0},{2,1},{3,2},{5,4},{6,5},{7,6},{9,8},{10,9},{11,10},{13,12},{... | collective-permute-start | bytes 3145736 | tf_op jit(solution)/shard_map/ppermute | solution.py:23
  120.3 28.7 %collective-permute-start.12 = (f32[6,1,4096]{2,1,0:T(1,128)S(1)}, f32[6,1,4096]{2,1,0:T(1,128)S(1)}, u32[]{:S(2)}, u32[]{:S(2)}) collective-permute-start(f32[6,1,4096]{2,1,0:T(1,128)S(1)} %bitcast.49), channel_id=1, source_target_pairs={{1,0},{2,1},{3,2},{5,4},{6,5},{7,6},{9,8},{10,9},{11,10},{13,12},{... | collective-permute-start | bytes 294920 | tf_op jit(solution)/shard_map/ppermute | solution.py:23
  124.2 28.8 %collective-permute-start.19 = (f32[9,1,4096]{2,1,0:T(1,128)S(1)}, f32[9,1,4096]{2,1,0:T(1,128)S(1)}, u32[]{:S(2)}, u32[]{:S(2)}) collective-permute-start(f32[9,1,4096]{2,1,0:T(1,128)S(1)} %add.10), channel_id=1, source_target_pairs={{0,16},{4,20},{8,24},{12,28},{16,0},{20,4},{24,8},{28,12},{1,17},{... | collective-permute-start | bytes 442376 | tf_op jit(solution)/shard_map/ppermute | solution.py:312
  125.8 24.5 %collective-permute-start.11 = (bf16[4,2,4096]{2,1,0:T(2,128)(2,1)S(1)}, bf16[4,2,4096]{2,1,0:T(2,128)(2,1)S(1)}, u32[]{:S(2)}, u32[]{:S(2)}) collective-permute-start(bf16[4,2,4096]{2,1,0:T(2,128)(2,1)S(1)} %pad_maximum_fusion), channel_id=1, source_target_pairs={{1,0},{2,1},{3,2},{5,4},{6,5},{7,6},{9,8},{10,9},{11,10},{13,12},{... | collective-permute-start | bytes 196616 | tf_op jit(solution)/shard_map/ppermute | solution.py:23
  149.0 17.0 %collective-permute-start.16 = (bf16[264,1024]{1,0:T(8,128)(2,1)S(1)}, bf16[264,1024]{1,0:T(8,128)(2,1)S(1)}, u32[]{:S(2)}, u32[]{:S(2)}) collective-permute-start(bf16[264,1024]{1,0:T(8,128)(2,1)S(1)} %get-tuple-element.53), channel_id=1, source_target_pairs={{1,0},{2,1},{3,2},{5,4},{6,5},{7,6},{9,8},{10,9},{11,10},{13,12},{... | collective-permute-start | bytes 1622024 | tf_op jit(solution)/shard_map/ppermute | solution.py:23
  150.3 27.3 %collective-permute-start.15 = (bf16[264,1024]{1,0:T(8,128)(2,1)}, bf16[264,1024]{1,0:T(8,128)(2,1)S(1)}, u32[]{:S(2)}, u32[]{:S(2)}) collective-permute-start(bf16[264,1024]{1,0:T(8,128)(2,1)} %get-tuple-element.52), channel_id=1, source_target_pairs={{1,0},{2,1},{3,2},{5,4},{6,5},{7,6},{9,8},{10,9},{11,10},{13,12},{... | collective-permute-start | bytes 1622024 | tf_op jit(solution)/shard_map/ppermute | solution.py:23
  151.7 37.6 %collective-permute-start.14 = (bf16[264,1024]{1,0:T(8,128)(2,1)}, bf16[264,1024]{1,0:T(8,128)(2,1)S(1)}, u32[]{:S(2)}, u32[]{:S(2)}) collective-permute-start(bf16[264,1024]{1,0:T(8,128)(2,1)} %copy-done.10), channel_id=1, source_target_pairs={{1,0},{2,1},{3,2},{5,4},{6,5},{7,6},{9,8},{10,9},{11,10},{13,12},{... | collective-permute-start | bytes 1622024 | tf_op jit(solution)/shard_map/ppermute | solution.py:23
  153.0 45.4 %collective-permute-start.13 = (bf16[264,1024]{1,0:T(8,128)(2,1)}, bf16[264,1024]{1,0:T(8,128)(2,1)S(1)}, u32[]{:S(2)}, u32[]{:S(2)}) collective-permute-start(bf16[264,1024]{1,0:T(8,128)(2,1)} %get-tuple-element.50), channel_id=1, source_target_pairs={{1,0},{2,1},{3,2},{5,4},{6,5},{7,6},{9,8},{10,9},{11,10},{13,12},{... | collective-permute-start | bytes 1622024 | tf_op jit(solution)/shard_map/ppermute | solution.py:23
  (14 other events, 142.7 us)

commit v6 on v5

--- a/solution.py
+++ b/solution.py
@@ -162,14 +162,15 @@
     ]
 
 
-def conv_kernel(groups, chunk, count, scale, *refs):
-    if chunk is None:
-        in_ref = refs[0]
+def conv_kernel(groups, spread_out, chunk, count, height, scale, *refs):
+    if not spread_out:
+        in_ref = refs[0].at[:, pl.ds(chunk * height, height), :]
         refs = refs[1:]
     else:
         in_ref = refs[-1]
         for step in range(count):
-            in_ref[partner(refs[0][0], step, count, -1)] = refs[1 + step][...]
+            block = refs[1 + step][pl.ds(chunk * height, height), :]
+            in_ref[partner(refs[0][0], step, count, -1)] = block
         refs = refs[1 + count : -1]
     out_ref, corr, taps, even_taps, odd_taps, even_cross, odd_cross = refs
     blocks = in_ref.shape[0]
@@ -314,7 +315,8 @@
 
 
 def batches(chunks):
-    return [(0, 1), (1, chunks)] if chunks > 1 else [(0, 1)]
+    first = (chunks + 1) // 2
+    return [(0, first), (first, chunks)] if chunks > 1 else [(0, 1)]
 
 
 def layer_step(query_in, key_in, value_in, grad_out, long_filter, short_taps):
@@ -353,6 +355,7 @@
 
     rank = lax.axis_index("seq").astype(jnp.int32).reshape(1)
     scalar = pl.BlockSpec(memory_space=pltpu.SMEM)
+    whole = pl.BlockSpec(memory_space=pltpu.VMEM)
     arrived = []
     for part, (low, high) in enumerate(batches(chunks)):
         main = pl.BlockSpec((rows, across), lambda c, low=low: (0, low + c))
@@ -361,7 +364,7 @@
             out_shape = [jax.ShapeDtypeStruct(((high - low) * height, rows), BF16)] * seq
         else:
             out_specs = [pl.BlockSpec((seq, height, rows), lambda c: (0, c, 0))]
-            out_shape = [jax.ShapeDtypeStruct((seq, height, rows), BF16)]
+            out_shape = [jax.ShapeDtypeStruct((seq, (high - low) * height, rows), BF16)]
         sent = pl.pallas_call(
             functools.partial(send_kernel, low, chunks, part > 0),
             grid=(high - low,),
@@ -378,13 +381,14 @@
             compiler_params=pltpu.CompilerParams(vmem_limit_bytes=32 * 2**20),
         )(rank, query, key, value, grad, before, taps, long_filter[0])
         if not part:
-            arrived.append((None, (exchange(sent[0]),)))
+            there = (exchange(sent[0]),)
+            arrived += [(False, chunk, there) for chunk in range(high - low)]
             continue
         there = [sent[0]]
         for step in range(1, seq):
             pairs = [(i, i ^ step if seq & (seq - 1) == 0 else (i + step) % seq) for i in range(seq)]
             there.append(lax.ppermute(sent[step], "seq", pairs))
-        arrived += [(chunk, (rank, *there)) for chunk in range(high - low)]
+        arrived += [(True, chunk, (rank, *there)) for chunk in range(high - low)]
 
     early = {}
     edges = jnp.concatenate([before[1:], after[:2]], axis=0)
@@ -393,19 +397,16 @@
 
     layer, passed, tap_sums, corr = None, None, None, None
     for chunk in range(chunks):
-        place, there = arrived[chunk]
+        split, place, there = arrived[chunk]
         returned = pl.pallas_call(
-            functools.partial(conv_kernel, own_groups, place, seq, 1.0 / math.sqrt(total_rows * wide)),
-            grid=(1,),
-            in_specs=[pl.BlockSpec((seq, height, rows), lambda i: (0, 0, 0))]
-            if place is None
-            else [scalar] + [pl.BlockSpec((height, rows), lambda i, place=place: (place, 0))] * seq,
-            out_specs=pl.BlockSpec((seq, back_height, rows), lambda i: (0, 0, 0)),
+            functools.partial(conv_kernel, own_groups, split, place, seq, height, 1.0 / math.sqrt(total_rows * wide)),
+            in_specs=[scalar] + [whole] * seq if split else [whole],
+            out_specs=whole,
             out_shape=jax.ShapeDtypeStruct((seq, back_height, rows), BF16),
             scratch_shapes=[pltpu.VMEM((seq, own_groups, LANES), F32), pltpu.VMEM((seq, TILE, LANES), F32)]
             + [pltpu.VMEM((LANES, total_rows), BF16)] * 2
             + [pltpu.VMEM((LANES, total_rows), F32)] * 2
-            + [pltpu.VMEM((seq, height, LANES), BF16)] * (place is not None),
+            + [pltpu.VMEM((seq, height, LANES), BF16)] * split,
             name="conv",
             compiler_params=pltpu.CompilerParams(vmem_limit_bytes=24 * 2**20),
         )(*there)

time: 202 us -> 207 us (1.025)
  local copies, waits for them, and re-layouts: 4.57 us -> 10.3 us
  Pallas kernels: 52.4 us -> 50.3 us
    unnamed x27 -> x31, local copies, waits for them, and re-layouts: 4.51 us -> 10.2 us
  transfers between devices with their start and end apart: 25 -> 25, of which waited for: 16 -> 15; matrix products, arithmetic and copies ran while one was open for 1% -> 1% of each run, Pallas kernels for 21% -> 20%
where the time goes in v6:
time: 207 us; the launch traced here: 205 us
  waiting for transfers between devices  92 us (44%)
  starting transfers between devices  50.8 us (25%)
  Pallas kernels  50.3 us (24%)
  local copies, waits for them, and re-layouts  10.3 us (5%)
    ppermute x10, waiting for transfers between devices, passed_along(): return lax.ppermute(x, axis, pairs)  60 us
    all_to_all x5, starting transfers between devices, exchange(): return lax.all_to_all(x, 'seq', split_axis=0, concat_axis=0, tiled=True)  21.6 us
    pallas_call x4, Pallas kernels, layer_step(): pl.pallas_call(functools.partial(conv_kernel, own_groups, split, place, s...  19.7 us
    ppermute x7, waiting for transfers between devices, layer_step(): there.append(lax.ppermute(sent[step], 'seq', pairs))  18 us
    ppermute x10, starting transfers between devices, passed_along(): return lax.ppermute(x, axis, pairs)  14 us
    pallas_call x4, Pallas kernels, layer_step(): pl.pallas_call(functools.partial(finish_kernel, 1.0 / math.sqrt(total_row...  13.5 us
    all_to_all x5, waiting for transfers between devices, exchange(): return lax.all_to_all(x, 'seq', split_axis=0, concat_axis=0, tiled=True)  10.5 us
    unnamed x31, local copies, waits for them, and re-layouts  10.2 us
  transfers between devices with their start and end apart: 25, of which 15 were waited for; matrix products, arithmetic and copies ran while one was open for 1% of the time, Pallas kernels for 20%

profile of v6, /device:TPU:0, one launch (start us, length us, event | category | flops | bytes accessed | tf_op | source)
XLA Modules:
  0.0 205.5 jit_solution(12264777607792343745)
XLA Ops:
  5.0 3.5 %send.3 = bf16[8,544,128]{2,1,0:T(8,128)(2,1)} custom-call(s32[1]{0:T(128)} %bitcast.5.rank_ref.refs_0_, bf16[128,4096]{1,0:T(8,128)(2,1)} %bitcast.33, bf16[128,4096]{1,0:T(8,128)(2,1)} %bitcast.25, bf16[128,4096]{1,0:T(8,128)(2,1)} %bitcast.2.value_ref.value_top, bf16[128,4096]{1,0:T(8,128)(2,1)} %bitcast.40, ...), custom_call_target="tpu_custom_call" | custom-call | tf_op jit(solution)/shard_map/send/pallas_call | solution.py:368
  8.5 7.3 %all-to-all-start.2 = ((bf16[8,544,128]{2,1,0:T(8,128)(2,1)}), bf16[8,544,128]{2,1,0:T(8,128)(2,1)S(1)}, u32[]{:S(2)}, u32[]{:S(2)}) async-start(bf16[8,544,128]{2,1,0:T(8,128)(2,1)} %send.3), calls=%async_computation.2 | async-start | bytes 2228224 | tf_op jit(solution)/shard_map/all_to_all | solution.py:27
  15.8 2.9 %send.2 = (bf16[544,128]{1,0:T(8,128)(2,1)S(1)}, bf16[544,128]{1,0:T(8,128)(2,1)S(1)}, bf16[544,128]{1,0:T(8,128)(2,1)S(1)}, bf16[544,128]{1,0:T(8,128)(2,1)S(1)...) custom-call(s32[1]{0:T(128)} %bitcast.5.rank_ref.refs_0_, ...), custom_call_target="tpu_custom_call" | custom-call | tf_op jit(solution)/shard_map/send/pallas_call | solution.py:368
  25.3 9.3 %collective-permute-done.3.refs_3_ = bf16[544,128]{1,0:T(8,128)(2,1)S(1)} collective-permute-done((bf16[544,128]{1,0:T(8,128)(2,1)S(1)}, bf16[544,128]{1,0:T(8,128)(2,1)S(1)}, u32[]{:S(2)}, u32[]{:S(2)}) %collective-permute-start.3) | collective-permute-done | bytes 139296 | tf_op jit(solution)/shard_map/ppermute | solution.py:390
  36.4 5.0 %collective-permute-done.7.refs_7_ = bf16[544,128]{1,0:T(8,128)(2,1)S(1)} collective-permute-done((bf16[544,128]{1,0:T(8,128)(2,1)S(1)}, bf16[544,128]{1,0:T(8,128)(2,1)S(1)}, u32[]{:S(2)}, u32[]{:S(2)}) %collective-permute-start.7) | collective-permute-done | bytes 139296 | tf_op jit(solution)/shard_map/ppermute | solution.py:390
  43.3 5.4 %conv.5 = bf16[8,288,128]{2,1,0:T(8,128)(2,1)} custom-call(s32[1]{0:T(128)} %bitcast.5.rank_ref.refs_0_, bf16[544,128]{1,0:T(8,128)(2,1)S(1)} %get-tuple-element.32.refs_1_, bf16[544,128]{1,0:T(8,128)(2,1)S(1)} %collective-permute-done.2.refs_2_, bf16[544,128]{1,0:T(8,128)(2,1)S(1)} %collective-permute-done.3.refs_3_, ...), custom_call_target="tpu_custom_call" | custom-call | tf_op jit(solution)/shard_map/conv/pallas_call | solution.py:401
  51.9 3.5 %all-to-all-start.1 = ((bf16[8,288,128]{2,1,0:T(8,128)(2,1)}), bf16[8,288,128]{2,1,0:T(8,128)(2,1)S(1)}, u32[]{:S(2)}, u32[]{:S(2)}) async-start(bf16[8,288,128]{2,1,0:T(8,128)(2,1)} %conv.5), calls=%async_computation.1 | async-start | bytes 1179648 | tf_op jit(solution)/shard_map/all_to_all | solution.py:27
  55.5 5.3 %conv.6 = bf16[8,288,128]{2,1,0:T(8,128)(2,1)} custom-call(bf16[8,544,128]{2,1,0:T(8,128)(2,1)S(1)} %all-to-all-done.2.refs_0_), custom_call_target="tpu_custom_call" | custom-call | tf_op jit(solution)/shard_map/conv/pallas_call | solution.py:401
  60.8 5.0 %all-to-all-done.1.in_ref = bf16[8,288,128]{2,1,0:T(8,128)(2,1)S(1)} async-done(((bf16[8,288,128]{2,1,0:T(8,128)(2,1)}), bf16[8,288,128]{2,1,0:T(8,128)(2,1)S(1)}, u32[]{:S(2)}, u32[]{:S(2)}) %all-to-all-start.1) | async-done | bytes 589856 | tf_op jit(solution)/shard_map/all_to_all | solution.py:27
  65.8 3.5 %all-to-all-start.3 = ((bf16[8,288,128]{2,1,0:T(8,128)(2,1)}), bf16[8,288,128]{2,1,0:T(8,128)(2,1)S(1)}, u32[]{:S(2)}, u32[]{:S(2)}) async-start(bf16[8,288,128]{2,1,0:T(8,128)(2,1)} %conv.6), calls=%async_computation.3 | async-start | bytes 1179648 | tf_op jit(solution)/shard_map/all_to_all | solution.py:27
  69.4 4.5 %conv.7 = bf16[8,288,128]{2,1,0:T(8,128)(2,1)S(1)} custom-call(bf16[8,544,128]{2,1,0:T(8,128)(2,1)S(1)} %all-to-all-done.2.refs_0_), custom_call_target="tpu_custom_call" | custom-call | tf_op jit(solution)/shard_map/conv/pallas_call | solution.py:401
  74.7 5.0 %all-to-all-done.3.in_ref = bf16[8,288,128]{2,1,0:T(8,128)(2,1)S(1)} async-done(((bf16[8,288,128]{2,1,0:T(8,128)(2,1)}), bf16[8,288,128]{2,1,0:T(8,128)(2,1)S(1)}, u32[]{:S(2)}, u32[]{:S(2)}) %all-to-all-start.3) | async-done | bytes 589856 | tf_op jit(solution)/shard_map/all_to_all | solution.py:27
  79.7 3.5 %all-to-all-start.4 = ((bf16[8,288,128]{2,1,0:T(8,128)(2,1)}), bf16[8,288,128]{2,1,0:T(8,128)(2,1)S(1)}, u32[]{:S(2)}, u32[]{:S(2)}) async-start(bf16[8,288,128]{2,1,0:T(8,128)(2,1)} %copy-done.2), calls=%async_computation.4 | async-start | bytes 1179648 | tf_op jit(solution)/shard_map/all_to_all | solution.py:27
  87.8 4.5 %conv.4 = bf16[8,288,128]{2,1,0:T(8,128)(2,1)S(1)} custom-call(s32[1]{0:T(128)} %bitcast.5.rank_ref.refs_0_, bf16[544,128]{1,0:T(8,128)(2,1)S(1)} %get-tuple-element.32.refs_1_, bf16[544,128]{1,0:T(8,128)(2,1)S(1)} %collective-permute-done.2.refs_2_, bf16[544,128]{1,0:T(8,128)(2,1)S(1)} %collective-permute-done.3.refs_3_, bf16[544,128]{1,0:T(8,128)(2,1)S(1)} %copy-done.4, ...), custom_call_target="tpu_custom_call" | custom-call | tf_op jit(solution)/shard_map/conv/pallas_call | solution.py:401
  93.6 3.7 %all-to-all-start = ((bf16[8,288,128]{2,1,0:T(8,128)(2,1)}), bf16[8,288,128]{2,1,0:T(8,128)(2,1)S(1)}, u32[]{:S(2)}, u32[]{:S(2)}) async-start(bf16[8,288,128]{2,1,0:T(8,128)(2,1)} %copy-done.1), calls=%async_computation | async-start | bytes 1179648 | tf_op jit(solution)/shard_map/all_to_all | solution.py:27
  101.7 3.3 %finish.4 = (bf16[128,4096]{1,0:T(8,128)(2,1)}, bf16[264,1024]{1,0:T(8,128)(2,1)}, f32[9,1,4096]{2,1,0:T(1,128)S(1)}, f32[256,128]{1,0:T(8,128)S(1)}) custom-call(bf16[128,4096]{1,0:T(8,128)(2,1)} %bitcast.35, bf16[128,4096]{1,0:T(8,128)(2,1)} %bitcast.28, bf16[128,4096]{1,0:T(8,128)(2,1)} %bitcast.2.value_ref.value_top, bf16[128,4096]{1,0:T(8,128)(2,1)} %bitcast.42, ...), custom_call_target="tpu_custom_call" | custom-call | tf_op jit(solution)/shard_map/finish/pallas_call | solution.py:424
  105.1 3.4 %finish.5 = (bf16[128,4096]{1,0:T(8,128)(2,1)}, bf16[264,1024]{1,0:T(8,128)(2,1)}, f32[9,1,4096]{2,1,0:T(1,128)S(1)}, f32[256,128]{1,0:T(8,128)S(1)}) custom-call(bf16[128,4096]{1,0:T(8,128)(2,1)} %bitcast.36, bf16[128,4096]{1,0:T(8,128)(2,1)} %bitcast.29, ...), custom_call_target="tpu_custom_call", output_to_operand_aliasing={{0}: (8, {}), {2}: (9, {}), {3}: (10, {})} | custom-call | tf_op jit(solution)/shard_map/finish/pallas_call | solution.py:424
  108.4 3.2 %finish.6 = (bf16[128,4096]{1,0:T(8,128)(2,1)}, bf16[264,1024]{1,0:T(8,128)(2,1)S(1)}, f32[9,1,4096]{2,1,0:T(1,128)S(1)}, f32[256,128]{1,0:T(8,128)S(1)}) custom-call(bf16[128,4096]{1,0:T(8,128)(2,1)} %bitcast.37, bf16[128,4096]{1,0:T(8,128)(2,1)} %bitcast.30, ...), custom_call_target="tpu_custom_call", output_to_operand_aliasing={{0}: (8, {}), {2}: (9, {}), {3}: (10, {})} | custom-call | tf_op jit(solution)/shard_map/finish/pallas_call | solution.py:424
  111.7 3.5 %finish.7 = (bf16[128,4096]{1,0:T(8,128)(2,1)}, bf16[264,1024]{1,0:T(8,128)(2,1)}, f32[9,1,4096]{2,1,0:T(1,128)S(1)}, f32[256,128]{1,0:T(8,128)S(1)}) custom-call(bf16[128,4096]{1,0:T(8,128)(2,1)} %bitcast.38, bf16[128,4096]{1,0:T(8,128)(2,1)} %bitcast.31, ...), custom_call_target="tpu_custom_call", output_to_operand_aliasing={{0}: (8, {}), {2}: (9, {}), {3}: (10, {})} | custom-call | tf_op jit(solution)/shard_map/finish/pallas_call | solution.py:424
  115.2 5.9 %collective-permute-start.17 = (f32[9,1,4096]{2,1,0:T(1,128)S(1)}, f32[9,1,4096]{2,1,0:T(1,128)S(1)}, u32[]{:S(2)}, u32[]{:S(2)}) collective-permute-start(f32[9,1,4096]{2,1,0:T(1,128)S(1)} %get-tuple-element.55), channel_id=1, source_target_pairs={{0,4},{4,0},{8,12},{12,8},{16,20},{20,16},{24,28},{28,24},{1,5},{5... | collective-permute-start | bytes 442376 | tf_op jit(solution)/shard_map/ppermute | solution.py:313
  131.5 21.9 %collective-permute-done.12.taps_ref = f32[6,1,4096]{2,1,0:T(1,128)S(1)} collective-permute-done((f32[6,1,4096]{2,1,0:T(1,128)S(1)}, f32[6,1,4096]{2,1,0:T(1,128)S(1)}, u32[]{:S(2)}, u32[]{:S(2)}) %collective-permute-start.12) | collective-permute-done | bytes 98336 | tf_op jit(solution)/shard_map/ppermute | solution.py:23
  160.3 22.0 %collective-permute-done.16.late_ref = bf16[264,1024]{1,0:T(8,128)(2,1)S(1)} collective-permute-done((bf16[264,1024]{1,0:T(8,128)(2,1)}, bf16[264,1024]{1,0:T(8,128)(2,1)S(1)}, u32[]{:S(2)}, u32[]{:S(2)}) %collective-permute-start.16) | collective-permute-done | bytes 540704 | tf_op jit(solution)/shard_map/ppermute | solution.py:23
  187.2 6.7 %collective-permute-done.14.late_ref = bf16[264,1024]{1,0:T(8,128)(2,1)S(1)} collective-permute-done((bf16[264,1024]{1,0:T(8,128)(2,1)}, bf16[264,1024]{1,0:T(8,128)(2,1)S(1)}, u32[]{:S(2)}, u32[]{:S(2)}) %collective-permute-start.14) | collective-permute-done | bytes 540704 | tf_op jit(solution)/shard_map/ppermute | solution.py:23
  196.3 6.7 %collective-permute-done.13.late_ref = bf16[264,1024]{1,0:T(8,128)(2,1)S(1)} collective-permute-done((bf16[264,1024]{1,0:T(8,128)(2,1)}, bf16[264,1024]{1,0:T(8,128)(2,1)S(1)}, u32[]{:S(2)}, u32[]{:S(2)}) %collective-permute-start.13) | collective-permute-done | bytes 540704 | tf_op jit(solution)/shard_map/ppermute | solution.py:23
  (79 shorter events, 55.8 us)
Async XLA Ops:
  1.7 3.3 %collective-permute-start = (bf16[3,2,4096]{2,1,0:T(2,128)(2,1)S(1)}, bf16[3,2,4096]{2,1,0:T(2,128)(2,1)S(1)}, u32[]{:S(2)}, u32[]{:S(2)}) collective-permute-start(bf16[3,2,4096]{2,1,0:T(2,128)(2,1)S(1)} %get-tuple-element.30), channel_id=1, source_target_pairs={{0,4},{4,8},{8,12},{12,16},{16,20},{20,24},{24,28},{1,5},{5,9},{9,... | collective-permute-start | bytes 147464 | tf_op jit(solution)/shard_map/ppermute | solution.py:23
  8.5 43.5 %all-to-all-start.2 = ((bf16[8,544,128]{2,1,0:T(8,128)(2,1)}), bf16[8,544,128]{2,1,0:T(8,128)(2,1)S(1)}, u32[]{:S(2)}, u32[]{:S(2)}) async-start(bf16[8,544,128]{2,1,0:T(8,128)(2,1)} %send.3), calls=%async_computation.2 | async-start | bytes 2228224 | tf_op jit(solution)/shard_map/all_to_all | solution.py:27
  18.7 4.2 %collective-permute-start.2 = (bf16[544,128]{1,0:T(8,128)(2,1)S(1)}, bf16[544,128]{1,0:T(8,128)(2,1)S(1)}, u32[]{:S(2)}, u32[]{:S(2)}) collective-permute-start(bf16[544,128]{1,0:T(8,128)(2,1)S(1)} %get-tuple-element.33), channel_id=1, source_target_pairs={{0,4},{4,0},{8,12},{12,8},{16,20},{20,16},{24,28},{28,24},{1,5},{5... | collective-permute-start | bytes 417800 | tf_op jit(solution)/shard_map/ppermute | solution.py:390
  19.2 15.4 %collective-permute-start.3 = (bf16[544,128]{1,0:T(8,128)(2,1)S(1)}, bf16[544,128]{1,0:T(8,128)(2,1)S(1)}, u32[]{:S(2)}, u32[]{:S(2)}) collective-permute-start(bf16[544,128]{1,0:T(8,128)(2,1)S(1)} %get-tuple-element.34), channel_id=1, source_target_pairs={{0,8},{4,12},{8,0},{12,4},{16,24},{20,28},{24,16},{28,20},{1,9},{5... | collective-permute-start | bytes 417800 | tf_op jit(solution)/shard_map/ppermute | solution.py:390
  20.9 15.6 %collective-permute-start.4 = (bf16[544,128]{1,0:T(8,128)(2,1)S(1)}, bf16[544,128]{1,0:T(8,128)(2,1)S(1)}, u32[]{:S(2)}, u32[]{:S(2)}) collective-permute-start(bf16[544,128]{1,0:T(8,128)(2,1)S(1)} %get-tuple-element.35), channel_id=1, source_target_pairs={{0,12},{4,8},{8,4},{12,0},{16,28},{20,24},{24,20},{28,16},{1,13},{... | collective-permute-start | bytes 417800 | tf_op jit(solution)/shard_map/ppermute | solution.py:390
  20.9 15.6 %collective-permute-start.5 = (bf16[544,128]{1,0:T(8,128)(2,1)S(1)}, bf16[544,128]{1,0:T(8,128)(2,1)S(1)}, u32[]{:S(2)}, u32[]{:S(2)}) collective-permute-start(bf16[544,128]{1,0:T(8,128)(2,1)S(1)} %get-tuple-element.36), channel_id=1, source_target_pairs={{0,16},{4,20},{8,24},{12,28},{16,0},{20,4},{24,8},{28,12},{1,17},{... | collective-permute-start | bytes 417800 | tf_op jit(solution)/shard_map/ppermute | solution.py:390
  22.8 13.6 %collective-permute-start.6 = (bf16[544,128]{1,0:T(8,128)(2,1)S(1)}, bf16[544,128]{1,0:T(8,128)(2,1)S(1)}, u32[]{:S(2)}, u32[]{:S(2)}) collective-permute-start(bf16[544,128]{1,0:T(8,128)(2,1)S(1)} %get-tuple-element.37), channel_id=1, source_target_pairs={{0,20},{4,16},{8,28},{12,24},{16,4},{20,0},{24,12},{28,8},{1,21},{... | collective-permute-start | bytes 417800 | tf_op jit(solution)/shard_map/ppermute | solution.py:390
  22.8 18.6 %collective-permute-start.7 = (bf16[544,128]{1,0:T(8,128)(2,1)S(1)}, bf16[544,128]{1,0:T(8,128)(2,1)S(1)}, u32[]{:S(2)}, u32[]{:S(2)}) collective-permute-start(bf16[544,128]{1,0:T(8,128)(2,1)S(1)} %get-tuple-element.38), channel_id=1, source_target_pairs={{0,24},{4,28},{8,16},{12,20},{16,8},{20,12},{24,0},{28,4},{1,25},{... | collective-permute-start | bytes 417800 | tf_op jit(solution)/shard_map/ppermute | solution.py:390
  34.6 8.7 %collective-permute-start.8 = (bf16[544,128]{1,0:T(8,128)(2,1)S(1)}, bf16[544,128]{1,0:T(8,128)(2,1)S(1)}, u32[]{:S(2)}, u32[]{:S(2)}) collective-permute-start(bf16[544,128]{1,0:T(8,128)(2,1)S(1)} %get-tuple-element.39), channel_id=1, source_target_pairs={{0,28},{4,24},{8,20},{12,16},{16,12},{20,8},{24,4},{28,0},{1,29},{... | collective-permute-start | bytes 417800 | tf_op jit(solution)/shard_map/ppermute | solution.py:390
  51.9 13.9 %all-to-all-start.1 = ((bf16[8,288,128]{2,1,0:T(8,128)(2,1)}), bf16[8,288,128]{2,1,0:T(8,128)(2,1)S(1)}, u32[]{:S(2)}, u32[]{:S(2)}) async-start(bf16[8,288,128]{2,1,0:T(8,128)(2,1)} %conv.5), calls=%async_computation.1 | async-start | bytes 1179648 | tf_op jit(solution)/shard_map/all_to_all | solution.py:27
  65.8 13.9 %all-to-all-start.3 = ((bf16[8,288,128]{2,1,0:T(8,128)(2,1)}), bf16[8,288,128]{2,1,0:T(8,128)(2,1)S(1)}, u32[]{:S(2)}, u32[]{:S(2)}) async-start(bf16[8,288,128]{2,1,0:T(8,128)(2,1)} %conv.6), calls=%async_computation.3 | async-start | bytes 1179648 | tf_op jit(solution)/shard_map/all_to_all | solution.py:27
  79.7 13.9 %all-to-all-start.4 = ((bf16[8,288,128]{2,1,0:T(8,128)(2,1)}), bf16[8,288,128]{2,1,0:T(8,128)(2,1)S(1)}, u32[]{:S(2)}, u32[]{:S(2)}) async-start(bf16[8,288,128]{2,1,0:T(8,128)(2,1)} %copy-done.2), calls=%async_computation.4 | async-start | bytes 1179648 | tf_op jit(solution)/shard_map/all_to_all | solution.py:27
  93.6 18.1 %all-to-all-start = ((bf16[8,288,128]{2,1,0:T(8,128)(2,1)}), bf16[8,288,128]{2,1,0:T(8,128)(2,1)S(1)}, u32[]{:S(2)}, u32[]{:S(2)}) async-start(bf16[8,288,128]{2,1,0:T(8,128)(2,1)} %copy-done.1), calls=%async_computation | async-start | bytes 1179648 | tf_op jit(solution)/shard_map/all_to_all | solution.py:27
  97.3 58.7 %collective-permute-start.9 = (bf16[128,4096]{1,0:T(8,128)(2,1)}, bf16[128,4096]{1,0:T(8,128)(2,1)}, u32[]{:S(2)}, u32[]{:S(2)}) collective-permute-start(bf16[128,4096]{1,0:T(8,128)(2,1)} %bitcast.27), channel_id=1, source_target_pairs={{1,0},{2,1},{3,2},{5,4},{6,5},{7,6},{9,8},{10,9},{11,10},{13,12},{... | collective-permute-start | bytes 3145736 | tf_op jit(solution)/shard_map/ppermute | solution.py:23
  115.2 6.9 %collective-permute-start.17 = (f32[9,1,4096]{2,1,0:T(1,128)S(1)}, f32[9,1,4096]{2,1,0:T(1,128)S(1)}, u32[]{:S(2)}, u32[]{:S(2)}) collective-permute-start(f32[9,1,4096]{2,1,0:T(1,128)S(1)} %get-tuple-element.55), channel_id=1, source_target_pairs={{0,4},{4,0},{8,12},{12,8},{16,20},{20,16},{24,28},{28,24},{1,5},{5... | collective-permute-start | bytes 442376 | tf_op jit(solution)/shard_map/ppermute | solution.py:313
  122.3 6.2 %collective-permute-start.18 = (f32[9,1,4096]{2,1,0:T(1,128)S(1)}, f32[9,1,4096]{2,1,0:T(1,128)S(1)}, u32[]{:S(2)}, u32[]{:S(2)}) collective-permute-start(f32[9,1,4096]{2,1,0:T(1,128)S(1)} %add.9), channel_id=1, source_target_pairs={{0,8},{4,12},{8,0},{12,4},{16,24},{20,28},{24,16},{28,20},{1,9},{5... | collective-permute-start | bytes 442376 | tf_op jit(solution)/shard_map/ppermute | solution.py:313
  123.4 36.8 %collective-permute-start.10 = (bf16[128,4096]{1,0:T(8,128)(2,1)}, bf16[128,4096]{1,0:T(8,128)(2,1)}, u32[]{:S(2)}, u32[]{:S(2)}) collective-permute-start(bf16[128,4096]{1,0:T(8,128)(2,1)} %bitcast.2.value_ref.value_top), channel_id=1, source_target_pairs={{1,0},{2,1},{3,2},{5,4},{6,5},{7,6},{9,8},{10,9},{11,10},{13,12},{... | collective-permute-start | bytes 3145736 | tf_op jit(solution)/shard_map/ppermute | solution.py:23
  124.7 28.7 %collective-permute-start.12 = (f32[6,1,4096]{2,1,0:T(1,128)S(1)}, f32[6,1,4096]{2,1,0:T(1,128)S(1)}, u32[]{:S(2)}, u32[]{:S(2)}) collective-permute-start(f32[6,1,4096]{2,1,0:T(1,128)S(1)} %bitcast.49), channel_id=1, source_target_pairs={{1,0},{2,1},{3,2},{5,4},{6,5},{7,6},{9,8},{10,9},{11,10},{13,12},{... | collective-permute-start | bytes 294920 | tf_op jit(solution)/shard_map/ppermute | solution.py:23
  128.6 28.8 %collective-permute-start.19 = (f32[9,1,4096]{2,1,0:T(1,128)S(1)}, f32[9,1,4096]{2,1,0:T(1,128)S(1)}, u32[]{:S(2)}, u32[]{:S(2)}) collective-permute-start(f32[9,1,4096]{2,1,0:T(1,128)S(1)} %add.10), channel_id=1, source_target_pairs={{0,16},{4,20},{8,24},{12,28},{16,0},{20,4},{24,8},{28,12},{1,17},{... | collective-permute-start | bytes 442376 | tf_op jit(solution)/shard_map/ppermute | solution.py:313
  130.2 24.5 %collective-permute-start.11 = (bf16[4,2,4096]{2,1,0:T(2,128)(2,1)S(1)}, bf16[4,2,4096]{2,1,0:T(2,128)(2,1)S(1)}, u32[]{:S(2)}, u32[]{:S(2)}) collective-permute-start(bf16[4,2,4096]{2,1,0:T(2,128)(2,1)S(1)} %pad_maximum_fusion), channel_id=1, source_target_pairs={{1,0},{2,1},{3,2},{5,4},{6,5},{7,6},{9,8},{10,9},{11,10},{13,12},{... | collective-permute-start | bytes 196616 | tf_op jit(solution)/shard_map/ppermute | solution.py:23
  153.5 31.3 %collective-permute-start.15 = (bf16[264,1024]{1,0:T(8,128)(2,1)}, bf16[264,1024]{1,0:T(8,128)(2,1)S(1)}, u32[]{:S(2)}, u32[]{:S(2)}) collective-permute-start(bf16[264,1024]{1,0:T(8,128)(2,1)} %get-tuple-element.52), channel_id=1, source_target_pairs={{1,0},{2,1},{3,2},{5,4},{6,5},{7,6},{9,8},{10,9},{11,10},{13,12},{... | collective-permute-start | bytes 1622024 | tf_op jit(solution)/shard_map/ppermute | solution.py:23
  154.8 27.5 %collective-permute-start.16 = (bf16[264,1024]{1,0:T(8,128)(2,1)}, bf16[264,1024]{1,0:T(8,128)(2,1)S(1)}, u32[]{:S(2)}, u32[]{:S(2)}) collective-permute-start(bf16[264,1024]{1,0:T(8,128)(2,1)} %get-tuple-element.53), channel_id=1, source_target_pairs={{1,0},{2,1},{3,2},{5,4},{6,5},{7,6},{9,8},{10,9},{11,10},{13,12},{... | collective-permute-start | bytes 1622024 | tf_op jit(solution)/shard_map/ppermute | solution.py:23
  156.1 37.8 %collective-permute-start.14 = (bf16[264,1024]{1,0:T(8,128)(2,1)}, bf16[264,1024]{1,0:T(8,128)(2,1)S(1)}, u32[]{:S(2)}, u32[]{:S(2)}) collective-permute-start(bf16[264,1024]{1,0:T(8,128)(2,1)} %copy-done.14), channel_id=1, source_target_pairs={{1,0},{2,1},{3,2},{5,4},{6,5},{7,6},{9,8},{10,9},{11,10},{13,12},{... | collective-permute-start | bytes 1622024 | tf_op jit(solution)/shard_map/ppermute | solution.py:23
  157.4 45.6 %collective-permute-start.13 = (bf16[264,1024]{1,0:T(8,128)(2,1)}, bf16[264,1024]{1,0:T(8,128)(2,1)S(1)}, u32[]{:S(2)}, u32[]{:S(2)}) collective-permute-start(bf16[264,1024]{1,0:T(8,128)(2,1)} %get-tuple-element.50), channel_id=1, source_target_pairs={{1,0},{2,1},{3,2},{5,4},{6,5},{7,6},{9,8},{10,9},{11,10},{13,12},{... | collective-permute-start | bytes 1622024 | tf_op jit(solution)/shard_map/ppermute | solution.py:23
  (16 other events, 24.9 us)
